TPU v7x, 128 devices: a whole 4x4x4 slice. The times are simulated.
128 devices in a mesh: seq: 32 (over z, y, core), head: 4 (over x).
Axes of the slice: x: 4, y: 4, z: 4, core: 2. Of those that a mesh axis runs over, the one named last changes fastest.
Arguments:
- tokens: bfloat16 [16384, 4096], P('seq'), may hold values from -6 to 6
- w_query: bfloat16 [4096, 2048], P('seq', 'head'), may hold values from -0.09375 to 0.09375
- w_key: bfloat16 [4096, 2048], P('seq', 'head'), may hold values from -0.09375 to 0.09375
- w_value: bfloat16 [4096, 2048], P('seq', 'head'), may hold values from -0.09375 to 0.09375
- omega_seed: int32 [16, 128, 256], P('head'), may hold values from -4 to 4
- grad_out: bfloat16 [16384, 2048], P('seq', 'head'), may hold values from -6 to 6
Outputs:
- input_grad: bfloat16 [16384, 4096], P('seq', 'head')
- query_wgrad: float32 [4096, 2048], P('seq', 'head')
- key_wgrad: float32 [4096, 2048], P('seq', 'head')
- value_wgrad: float32 [4096, 2048], P('seq', 'head')
Inputs may be any that keep to these rules, and one draw needn't show every extreme that they name: `omega_seed`: the feature seeds are small whole numbers.
All inputs are finite; a program needn't handle non-finite values.
Results may differ from a plain program's by a relative error of at most 0.02.
Values may be sent and summed in bfloat16 or wider, within the bound.
No kernel may reach another device: no remote copies, remote signals or barrier semaphores. Data moves between devices by JAX's collectives and lax.ppermute only.
A program may use at most 128 MiB of HBM per device.

v0:
```python
import math

import jax
import jax.numpy as jnp
from jax import lax
from jax.experimental import pallas as pl
from jax.experimental.pallas import tpu as pltpu
from jax.sharding import Mesh, PartitionSpec as P


F32 = jnp.float32
BF16 = jnp.bfloat16
SEED_STEP = 0.4
CHUNK = 256
NT = (((1,), (1,)), ((), ()))
TN = (((0,), (0,)), ((), ()))
NN = (((1,), (0,)), ((), ()))
SWAP = ((0, 1), (1, 0))
STATE_ROWS = 144
MIB = 1 << 20


def dot(a, b, dims):
    return lax.dot_general(a, b, dims, preferred_element_type=F32)


GRANT = 12


def params(vmem=GRANT):
    return pltpu.CompilerParams(vmem_limit_bytes=vmem * MIB)


def cost(flops, nbytes):
    return pl.CostEstimate(flops=flops, bytes_accessed=nbytes, transcendentals=0)


def arrange_body(idx_ref, own_ref, other_ref, rows_ref, columns_ref):
    core = idx_ref[16]
    size = own_ref.shape[0]
    mine = pl.ds(pl.multiple_of(core * size, size), size)
    theirs = pl.ds(pl.multiple_of((1 - core) * size, size), size)
    own, other = own_ref[...], other_ref[...]
    rows_ref[mine, :] = own
    rows_ref[theirs, :] = other
    columns_ref[:, mine] = own.T
    columns_ref[:, theirs] = other.T


def arrange(idx, own, other, group):
    size, depth = own.shape
    width = depth // 16
    source = pl.BlockSpec((size, width), lambda k, idx: (0, idx[4 * group + k]))
    return pl.pallas_call(
        arrange_body,
        out_shape=[
            jax.ShapeDtypeStruct((2 * size, 4 * width), BF16),
            jax.ShapeDtypeStruct((4 * width, 2 * size), BF16),
        ],
        grid_spec=pltpu.PrefetchScalarGridSpec(
            num_scalar_prefetch=1,
            grid=(4,),
            in_specs=[source, source],
            out_specs=[
                pl.BlockSpec((2 * size, width), lambda k, idx: (0, k)),
                pl.BlockSpec((width, 2 * size), lambda k, idx: (k, 0)),
            ],
        ),
        compiler_params=params(),
        cost_estimate=cost(4 * MIB, 6 * MIB),
        name="arrange",
    )(idx, own, other)


def halves_dot(x_ref, wa_ref, wb_ref):
    half = wa_ref.shape[0]
    return dot(x_ref[:, :half], wa_ref[...], NN) + dot(x_ref[:, half:], wb_ref[...], NN)


def first_body(x_ref, wa_ref, wb_ref, out_ref):
    out_ref[...] = halves_dot(x_ref, wa_ref, wb_ref)


def more_body(acc_ref, xa_ref, xb_ref, *rest):
    *w_refs, out_ref = rest
    total = acc_ref[...]
    for x_ref, pair in ((xa_ref, w_refs[:2]), (xb_ref, w_refs[2:])):
        total += halves_dot(x_ref, *pair)
    out_ref[...] = total


def end_body(acc_ref, x_ref, wa_ref, wb_ref, out_ref):
    out_ref[...] = (acc_ref[...] + halves_dot(x_ref, wa_ref, wb_ref)).astype(BF16)


def project(body, acc, xs, ws, dtype):
    tok = xs[0].shape[0]
    columns = ws[0].shape[1]
    size = 256

    def tall(a):
        return pl.BlockSpec((size, a.shape[1]), lambda i: (i, 0))

    def whole(a):
        return pl.BlockSpec(a.shape, lambda i: (0, 0))

    ops = acc + xs + ws
    depth = sum(x.shape[1] for x in xs)
    return pl.pallas_call(
        body,
        grid=(tok // size,),
        in_specs=[tall(a) for a in acc + xs] + [whole(w) for w in ws],
        out_specs=pl.BlockSpec((size, columns), lambda i: (i, 0)),
        out_shape=jax.ShapeDtypeStruct((tok, columns), dtype),
        compiler_params=params(16),
        cost_estimate=cost(2 * tok * depth * columns, 8 * MIB),
    )(*ops)


def features(rows, seed):
    size = rows.shape[1]
    scale = size ** (-0.25)
    scaled = rows.astype(F32) * scale
    projected = dot(rows, seed, NN) * (SEED_STEP * scale)
    norm = 0.5 * jnp.sum(scaled * scaled, -1, keepdims=True)
    return jnp.exp(projected - norm) * (1.0 / math.sqrt(seed.shape[1]))


def feature_grad(weighted, rows, seed):
    scale = rows.shape[1] ** (-0.25)
    projected = dot(weighted.astype(BF16), seed, NT) * SEED_STEP
    total = jnp.sum(weighted, -1, keepdims=True)
    return (projected - total * (rows.astype(F32) * scale)) * scale


def mask_of(size):
    return lax.broadcasted_iota(jnp.int32, (size, size), 0) >= lax.broadcasted_iota(
        jnp.int32, (size, size), 1
    )


def keys_body(k_ref, v_ref, seed_ref, kf_ref, before_ref, total_ref, carry_ref):
    step = pl.program_id(0)

    @pl.when(step == 0)
    def _():
        carry_ref[...] = jnp.zeros_like(carry_ref)

    before_ref[0] = carry_ref[...]
    for head in range(2):
        cols = slice(128 * head, 128 * head + 128)
        kf = features(k_ref[:, cols], seed_ref[head]).astype(BF16)
        kf_ref[:, 256 * head : 256 * head + 256] = kf
        main = dot(v_ref[:, cols], kf, TN)
        row = jnp.sum(kf.astype(F32), 0, keepdims=True)
        pad = jnp.zeros((STATE_ROWS - 129, 256), F32)
        carry_ref[head] += jnp.concatenate([main, row, pad], 0)

    @pl.when(step == pl.num_programs(0) - 1)
    def _():
        total_ref[...] = carry_ref[...].astype(BF16)


def keys_stage(kvq, seed):
    tok = kvq.shape[0]
    n = tok // CHUNK
    state = (2, STATE_ROWS, 256)
    return pl.pallas_call(
        keys_body,
        grid=(n,),
        in_specs=[
            pl.BlockSpec((CHUNK, 256), lambda i: (i, 0)),
            pl.BlockSpec((CHUNK, 256), lambda i: (i, 1)),
            pl.BlockSpec((2, 128, 256), lambda i: (0, 0, 0)),
        ],
        out_specs=[
            pl.BlockSpec((CHUNK, 512), lambda i: (i, 0)),
            pl.BlockSpec((1,) + state, lambda i: (i, 0, 0, 0)),
            pl.BlockSpec(state, lambda i: (0, 0, 0)),
        ],
        out_shape=[
            jax.ShapeDtypeStruct((tok, 512), BF16),
            jax.ShapeDtypeStruct((n,) + state, F32),
            jax.ShapeDtypeStruct(state, BF16),
        ],
        scratch_shapes=[pltpu.VMEM(state, F32)],
        compiler_params=params(),
        cost_estimate=cost(n * 2 * 4 * 256 * 256 * 128, 4 * MIB),
        name="keys_stage",
    )(kvq, kvq, seed)


def local_body(q_ref, v_ref, kf_ref, seed_ref, before_ref, qf_ref, s_ref, num_ref, den_ref):
    mask = mask_of(CHUNK)
    for head in range(2):
        cols = slice(128 * head, 128 * head + 128)
        wide = slice(256 * head, 256 * head + 256)
        qf = features(q_ref[:, cols], seed_ref[head]).astype(BF16)
        qf_ref[:, wide] = qf
        scores = jnp.where(mask, dot(qf, kf_ref[:, wide], NT), 0.0)
        s16 = scores.astype(BF16)
        s_ref[:, wide] = s16
        main = before_ref[0, head, :128, :].astype(BF16)
        row = before_ref[0, head, 128:129, :]
        num_ref[:, cols] = dot(s16, v_ref[:, cols], NN) + dot(qf, main, NT)
        den_ref[head] = jnp.sum(scores, -1, keepdims=True) + jnp.sum(
            qf.astype(F32) * row, -1, keepdims=True
        )


def local_stage(kvq, kf, seed, before):
    tok = kvq.shape[0]
    n = tok // CHUNK
    return pl.pallas_call(
        local_body,
        grid=(n,),
        in_specs=[
            pl.BlockSpec((CHUNK, 256), lambda i: (i, 2)),
            pl.BlockSpec((CHUNK, 256), lambda i: (i, 1)),
            pl.BlockSpec((CHUNK, 512), lambda i: (i, 0)),
            pl.BlockSpec((2, 128, 256), lambda i: (0, 0, 0)),
            pl.BlockSpec((1, 2, STATE_ROWS, 256), lambda i: (i, 0, 0, 0)),
        ],
        out_specs=[
            pl.BlockSpec((CHUNK, 512), lambda i: (i, 0)),
            pl.BlockSpec((CHUNK, 512), lambda i: (i, 0)),
            pl.BlockSpec((CHUNK, 256), lambda i: (i, 0)),
            pl.BlockSpec((2, CHUNK, 1), lambda i: (0, i, 0)),
        ],
        out_shape=[
            jax.ShapeDtypeStruct((tok, 512), BF16),
            jax.ShapeDtypeStruct((tok, 512), BF16),
            jax.ShapeDtypeStruct((tok, 256), F32),
            jax.ShapeDtypeStruct((2, tok, 1), F32),
        ],
        compiler_params=params(),
        cost_estimate=cost(n * 2 * 10 * 256 * 256 * 128, 6 * MIB),
        name="local_stage",
    )(kvq, kvq, kf, seed, before)


def ratio_body(qf_ref, num_ref, den_ref, g_ref, prefix_ref, gn_ref, gd_ref, total_ref, carry_ref):
    step = pl.program_id(0)

    @pl.when(step == 0)
    def _():
        carry_ref[...] = jnp.zeros_like(carry_ref)

    for head in range(2):
        cols = slice(128 * head, 128 * head + 128)
        wide = slice(256 * head, 256 * head + 256)
        qf = qf_ref[:, wide]
        qf32 = qf.astype(F32)
        main = prefix_ref[head, :128, :].astype(BF16)
        row = prefix_ref[head, 128:129, :]
        num = num_ref[:, cols] + dot(qf, main, NT)
        den = den_ref[head] + jnp.sum(qf32 * row, -1, keepdims=True)
        inverse = 1.0 / den
        g = g_ref[:, cols].astype(F32)
        gn = (g * inverse).astype(BF16)
        gd = -jnp.sum(g * num, -1, keepdims=True) * inverse * inverse
        gn_ref[:, cols] = gn
        gd_ref[head] = gd
        carry_ref[head, :128, :] += dot(gn, qf, TN)
        carry_ref[head, 128:129, :] += jnp.sum(qf32 * gd, 0, keepdims=True)

    @pl.when(step == pl.num_programs(0) - 1)
    def _():
        total_ref[...] = carry_ref[...].astype(BF16)


def ratio_stage(qf, num, den, g, prefix):
    tok = qf.shape[0]
    n = tok // CHUNK
    state = (2, STATE_ROWS, 256)
    return pl.pallas_call(
        ratio_body,
        grid=(n,),
        in_specs=[
            pl.BlockSpec((CHUNK, 512), lambda i: (i, 0)),
            pl.BlockSpec((CHUNK, 256), lambda i: (i, 0)),
            pl.BlockSpec((2, CHUNK, 1), lambda i: (0, i, 0)),
            pl.BlockSpec((CHUNK, 256), lambda i: (i, 0)),
            pl.BlockSpec(state, lambda i: (0, 0, 0)),
        ],
        out_specs=[
            pl.BlockSpec((CHUNK, 256), lambda i: (i, 0)),
            pl.BlockSpec((2, CHUNK, 1), lambda i: (0, i, 0)),
            pl.BlockSpec(state, lambda i: (0, 0, 0)),
        ],
        out_shape=[
            jax.ShapeDtypeStruct((tok, 256), BF16),
            jax.ShapeDtypeStruct((2, tok, 1), F32),
            jax.ShapeDtypeStruct(state, BF16),
        ],
        scratch_shapes=[pltpu.VMEM(state, F32)],
        compiler_params=params(),
        cost_estimate=cost(n * 2 * 4 * 256 * 256 * 128, 4 * MIB),
        name="ratio_stage",
    )(qf, num, den, g, prefix)


def middle_body(
    q_ref, v_ref, kf_ref, qf_ref, s_ref, gn_ref, gd_ref, seed_ref, before_ref, prefix_ref,
    dq_ref, dqt_ref, dkf_ref, dv_ref, carry_ref,
):
    step = pl.program_id(0)
    mask = mask_of(CHUNK)

    @pl.when(step == 0)
    def _():
        carry_ref[...] = jnp.zeros_like(carry_ref)

    for head in range(2):
        cols = slice(128 * head, 128 * head + 128)
        wide = slice(256 * head, 256 * head + 256)
        qf, kf, gn, gd = qf_ref[:, wide], kf_ref[:, wide], gn_ref[:, cols], gd_ref[head]
        v = v_ref[:, cols]
        qf32 = qf.astype(F32)
        pairs = jnp.where(mask, dot(gn, v, NT) + gd, 0.0).astype(BF16)
        earlier = prefix_ref[head] + before_ref[0, head]
        main, row = earlier[:128].astype(BF16), earlier[128:129]
        dqf = dot(pairs, kf, NN) + dot(gn, main, NN) + gd * row
        dq = feature_grad(dqf * qf32, q_ref[:, cols], seed_ref[head]).astype(BF16)
        dq_ref[:, cols] = dq
        dqt_ref[cols, :] = dq.T
        later = carry_ref[head]
        later_main, later_row = later[:128].astype(BF16), later[128:129]
        dkf_ref[:, wide] = dot(pairs, qf, TN) + dot(v, later_main, NN) + later_row
        dv_ref[:, cols] = dot(s_ref[:, wide], gn, TN) + dot(kf, later_main, NT)
        carry_ref[head, :128, :] += dot(gn, qf, TN)
        carry_ref[head, 128:129, :] += jnp.sum(qf32 * gd, 0, keepdims=True)


def middle_stage(kvq, kf, qf, s, gn, gd, seed, before, prefix):
    tok = qf.shape[0]
    n = tok // CHUNK
    state = (2, STATE_ROWS, 256)

    def narrow(column):
        return pl.BlockSpec((CHUNK, 256), lambda i: (n - 1 - i, column))

    wide = pl.BlockSpec((CHUNK, 512), lambda i: (n - 1 - i, 0))
    return pl.pallas_call(
        middle_body,
        grid=(n,),
        in_specs=[
            narrow(2), narrow(1), wide, wide, wide, narrow(0),
            pl.BlockSpec((2, CHUNK, 1), lambda i: (0, n - 1 - i, 0)),
            pl.BlockSpec((2, 128, 256), lambda i: (0, 0, 0)),
            pl.BlockSpec((1,) + state, lambda i: (n - 1 - i, 0, 0, 0)),
            pl.BlockSpec(state, lambda i: (0, 0, 0)),
        ],
        out_specs=[
            narrow(0),
            pl.BlockSpec((256, CHUNK), lambda i: (0, n - 1 - i)),
            wide,
            narrow(0),
        ],
        out_shape=[
            jax.ShapeDtypeStruct((tok, 256), BF16),
            jax.ShapeDtypeStruct((256, tok), BF16),
            jax.ShapeDtypeStruct((tok, 512), F32),
            jax.ShapeDtypeStruct((tok, 256), F32),
        ],
        scratch_shapes=[pltpu.VMEM(state, F32)],
        compiler_params=params(),
        cost_estimate=cost(n * 2 * 20 * 256 * 256 * 128, 10 * MIB),
        name="middle_stage",
    )(kvq, kvq, kf, qf, s, gn, gd, seed, before, prefix)


def last_body(k_ref, v_ref, kf_ref, dkf_ref, dv_ref, seed_ref, suffix_ref, out_ref, outt_ref):
    for head in range(2):
        cols = slice(128 * head, 128 * head + 128)
        wide = slice(256 * head, 256 * head + 256)
        kf = kf_ref[:, wide]
        main = suffix_ref[head, :128, :].astype(BF16)
        row = suffix_ref[head, 128:129, :]
        dkf = dkf_ref[:, wide] + dot(v_ref[:, cols], main, NN) + row
        dk = feature_grad(dkf * kf.astype(F32), k_ref[:, cols], seed_ref[head]).astype(BF16)
        dv = (dv_ref[:, cols] + dot(kf, main, NT)).astype(BF16)
        dv_cols = slice(256 + 128 * head, 384 + 128 * head)
        out_ref[:, cols] = dk
        out_ref[:, dv_cols] = dv
        outt_ref[cols, :] = dk.T
        outt_ref[dv_cols, :] = dv.T


def last_stage(kvq, kf, dkf, dv, seed, suffix):
    tok = kf.shape[0]
    n = tok // CHUNK
    state = (2, STATE_ROWS, 256)
    return pl.pallas_call(
        last_body,
        grid=(n,),
        in_specs=[
            pl.BlockSpec((CHUNK, 256), lambda i: (i, 0)),
            pl.BlockSpec((CHUNK, 256), lambda i: (i, 1)),
            pl.BlockSpec((CHUNK, 512), lambda i: (i, 0)),
            pl.BlockSpec((CHUNK, 512), lambda i: (i, 0)),
            pl.BlockSpec((CHUNK, 256), lambda i: (i, 0)),
            pl.BlockSpec((2, 128, 256), lambda i: (0, 0, 0)),
            pl.BlockSpec(state, lambda i: (0, 0, 0)),
        ],
        out_specs=[
            pl.BlockSpec((CHUNK, 512), lambda i: (i, 0)),
            pl.BlockSpec((512, CHUNK), lambda i: (0, i)),
        ],
        out_shape=[
            jax.ShapeDtypeStruct((tok, 512), BF16),
            jax.ShapeDtypeStruct((512, tok), BF16),
        ],
        compiler_params=params(),
        cost_estimate=cost(n * 2 * 6 * 256 * 256 * 128, 6 * MIB),
        name="last_stage",
    )(kvq, kvq, kf, dkf, dv, seed, suffix)


def wgrad_body(x_ref, dkv_ref, dq_ref, out_ref):
    x = x_ref[...]
    out_ref[:, :512] = dot(x, dkv_ref[...], NN)
    out_ref[:, 512:] = dot(x, dq_ref[...], NN)


def wgrad(x, dkv, dq):
    depth, tok = x.shape
    columns = dkv.shape[1] + dq.shape[1]
    size = 256
    return pl.pallas_call(
        wgrad_body,
        grid=(depth // size,),
        in_specs=[
            pl.BlockSpec((size, tok), lambda i: (i, 0)),
            pl.BlockSpec(dkv.shape, lambda i: (0, 0)),
            pl.BlockSpec(dq.shape, lambda i: (0, 0)),
        ],
        out_specs=pl.BlockSpec((size, columns), lambda i: (i, 0)),
        out_shape=jax.ShapeDtypeStruct((depth, columns), F32),
        compiler_params=params(),
        cost_estimate=cost(2 * tok * depth * columns, 6 * MIB),
        name="wgrad",
    )(x, dkv, dq)


def finish_body(core_ref, keep_ref, got_ref, q_ref, k_ref, v_ref):
    core = core_ref[0]
    mine = pl.ds(pl.multiple_of(core * 256, 256), 256)
    theirs = pl.ds(pl.multiple_of((1 - core) * 256, 256), 256)
    for place, ref in enumerate((k_ref, v_ref, q_ref)):
        cols = slice(256 * place, 256 * place + 256)
        ref[:, mine] = keep_ref[:, cols].astype(F32)
        ref[:, theirs] = got_ref[:, cols].astype(F32)


def finish(core, keep, got):
    rows = keep.shape[0]
    out = jax.ShapeDtypeStruct((rows, 512), F32)
    whole = pl.BlockSpec(keep.shape, lambda i, core: (0, 0))
    return pl.pallas_call(
        finish_body,
        out_shape=[out] * 3,
        grid_spec=pltpu.PrefetchScalarGridSpec(
            num_scalar_prefetch=1,
            grid=(1,),
            in_specs=[whole, whole],
            out_specs=[pl.BlockSpec((rows, 512), lambda i, core: (0, 0))] * 3,
        ),
        compiler_params=params(8),
        cost_estimate=cost(MIB, MIB),
        name="finish",
    )(core, keep, got)


def collect_body(place_ref, *refs):
    *pieces, out_ref, sems = refs
    size = pieces[0].shape[0] // 2
    copies = []
    for slot in range(2 * len(pieces)):
        to = pl.ds(pl.multiple_of(place_ref[slot] * size, size), size)
        source = pieces[slot // 2].at[pl.ds(slot % 2 * size, size), :]
        copies.append(pltpu.make_async_copy(source, out_ref.at[to, :], sems.at[slot]))
    for copy in copies:
        copy.start()
    for copy in copies:
        copy.wait()


def collect(place, pieces):
    rows, columns = pieces[0].shape
    n = len(pieces)
    return pl.pallas_call(
        collect_body,
        out_shape=jax.ShapeDtypeStruct((n * rows, columns), BF16),
        grid_spec=pltpu.PrefetchScalarGridSpec(
            num_scalar_prefetch=1,
            grid=(1,),
            in_specs=[pl.BlockSpec((rows, columns), lambda i, place: (0, 0))] * n,
            out_specs=pl.BlockSpec(memory_space=pl.ANY),
            scratch_shapes=[pltpu.SemaphoreType.DMA((2 * n,))],
        ),
        compiler_params=params(16),
        cost_estimate=cost(MIB, 12 * MIB),
        name="collect",
    )(place, *pieces)


def back_body(place_ref, mkv_ref, mq_ref, tkv_ref, tq_ref, wm_ref, wt_ref, out_ref):
    out_ref[...] = (
        dot(wm_ref[:, :512], mkv_ref[...], NN)
        + dot(wm_ref[:, 512:], mq_ref[...], NN)
        + dot(wt_ref[:, :512], tkv_ref[...], NN)
        + dot(wt_ref[:, 512:], tq_ref[...], NN)
    )


def back(place, dkvt, dqt, theirs_kv, theirs_q, w_mine, w_theirs):
    rows = theirs_kv.shape[1]
    depth = w_mine.shape[1]
    width = 512
    n = place.shape[0] - 1

    def half_of(a):
        return pl.BlockSpec((a.shape[0], rows), lambda k, p: (0, p[0]))

    def whole(a):
        return pl.BlockSpec(a.shape, lambda k, p: (0, 0))

    weights = pl.BlockSpec((width, depth), lambda k, p: (p[1 + k], 0))
    return pl.pallas_call(
        back_body,
        out_shape=jax.ShapeDtypeStruct((n * width, rows), F32),
        grid_spec=pltpu.PrefetchScalarGridSpec(
            num_scalar_prefetch=1,
            grid=(n,),
            in_specs=[
                half_of(dkvt), half_of(dqt), whole(theirs_kv), whole(theirs_q), weights, weights,
            ],
            out_specs=pl.BlockSpec((width, rows), lambda k, p: (k, 0)),
        ),
        compiler_params=params(),
        cost_estimate=cost(4 * rows * n * width * depth, 8 * MIB),
        name="back",
    )(place, dkvt, dqt, theirs_kv, theirs_q, w_mine, w_theirs)


def turn_body(own_ref, at_ref, ab_ref, bt_ref, bb_ref, out_ref):
    upper = pl.program_id(0) < pl.num_programs(0) // 2
    after = jnp.where(upper, at_ref[...].astype(F32), ab_ref[...].astype(F32))
    before = jnp.where(upper, bt_ref[...].astype(F32), bb_ref[...].astype(F32))
    out_ref[...] = (own_ref[...] + after + before).astype(BF16).T


def turn(own, after, before):
    columns, rows = own.shape
    size = 256
    n = columns // size
    part = pl.BlockSpec((size, rows), lambda i: (i, 0))
    top = pl.BlockSpec((size, rows), lambda i: (jnp.minimum(i, n // 2 - 1), 0))
    bottom = pl.BlockSpec((size, rows), lambda i: (jnp.maximum(i - n // 2, 0), 0))
    return pl.pallas_call(
        turn_body,
        grid=(n,),
        in_specs=[part, top, bottom, top, bottom],
        out_specs=pl.BlockSpec((rows, size), lambda i: (0, i)),
        out_shape=jax.ShapeDtypeStruct((rows, columns), BF16),
        compiler_params=params(),
        cost_estimate=cost(4 * MIB, 6 * MIB),
        name="turn",
    )(own, *after, *before)


def swap(a):
    return lax.ppermute(a, "c", SWAP)


def ring(a, axis, by):
    return lax.ppermute(a, axis, [(i, (i + by) % 4) for i in range(4)])


def along(a, by, inner):
    pairs = []
    for z in range(4):
        for y in range(4):
            for c in range(2):
                over_y = (c == 0) == inner
                to = (z, (y + by) % 4) if over_y else ((z + by) % 4, y)
                pairs.append(((z * 4 + y) * 2 + c, (to[0] * 4 + to[1]) * 2 + c))
    return lax.ppermute(a, ("z", "y", "c"), pairs)


def gather_ring(a):
    half = a.shape[0] // 2
    before = along(a, 1, True)
    after = along(a, -1, True)
    top = along(before[:half], 1, True)
    bottom = along(after[half:], -1, True)
    return a, after, top, bottom, before


def gather_halves(top, bottom):
    top3 = along(top, 1, False)
    bottom1 = along(bottom, -1, False)
    bottom3 = along(bottom, 1, False)
    top1 = along(top, -1, False)
    top2 = along(top3, 1, False)
    bottom2 = along(bottom1, -1, False)
    return (top, bottom), (top1, bottom1), (top2, bottom2), (top3, bottom3)


def scatter_ring(far, after, before, send):
    far = far.astype(BF16)
    half = far.shape[0] // 2
    top = send(far[:half], 1).astype(F32)
    bottom = send(far[half:], -1).astype(F32)
    after_plain = send(after[half:].astype(BF16), 1)
    before_plain = send(before[:half].astype(BF16), -1)
    after_sum = send((after[:half] + top).astype(BF16), 1)
    before_sum = send((before[half:] + bottom).astype(BF16), -1)
    return (after_sum, after_plain), (before_plain, before_sum)


def scatter_small(part):
    far = part(2).astype(BF16)
    half = far.shape[0] // 2
    top = along(far[:half], 1, True).astype(F32)
    bottom = along(far[half:], -1, True).astype(F32)
    after, before = part(1), part(3)
    after = jnp.concatenate([after[:half] + top, after[half:]], 0).astype(BF16)
    before = jnp.concatenate([before[:half], before[half:] + bottom], 0).astype(BF16)
    after = along(after, 1, True).astype(F32)
    before = along(before, -1, True).astype(F32)
    return part(0) + after + before


def scan_flags(inner, outer, direction):
    inner = inner if direction == 1 else 3 - inner
    outer = outer if direction == 1 else 3 - outer
    return tuple((inner >= by, outer + by > 3) for by in (1, 3, 2))


def scan_chips(state, first, flags, direction):
    near = [along(state, direction * by, True).astype(F32) for by in (1, 3, 2)]
    own = state.astype(F32)
    ahead = jnp.zeros_like(own)
    for (passed, _), a in zip(flags, near):
        ahead = ahead + jnp.where(passed, a, 0.0)
    every = near[0] + near[1] + near[2] + own
    straight = jnp.where(first, every, ahead + own).astype(BF16)
    wrapped = jnp.where(first, 0.0, ahead).astype(BF16)
    total = ahead
    for by, (_, wraps) in zip((1, 3, 2), flags):
        message = jnp.where(wraps, wrapped, straight)
        total = total + along(message, direction * by, False).astype(F32)
    return total


def in_order(first, mine, theirs, axis=0):
    one = jnp.where(first, mine, theirs)
    two = jnp.where(first, theirs, mine)
    return jnp.concatenate([one, two], axis)


def half_of(first, a, axis):
    size = a.shape[axis] // 2
    low = lax.slice_in_dim(a, 0, size, axis=axis)
    high = lax.slice_in_dim(a, size, 2 * size, axis=axis)
    return jnp.where(first, low, high), jnp.where(first, high, low)


def per_device(tokens, w_query, w_key, w_value, omega_seed, grad_out):
    core, x, y, z = (lax.axis_index(name).astype(jnp.int32) for name in ("c", "x", "y", "z"))
    outer, inner = jnp.where(core == 0, z, y), jnp.where(core == 0, y, z)
    step = jnp.arange(4, dtype=jnp.int32)
    along_outer, along_inner = (outer + step) % 4, (inner + step) % 4
    chip = jnp.where(
        core == 0,
        along_outer[:, None] * 4 + along_inner[None, :],
        along_inner[None, :] * 4 + along_outer[:, None],
    ).reshape(16)

    def place_of(*steps):
        rows = [2 * lax.rem(x + by, 4) + i for by in steps for i in range(2)]
        return jnp.stack([core] + rows)

    where = (
        core == 0,
        jnp.concatenate([chip, core[None]]),
        chip,
        core[None],
        place_of(2),
        place_of(1, 3),
        place_of(0),
        scan_flags(inner, outer, 1),
        scan_flags(inner, outer, -1),
    )
    where, tokens, w_query, w_key, w_value, omega_seed, grad_out = lax.optimization_barrier(
        (where, tokens, w_query, w_key, w_value, omega_seed, grad_out)
    )
    first, idx, chip, core, far_place, side_place, own_place, ahead_flags, behind_flags = where

    def heads_of(*arrays):
        pairs = [half_of(first, a, 1) for a in arrays]
        return [jnp.concatenate([p[i] for p in pairs], 1) for i in range(2)]

    w_mine, w_give = heads_of(w_key, w_value, w_query)
    w_got = swap(w_give)
    w_chip = in_order(first, w_mine, w_got)
    g_mine, g_give = heads_of(grad_out)
    g_give, _ = lax.optimization_barrier((g_give, w_got))
    g_got = swap(g_give)
    g = in_order(first, g_mine, g_got)
    tokens_late, _ = lax.optimization_barrier((tokens, g_got))
    other = swap(tokens_late)
    seed = half_of(first, omega_seed, 0)[0].astype(BF16)

    w0, w1, w2_top, w2_bottom, w3 = gather_ring(w_chip)
    w_groups = gather_halves(
        jnp.concatenate([w0, w1], 0), jnp.concatenate([w2_top, w2_bottom, w3], 0)
    )
    arranged = [arrange(idx, tokens, other, a) for a in range(4)]
    xs = [a[0] for a in arranged]
    acc = project(first_body, [], [xs[0]], list(w_groups[0]), F32)
    pieces = list(w_groups[1] + w_groups[3])
    acc = project(more_body, [acc], [xs[1], xs[3]], pieces, F32)
    kvq = project(end_body, [acc], [xs[2]], list(w_groups[2]), BF16)

    kf, before, total = keys_stage(kvq, seed)
    prefix = scan_chips(total, first, ahead_flags, 1)
    weights = collect(chip, [p for pair in w_groups for p in pair])
    weights_theirs = swap(weights)
    qf, s, num, den = local_stage(kvq, kf, seed, before)
    gn, gd, later = ratio_stage(qf, num, den, g, prefix)
    suffix = scan_chips(later, first, behind_flags, -1)
    dq, dqt, dkf, dv = middle_stage(kvq, kf, qf, s, gn, gd, seed, before, prefix)
    dkv, dkvt = last_stage(kvq, kf, dkf, dv, seed, suffix)

    theirs_q = swap(half_of(first, dqt, 1)[1])
    theirs_kv = swap(half_of(first, dkvt, 1)[1])

    def group(a):
        return wgrad(arranged[a][1], dkv, dq)

    def quarters(place):
        return back(place, dkvt, dqt, theirs_kv, theirs_q, weights, weights_theirs)

    after, before = scatter_ring(group(2), group(1), group(3), lambda a, by: along(a, by, False))
    own = group(0)
    half = own.shape[0] // 2
    row_sum = [
        own[i * half : (i + 1) * half] + after[i].astype(F32) + before[i].astype(F32)
        for i in range(2)
    ]

    def strip_of(b):
        size = half // 2
        return row_sum[b // 2][b % 2 * size : (b % 2 + 1) * size]

    total_w = scatter_small(strip_of).astype(BF16)

    sides = quarters(side_place)
    columns = sides.shape[0] // 2
    after, before = scatter_ring(
        quarters(far_place), sides[:columns], sides[columns:], lambda a, by: ring(a, "x", by)
    )
    input_grad = turn(quarters(own_place), after, before)

    keep, give = half_of(first, total_w, 0)
    return input_grad, *finish(core, keep, swap(give))


def solution(mesh):
    chips = Mesh(mesh.devices.reshape(4, 4, 2, 4), ("z", "y", "c", "x"))
    seq = ("z", "y", "c")
    placed = (
        P(seq, None),
        P(seq, "x"),
        P(seq, "x"),
        P(seq, "x"),
        P("x", None, None),
        P(seq, "x"),
    )
    specs = (P(seq, "x"), P(seq, "x"), P(seq, "x"), P(seq, "x"))

    return jax.shard_map(per_device, mesh=chips, in_specs=placed, out_specs=specs, check_vma=False)
```

profile of v0, /device:TPU:1, one launch (start us, length us, event | category | flops | bytes accessed | tf_op | source)
XLA Modules:
  0.0 197.3 jit_solution(12802217672573858146)
XLA Ops:
  3.8 1.5 collective-permute-start
  5.3 1.0 collective-permute-done
  6.7 1.2 collective-permute-done.1
  8.4 1.8 collective-permute-start.4
  10.2 2.2 %collective-permute-start.3 = (bf16[256,768]{1,0:T(8,128)(2,1)S(1)}, bf16[256,768]{1,0:T(8,128)(2,1)S(1)}, u32[]{:S(2)}, u32[]{:S(2)}) collective-permute-start(bf16[256,768]{1,0:T(8,128)(2,1)S(1)} %pad_maximum_fusion.2), channel_id=1, source_target_pairs={{0,24},{4,100},{8,0},{12,108},{16,8},{20,116},{24,16},{28,124},{32... | collective-permute-start | bytes 1179656 | tf_op jit(solution)/shard_map/ppermute | solution.py:589
  12.4 5.1 %collective-permute-done.4 = bf16[256,768]{1,0:T(8,128)(2,1)S(1)} collective-permute-done((bf16[256,768]{1,0:T(8,128)(2,1)S(1)}, bf16[256,768]{1,0:T(8,128)(2,1)S(1)}, u32[]{:S(2)}, u32[]{:S(2)}) %collective-permute-start.4) | collective-permute-done | bytes 393248 | tf_op jit(solution)/shard_map/ppermute | solution.py:589
  17.6 3.0 %collective-permute-start.6 = (bf16[128,768]{1,0:T(8,128)(2,1)S(1)}, bf16[128,768]{1,0:T(8,128)(2,1)S(1)}, u32[]{:S(2)}, u32[]{:S(2)}) collective-permute-start(bf16[128,768]{1,0:T(8,128)(2,1)S(1)} %slice.179), channel_id=1, source_target_pairs={{0,24},{4,100},{8,0},{12,108},{16,8},{20,116},{24,16},{28,124},{32... | collective-permute-start | bytes 589832 | tf_op jit(solution)/shard_map/ppermute | solution.py:589
  20.7 1.1 collective-permute-start.9
  21.8 1.8 collective-permute-done.5
  23.7 2.8 %collective-permute-start.8 = (bf16[512,768]{1,0:T(8,128)(2,1)S(1)}, bf16[512,768]{1,0:T(8,128)(2,1)S(1)}, u32[]{:S(2)}, u32[]{:S(2)}) collective-permute-start(bf16[512,768]{1,0:T(8,128)(2,1)S(1)} %constant_dynamic-update-slice_fusion.wb_ref.refs_1_), channel_id=1, source_target_pairs={{0,96},{4,28},{8,104},{12,4},{16,112},{20,12},{24,120},{28,20},{32... | collective-permute-start | bytes 2359304 | tf_op jit(solution)/shard_map/ppermute | solution.py:589
  26.7 1.3 collective-permute-start.10
  28.0 5.2 %collective-permute-done.9.rest_2_.refs_6_ = bf16[512,768]{1,0:T(8,128)(2,1)S(1)} collective-permute-done((bf16[512,768]{1,0:T(8,128)(2,1)S(1)}, bf16[512,768]{1,0:T(8,128)(2,1)S(1)}, u32[]{:S(2)}, u32[]{:S(2)}) %collective-permute-start.9) | collective-permute-done | bytes 786464 | tf_op jit(solution)/shard_map/ppermute | solution.py:589
  33.2 2.3 %collective-permute-done.8.rest_1_.refs_3_ = bf16[512,768]{1,0:T(8,128)(2,1)S(1)} collective-permute-done((bf16[512,768]{1,0:T(8,128)(2,1)S(1)}, bf16[512,768]{1,0:T(8,128)(2,1)S(1)}, u32[]{:S(2)}, u32[]{:S(2)}) %collective-permute-start.8) | collective-permute-done | bytes 786464 | tf_op jit(solution)/shard_map/ppermute | solution.py:589
  35.4 3.4 %collective-permute-start.12 = (bf16[512,768]{1,0:T(8,128)(2,1)S(1)}, bf16[512,768]{1,0:T(8,128)(2,1)S(1)}, u32[]{:S(2)}, u32[]{:S(2)}) collective-permute-start(bf16[512,768]{1,0:T(8,128)(2,1)S(1)} %collective-permute-done.8.rest_1_.refs_3_), channel_id=1, source_target_pairs={{0,96},{4,28},{8,104},{12,4},{16,112},{20,12},{24,120},{28,20},{32... | collective-permute-start | bytes 2359304 | tf_op jit(solution)/shard_map/ppermute | solution.py:589
  38.9 2.0 arrange.4
  40.9 2.0 %arrange.5 = (bf16[1024,1024]{1,0:T(8,128)(2,1)S(1)}, bf16[1024,1024]{1,0:T(8,128)(2,1)S(1)}) custom-call(s32[17]{0:T(128)S(1)} %pad_add_fusion.idx_ref, bf16[512,4096]{1,0:T(8,128)(2,1)S(1)} %copy-done, bf16[512,4096]{1,0:T(8,128)(2,1)S(1)} %collective-permute-done.2.other_ref), custom_call_target="tpu_custom_call" | custom-call | flops 4194304 | bytes 6291456 | tf_op jit(solution)/shard_map/arrange/pallas_call | solution.py:54
  42.9 2.0 %arrange.6 = (bf16[1024,1024]{1,0:T(8,128)(2,1)S(1)}, bf16[1024,1024]{1,0:T(8,128)(2,1)S(1)}) custom-call(s32[17]{0:T(128)S(1)} %pad_add_fusion.idx_ref, bf16[512,4096]{1,0:T(8,128)(2,1)S(1)} %copy-done, bf16[512,4096]{1,0:T(8,128)(2,1)S(1)} %collective-permute-done.2.other_ref), custom_call_target="tpu_custom_call" | custom-call | flops 4194304 | bytes 6291456 | tf_op jit(solution)/shard_map/arrange/pallas_call | solution.py:54
  44.8 2.0 %arrange.7 = (bf16[1024,1024]{1,0:T(8,128)(2,1)S(1)}, bf16[1024,1024]{1,0:T(8,128)(2,1)S(1)}) custom-call(s32[17]{0:T(128)S(1)} %pad_add_fusion.idx_ref, bf16[512,4096]{1,0:T(8,128)(2,1)S(1)} %copy-done, bf16[512,4096]{1,0:T(8,128)(2,1)S(1)} %collective-permute-done.2.other_ref), custom_call_target="tpu_custom_call" | custom-call | flops 4194304 | bytes 6291456 | tf_op jit(solution)/shard_map/arrange/pallas_call | solution.py:54
  46.8 2.3 %shard_map.93.acc_ref = f32[1024,768]{1,0:T(8,128)S(1)} custom-call(bf16[1024,1024]{1,0:T(8,128)(2,1)S(1)} %get-tuple-element.68.x_ref, bf16[512,768]{1,0:T(8,128)(2,1)S(1)} %pad_maximum_fusion.wa_ref.refs_0_, bf16[512,768]{1,0:T(8,128)(2,1)S(1)} %constant_dynamic-update-slice_fusion.wb_ref.refs_1_), custom_call_target="tpu_custom_call" | custom-call | flops 1610612736 | bytes 8388608 | tf_op jit(solution)/shard_map/pallas_call | solution.py:109
  49.2 4.0 %shard_map.94.acc_ref = f32[1024,768]{1,0:T(8,128)S(1)} custom-call(f32[1024,768]{1,0:T(8,128)S(1)} %shard_map.93.acc_ref, bf16[1024,1024]{1,0:T(8,128)(2,1)S(1)} %get-tuple-element.69.xa_ref, bf16[1024,1024]{1,0:T(8,128)(2,1)S(1)} %get-tuple-element.70.xb_ref, bf16[512,768]{1,0:T(8,128)(2,1)S(1)} %collective-permute-done.7.rest_0_.refs_2_, ...), custom_call_target="tpu_custom_call" | custom-call | flops 3221225472 | bytes 8388608 | tf_op jit(solution)/shard_map/pallas_call | solution.py:109
  53.2 2.4 %shard_map.95.k_ref.v_ref.q_ref = bf16[1024,768]{1,0:T(8,128)(2,1)S(1)} custom-call(f32[1024,768]{1,0:T(8,128)S(1)} %shard_map.94.acc_ref, bf16[1024,1024]{1,0:T(8,128)(2,1)S(1)} %get-tuple-element.71.x_ref, bf16[512,768]{1,0:T(8,128)(2,1)S(1)} %collective-permute-done.11.wa_ref.refs_4_, bf16[512,768]{1,0:T(8,128)(2,1)S(1)} %collective-permute-done.12.wb_ref.refs_5_), custom_call_target="tpu_custom_call" | custom-call | flops 1610612736 | bytes 8388608 | tf_op jit(solution)/shard_map/pallas_call | solution.py:109
  55.6 2.6 %keys_stage.1 = (bf16[1024,512]{1,0:T(8,128)(2,1)S(1)}, f32[4,2,144,256]{3,2,1,0:T(8,128)S(1)}, bf16[2,144,256]{2,1,0:T(8,128)(2,1)S(1)}) custom-call(bf16[1024,768]{1,0:T(8,128)(2,1)S(1)} %shard_map.95.k_ref.v_ref.q_ref, bf16[1024,768]{1,0:T(8,128)(2,1)S(1)} %shard_map.95.k_ref.v_ref.q_ref, bf16[2,128,256]{2,1,0:T(8,128)(2,1)S(1)} %select_convert_fusion.2.seed_ref), custom_call_target="tpu_custom_call" | custom-call | flops 268435456 | bytes 4194304 | tf_op jit(solution)/shard_map/keys_stage/pallas_call | solution.py:168
  58.3 3.1 %collective-permute-start.14 = (bf16[2,144,256]{2,1,0:T(8,128)(2,1)S(1)}, bf16[2,144,256]{2,1,0:T(8,128)(2,1)S(1)}, u32[]{:S(2)}, u32[]{:S(2)}) collective-permute-start(bf16[2,144,256]{2,1,0:T(8,128)(2,1)S(1)} %get-tuple-element.80), channel_id=1, source_target_pairs={{0,24},{4,100},{8,0},{12,108},{16,8},{20,116},{24,16},{28,124},{32... | collective-permute-start | bytes 442376 | tf_op jit(solution)/shard_map/ppermute | solution.py:589
  61.4 1.1 collective-permute-start.15
  62.6 1.3 collective-permute-done.13
  63.9 3.0 %collective-permute-done.15 = bf16[2,144,256]{2,1,0:T(8,128)(2,1)S(1)} collective-permute-done((bf16[2,144,256]{2,1,0:T(8,128)(2,1)S(1)}, bf16[2,144,256]{2,1,0:T(8,128)(2,1)S(1)}, u32[]{:S(2)}, u32[]{:S(2)}) %collective-permute-start.15) | collective-permute-done | bytes 147488 | tf_op jit(solution)/shard_map/ppermute | solution.py:589
  67.1 2.5 %collective-permute-start.17 = (bf16[2,144,256]{2,1,0:T(8,128)(2,1)S(1)}, bf16[2,144,256]{2,1,0:T(8,128)(2,1)S(1)}, u32[]{:S(2)}, u32[]{:S(2)}) collective-permute-start(bf16[2,144,256]{2,1,0:T(8,128)(2,1)S(1)} %get-tuple-element.140), channel_id=1, source_target_pairs={{0,96},{4,28},{8,104},{12,4},{16,112},{20,12},{24,120},{28,20},{32... | collective-permute-start | bytes 442376 | tf_op jit(solution)/shard_map/ppermute | solution.py:589
  70.3 4.0 %collect.1.wm_ref = bf16[4096,768]{1,0:T(8,128)(2,1)S(1)} custom-call(s32[16]{0:T(128)S(1)} %select_n.239.place_ref, bf16[512,768]{1,0:T(8,128)(2,1)S(1)} %pad_maximum_fusion.wa_ref.refs_0_, bf16[512,768]{1,0:T(8,128)(2,1)S(1)} %constant_dynamic-update-slice_fusion.wb_ref.refs_1_, bf16[512,768]{1,0:T(8,128)(2,1)S(1)} %collective-permute-done.7.rest_0_.refs_2_, ...), custom_call_target="tpu_custom_call" | custom-call | flops 1048576 | bytes 12582912 | tf_op jit(solution)/shard_map/collect/pallas_call | solution.py:492
  74.4 7.2 %collective-permute-start.27 = (bf16[4096,768]{1,0:T(8,128)(2,1)S(1)}, bf16[4096,768]{1,0:T(8,128)(2,1)S(1)}, u32[]{:S(2)}, u32[]{:S(2)}) collective-permute-start(bf16[4096,768]{1,0:T(8,128)(2,1)S(1)} %collect.1.wm_ref), channel_id=1, source_target_pairs={{0,4},{4,0},{1,5},{5,1},{2,6},{6,2},{3,7},{7,3},{8,12},{12,8},{9,1... | collective-permute-start | bytes 18874376 | tf_op jit(solution)/shard_map/ppermute | solution.py:574
  81.6 2.9 %local_stage.1 = (bf16[1024,512]{1,0:T(8,128)(2,1)S(1)}, bf16[1024,512]{1,0:T(8,128)(2,1)S(1)}, f32[1024,256]{1,0:T(8,128)S(1)}, f32[2,1024,1]{2,1,0:T(8,128)S(1)}) custom-call(bf16[1024,768]{1,0:T(8,128)(2,1)S(1)} %shard_map.95.k_ref.v_ref.q_ref, bf16[1024,768]{1,0:T(8,128)(2,1)S(1)} %shard_map.95.k_ref.v_ref.q_ref, ...), custom_call_target="tpu_custom_call" | custom-call | flops 671088640 | bytes 6291456 | tf_op jit(solution)/shard_map/local_stage/pallas_call | solution.py:214
  84.7 2.9 %ratio_stage.1 = (bf16[1024,256]{1,0:T(8,128)(2,1)S(1)}, f32[2,1024,1]{2,1,0:T(8,128)S(1)}, bf16[2,144,256]{2,1,0:T(8,128)(2,1)S(1)}) custom-call(bf16[1024,512]{1,0:T(8,128)(2,1)S(1)} %get-tuple-element.75.qf_ref, f32[1024,256]{1,0:T(8,128)S(1)} %get-tuple-element.77.num_ref, f32[2,1024,1]{2,1,0:T(8,128)S(1)} %get-tuple-element.78.den_ref, ...), custom_call_target="tpu_custom_call" | custom-call | flops 268435456 | bytes 4194304 | tf_op jit(solution)/shard_map/ratio_stage/pallas_call | solution.py:276
  87.7 2.1 %collective-permute-start.19 = (bf16[2,144,256]{2,1,0:T(8,128)(2,1)S(1)}, bf16[2,144,256]{2,1,0:T(8,128)(2,1)S(1)}, u32[]{:S(2)}, u32[]{:S(2)}) collective-permute-start(bf16[2,144,256]{2,1,0:T(8,128)(2,1)S(1)} %get-tuple-element.91), channel_id=1, source_target_pairs={{0,24},{4,100},{8,0},{12,108},{16,8},{20,116},{24,16},{28,124},{32... | collective-permute-start | bytes 442376 | tf_op jit(solution)/shard_map/ppermute | solution.py:589
  90.1 1.7 collective-permute-start.21
  92.5 4.3 %collective-permute-done.20 = bf16[2,144,256]{2,1,0:T(8,128)(2,1)S(1)} collective-permute-done((bf16[2,144,256]{2,1,0:T(8,128)(2,1)S(1)}, bf16[2,144,256]{2,1,0:T(8,128)(2,1)S(1)}, u32[]{:S(2)}, u32[]{:S(2)}) %collective-permute-start.20) | collective-permute-done | bytes 147488 | tf_op jit(solution)/shard_map/ppermute | solution.py:589
  97.1 4.3 %collective-permute-start.24 = (bf16[2,144,256]{2,1,0:T(8,128)(2,1)S(1)}, bf16[2,144,256]{2,1,0:T(8,128)(2,1)S(1)}, u32[]{:S(2)}, u32[]{:S(2)}) collective-permute-start(bf16[2,144,256]{2,1,0:T(8,128)(2,1)S(1)} %get-tuple-element.139), channel_id=1, source_target_pairs={{0,64},{4,20},{8,72},{12,28},{16,80},{20,4},{24,88},{28,12},{32,96... | collective-permute-start | bytes 442376 | tf_op jit(solution)/shard_map/ppermute | solution.py:589
  101.5 4.7 %middle_stage.1 = (bf16[1024,256]{1,0:T(8,128)(2,1)S(1)}, bf16[256,1024]{1,0:T(8,128)(2,1)S(1)}, f32[1024,512]{1,0:T(8,128)S(1)}, f32[1024,256]{1,0:T(8,128)S(1)}) custom-call(bf16[1024,768]{1,0:T(8,128)(2,1)S(1)} %shard_map.95.k_ref.v_ref.q_ref, bf16[1024,768]{1,0:T(8,128)(2,1)S(1)} %shard_map.95.k_ref.v_ref.q_ref, ...), custom_call_target="tpu_custom_call" | custom-call | flops 1342177280 | bytes 10485760 | tf_op jit(solution)/shard_map/middle_stage/pallas_call | solution.py:344
  106.4 2.6 %last_stage.1 = (bf16[1024,512]{1,0:T(8,128)(2,1)S(1)}, bf16[512,1024]{1,0:T(8,128)(2,1)S(1)}) custom-call(bf16[1024,768]{1,0:T(8,128)(2,1)S(1)} %shard_map.95.k_ref.v_ref.q_ref, bf16[1024,768]{1,0:T(8,128)(2,1)S(1)} %shard_map.95.k_ref.v_ref.q_ref, bf16[1024,512]{1,0:T(8,128)(2,1)S(1)} %get-tuple-element.73.kf_ref, ...), custom_call_target="tpu_custom_call" | custom-call | flops 402653184 | bytes 6291456 | tf_op jit(solution)/shard_map/last_stage/pallas_call | solution.py:394
  109.0 2.3 %wgrad.6 = f32[1024,768]{1,0:T(8,128)S(1)} custom-call(bf16[1024,1024]{1,0:T(8,128)(2,1)S(1)} %get-tuple-element.107.x_ref, bf16[1024,512]{1,0:T(8,128)(2,1)S(1)} %get-tuple-element.104.dkv_ref, bf16[1024,256]{1,0:T(8,128)(2,1)S(1)} %get-tuple-element.105.dq_ref), custom_call_target="tpu_custom_call" | custom-call | flops 1610612736 | bytes 6291456 | tf_op jit(solution)/shard_map/wgrad/pallas_call | solution.py:430
  111.7 1.5 collective-permute-start.34
  113.2 1.2 collective-permute-start.38
  114.4 2.3 %wgrad.5 = f32[1024,768]{1,0:T(8,128)S(1)} custom-call(bf16[1024,1024]{1,0:T(8,128)(2,1)S(1)} %get-tuple-element.106.x_ref, bf16[1024,512]{1,0:T(8,128)(2,1)S(1)} %get-tuple-element.104.dkv_ref, bf16[1024,256]{1,0:T(8,128)(2,1)S(1)} %get-tuple-element.105.dq_ref), custom_call_target="tpu_custom_call" | custom-call | flops 1610612736 | bytes 6291456 | tf_op jit(solution)/shard_map/wgrad/pallas_call | solution.py:430
  117.2 2.3 %wgrad.7 = f32[1024,768]{1,0:T(8,128)S(1)} custom-call(bf16[1024,1024]{1,0:T(8,128)(2,1)S(1)} %get-tuple-element.108.x_ref, bf16[1024,512]{1,0:T(8,128)(2,1)S(1)} %get-tuple-element.104.dkv_ref, bf16[1024,256]{1,0:T(8,128)(2,1)S(1)} %get-tuple-element.105.dq_ref), custom_call_target="tpu_custom_call" | custom-call | flops 1610612736 | bytes 6291456 | tf_op jit(solution)/shard_map/wgrad/pallas_call | solution.py:430
  119.6 2.5 %collective-permute-start.36 = (bf16[512,768]{1,0:T(8,128)(2,1)S(1)}, bf16[512,768]{1,0:T(8,128)(2,1)S(1)}, u32[]{:S(2)}, u32[]{:S(2)}) collective-permute-start(bf16[512,768]{1,0:T(8,128)(2,1)S(1)} %slice.270), channel_id=1, source_target_pairs={{0,96},{4,28},{8,104},{12,4},{16,112},{20,12},{24,120},{28,20},{32... | collective-permute-start | bytes 2359304 | tf_op jit(solution)/shard_map/ppermute | solution.py:589
  122.1 2.0 %collective-permute-done.34 = bf16[512,768]{1,0:T(8,128)(2,1)S(1)} collective-permute-done((bf16[512,768]{1,0:T(8,128)(2,1)S(1)}, bf16[512,768]{1,0:T(8,128)(2,1)S(1)}, u32[]{:S(2)}, u32[]{:S(2)}) %collective-permute-start.34) | collective-permute-done | bytes 786464 | tf_op jit(solution)/shard_map/ppermute | solution.py:589
  124.8 2.5 %collective-permute-start.39 = (bf16[512,768]{1,0:T(8,128)(2,1)S(1)}, bf16[512,768]{1,0:T(8,128)(2,1)S(1)}, u32[]{:S(2)}, u32[]{:S(2)}) collective-permute-start(bf16[512,768]{1,0:T(8,128)(2,1)S(1)} %fusion), channel_id=1, source_target_pairs={{0,96},{4,28},{8,104},{12,4},{16,112},{20,12},{24,120},{28,20},{32... | collective-permute-start | bytes 2359304 | tf_op jit(solution)/shard_map/ppermute | solution.py:589
  127.3 2.3 %wgrad.4 = f32[1024,768]{1,0:T(8,128)S(1)} custom-call(bf16[1024,1024]{1,0:T(8,128)(2,1)S(1)} %get-tuple-element.103.x_ref, bf16[1024,512]{1,0:T(8,128)(2,1)S(1)} %get-tuple-element.104.dkv_ref, bf16[1024,256]{1,0:T(8,128)(2,1)S(1)} %get-tuple-element.105.dq_ref), custom_call_target="tpu_custom_call" | custom-call | flops 1610612736 | bytes 6291456 | tf_op jit(solution)/shard_map/wgrad/pallas_call | solution.py:430
  129.6 2.8 %collective-permute-done.37 = bf16[512,768]{1,0:T(8,128)(2,1)S(1)} collective-permute-done((bf16[512,768]{1,0:T(8,128)(2,1)S(1)}, bf16[512,768]{1,0:T(8,128)(2,1)S(1)}, u32[]{:S(2)}, u32[]{:S(2)}) %collective-permute-start.37) | collective-permute-done | bytes 786464 | tf_op jit(solution)/shard_map/ppermute | solution.py:589
  132.7 8.2 %collective-permute-done.35 = bf16[512,768]{1,0:T(8,128)(2,1)S(1)} collective-permute-done((bf16[512,768]{1,0:T(8,128)(2,1)S(1)}, bf16[512,768]{1,0:T(8,128)(2,1)S(1)}, u32[]{:S(2)}, u32[]{:S(2)}) %collective-permute-start.35) | collective-permute-done | bytes 786464 | tf_op jit(solution)/shard_map/ppermute | solution.py:589
  141.9 2.6 %collective-permute-start.42 = (bf16[128,768]{1,0:T(8,128)(2,1)S(1)}, bf16[128,768]{1,0:T(8,128)(2,1)S(1)}, u32[]{:S(2)}, u32[]{:S(2)}) collective-permute-start(bf16[128,768]{1,0:T(8,128)(2,1)S(1)} %get-tuple-element.130), channel_id=1, source_target_pairs={{0,24},{4,100},{8,0},{12,108},{16,8},{20,116},{24,16},{28,124},{32... | collective-permute-start | bytes 589832 | tf_op jit(solution)/shard_map/ppermute | solution.py:589
  144.5 3.0 %collective-permute-done.40 = bf16[128,768]{1,0:T(8,128)(2,1)S(1)} collective-permute-done((bf16[128,768]{1,0:T(8,128)(2,1)S(1)}, bf16[128,768]{1,0:T(8,128)(2,1)S(1)}, u32[]{:S(2)}, u32[]{:S(2)}) %collective-permute-start.40) | collective-permute-done | bytes 196640 | tf_op jit(solution)/shard_map/ppermute | solution.py:589
  147.7 2.9 %collective-permute-start.43 = (bf16[256,768]{1,0:T(8,128)(2,1)S(1)}, bf16[256,768]{1,0:T(8,128)(2,1)S(1)}, u32[]{:S(2)}, u32[]{:S(2)}) collective-permute-start(bf16[256,768]{1,0:T(8,128)(2,1)S(1)} %pad_maximum_fusion.4), channel_id=1, source_target_pairs={{0,24},{4,100},{8,0},{12,108},{16,8},{20,116},{24,16},{28,124},{32... | collective-permute-start | bytes 1179656 | tf_op jit(solution)/shard_map/ppermute | solution.py:589
  150.7 5.7 %collective-permute-start.25 = (bf16[512,512]{1,0:T(8,128)(2,1)S(1)}, bf16[512,512]{1,0:T(8,128)(2,1)S(1)}, u32[]{:S(2)}, u32[]{:S(2)}) collective-permute-start(bf16[512,512]{1,0:T(8,128)(2,1)S(1)} %slice_select_fusion), channel_id=1, source_target_pairs={{0,4},{4,0},{1,5},{5,1},{2,6},{6,2},{3,7},{7,3},{8,12},{12,8},{9,1... | collective-permute-start | bytes 1572872 | tf_op jit(solution)/shard_map/ppermute | solution.py:574
  156.7 1.6 collective-permute-done.26.tq_ref
  158.3 2.6 %back.5 = f32[1024,512]{1,0:T(8,128)S(1)} custom-call(s32[3]{0:T(128)S(1)} %get-tuple-element.101.place_ref, bf16[512,1024]{1,0:T(8,128)(2,1)S(1)} %get-tuple-element.97.mkv_ref, bf16[256,1024]{1,0:T(8,128)(2,1)S(1)} %get-tuple-element.98.mq_ref, bf16[512,512]{1,0:T(8,128)(2,1)S(1)} %collective-permute-done.25.tkv_ref, ...), custom_call_target="tpu_custom_call" | custom-call | flops 1610612736 | bytes 8388608 | tf_op jit(solution)/shard_map/back/pallas_call | solution.py:530
  161.1 1.3 collective-permute-start.28
  162.4 1.5 collective-permute-start.32
  163.9 4.6 %back.4 = f32[2048,512]{1,0:T(8,128)S(1)} custom-call(s32[5]{0:T(128)S(1)} %stack.43.place_ref, bf16[512,1024]{1,0:T(8,128)(2,1)S(1)} %get-tuple-element.97.mkv_ref, bf16[256,1024]{1,0:T(8,128)(2,1)S(1)} %get-tuple-element.98.mq_ref, bf16[512,512]{1,0:T(8,128)(2,1)S(1)} %collective-permute-done.25.tkv_ref, ...), custom_call_target="tpu_custom_call" | custom-call | flops 3221225472 | bytes 8388608 | tf_op jit(solution)/shard_map/back/pallas_call | solution.py:530
  168.9 2.7 %collective-permute-start.31 = (bf16[512,512]{1,0:T(8,128)(2,1)S(1)}, bf16[512,512]{1,0:T(8,128)(2,1)S(1)}, u32[]{:S(2)}, u32[]{:S(2)}) collective-permute-start(bf16[512,512]{1,0:T(8,128)(2,1)S(1)} %get-tuple-element.123), channel_id=1, source_target_pairs={{0,3},{1,0},{2,1},{3,2},{4,7},{5,4},{6,5},{7,6},{8,11},{9,8},{10,9... | collective-permute-start | bytes 1572872 | tf_op jit(solution)/shard_map/ppermute | solution.py:578
  173.8 1.7 collective-permute-start.33
  175.6 9.2 %collective-permute-start.44 = (bf16[128,768]{1,0:T(8,128)(2,1)S(1)}, bf16[128,768]{1,0:T(8,128)(2,1)S(1)}, u32[]{:S(2)}, u32[]{:S(2)}) collective-permute-start(bf16[128,768]{1,0:T(8,128)(2,1)S(1)} %get-tuple-element.134), channel_id=1, source_target_pairs={{0,4},{4,0},{1,5},{5,1},{2,6},{6,2},{3,7},{7,3},{8,12},{12,8},{9,1... | collective-permute-start | bytes 589832 | tf_op jit(solution)/shard_map/ppermute | solution.py:574
  184.8 1.1 collective-permute-done.44.got_ref
  186.8 2.6 %back.3.own_ref = f32[1024,512]{1,0:T(8,128)S(1)} custom-call(s32[3]{0:T(128)S(1)} %get-tuple-element.58.place_ref, bf16[512,1024]{1,0:T(8,128)(2,1)S(1)} %get-tuple-element.97.mkv_ref, bf16[256,1024]{1,0:T(8,128)(2,1)S(1)} %get-tuple-element.98.mq_ref, bf16[512,512]{1,0:T(8,128)(2,1)S(1)} %collective-permute-done.25.tkv_ref, ...), custom_call_target="tpu_custom_call" | custom-call | flops 1610612736 | bytes 8388608 | tf_op jit(solution)/shard_map/back/pallas_call | solution.py:530
  189.4 5.9 %collective-permute-done.29.at_ref = bf16[512,512]{1,0:T(8,128)(2,1)S(1)} collective-permute-done((bf16[512,512]{1,0:T(8,128)(2,1)S(1)}, bf16[512,512]{1,0:T(8,128)(2,1)S(1)}, u32[]{:S(2)}, u32[]{:S(2)}) %collective-permute-start.29) | collective-permute-done | bytes 524320 | tf_op jit(solution)/shard_map/ppermute | solution.py:578
  195.3 2.1 %turn.1 = bf16[512,1024]{1,0:T(8,128)(2,1)} custom-call(f32[1024,512]{1,0:T(8,128)S(1)} %back.3.own_ref, bf16[512,512]{1,0:T(8,128)(2,1)S(1)} %collective-permute-done.29.at_ref, bf16[512,512]{1,0:T(8,128)(2,1)S(1)} %collective-permute-done.30.ab_ref, bf16[512,512]{1,0:T(8,128)(2,1)S(1)} %collective-permute-done.31.bt_ref, ...), custom_call_target="tpu_custom_call" | custom-call | flops 4194304 | bytes 6291456 | tf_op jit(solution)/shard_map/turn/pallas_call | solution.py:561
  (105 shorter events, 14.2 us)
Async XLA Ops:
  0.6 4.7 %copy-start.1 = (bf16[512,512]{1,0:T(8,128)(2,1)S(1)}, bf16[512,512]{1,0:T(8,128)(2,1)}, u32[]{:S(2)}) copy-start(bf16[512,512]{1,0:T(8,128)(2,1)} %param.11) | copy-start | bytes 1572868
  3.8 2.5 %collective-permute-start = (bf16[128,768]{1,0:T(8,128)(2,1)S(1)}, bf16[128,768]{1,0:T(8,128)(2,1)S(1)}, u32[]{:S(2)}, u32[]{:S(2)}) collective-permute-start(bf16[128,768]{1,0:T(8,128)(2,1)S(1)} %pad_maximum_fusion.5), channel_id=1, source_target_pairs={{0,4},{4,0},{1,5},{5,1},{2,6},{6,2},{3,7},{7,3},{8,12},{12,8},{9,1... | collective-permute-start | bytes 589832 | tf_op jit(solution)/shard_map/ppermute | solution.py:574
  6.4 1.5 collective-permute-start.1
  7.9 31.0 %collective-permute-start.2 = (bf16[512,4096]{1,0:T(8,128)(2,1)}, bf16[512,4096]{1,0:T(8,128)(2,1)S(1)}, u32[]{:S(2)}, u32[]{:S(2)}) collective-permute-start(bf16[512,4096]{1,0:T(8,128)(2,1)} %own_ref.3), channel_id=1, source_target_pairs={{0,4},{4,0},{1,5},{5,1},{2,6},{6,2},{3,7},{7,3},{8,12},{12,8},{9,1... | collective-permute-start | bytes 12582920 | tf_op jit(solution)/shard_map/ppermute | solution.py:574
  8.3 30.5 %copy-start.2 = (s32[4,128,256]{2,1,0:T(8,128)S(1)}, s32[4,128,256]{2,1,0:T(8,128)}, u32[]{:S(2)}) copy-start(s32[4,128,256]{2,1,0:T(8,128)} %param.10) | copy-start | bytes 1572868
  8.4 9.1 %collective-permute-start.4 = (bf16[256,768]{1,0:T(8,128)(2,1)S(1)}, bf16[256,768]{1,0:T(8,128)(2,1)S(1)}, u32[]{:S(2)}, u32[]{:S(2)}) collective-permute-start(bf16[256,768]{1,0:T(8,128)(2,1)S(1)} %pad_maximum_fusion.2), channel_id=1, source_target_pairs={{0,8},{4,36},{8,16},{12,44},{16,24},{20,52},{24,0},{28,60},{32,40}... | collective-permute-start | bytes 1179656 | tf_op jit(solution)/shard_map/ppermute | solution.py:589
  10.2 7.4 %collective-permute-start.3 = (bf16[256,768]{1,0:T(8,128)(2,1)S(1)}, bf16[256,768]{1,0:T(8,128)(2,1)S(1)}, u32[]{:S(2)}, u32[]{:S(2)}) collective-permute-start(bf16[256,768]{1,0:T(8,128)(2,1)S(1)} %pad_maximum_fusion.2), channel_id=1, source_target_pairs={{0,24},{4,100},{8,0},{12,108},{16,8},{20,116},{24,16},{28,124},{32... | collective-permute-start | bytes 1179656 | tf_op jit(solution)/shard_map/ppermute | solution.py:589
  17.5 6.1 %collective-permute-start.5 = (bf16[128,768]{1,0:T(8,128)(2,1)S(1)}, bf16[128,768]{1,0:T(8,128)(2,1)S(1)}, u32[]{:S(2)}, u32[]{:S(2)}) collective-permute-start(bf16[128,768]{1,0:T(8,128)(2,1)S(1)} %slice.178), channel_id=1, source_target_pairs={{0,8},{4,36},{8,16},{12,44},{16,24},{20,52},{24,0},{28,60},{32,40}... | collective-permute-start | bytes 589832 | tf_op jit(solution)/shard_map/ppermute | solution.py:589
  17.6 21.3 %copy-start = (bf16[512,4096]{1,0:T(8,128)(2,1)S(1)}, bf16[512,4096]{1,0:T(8,128)(2,1)}, u32[]{:S(2)}) copy-start(bf16[512,4096]{1,0:T(8,128)(2,1)} %own_ref.3) | copy-start | bytes 12582916
  17.6 6.0 %collective-permute-start.6 = (bf16[128,768]{1,0:T(8,128)(2,1)S(1)}, bf16[128,768]{1,0:T(8,128)(2,1)S(1)}, u32[]{:S(2)}, u32[]{:S(2)}) collective-permute-start(bf16[128,768]{1,0:T(8,128)(2,1)S(1)} %slice.179), channel_id=1, source_target_pairs={{0,24},{4,100},{8,0},{12,108},{16,8},{20,116},{24,16},{28,124},{32... | collective-permute-start | bytes 589832 | tf_op jit(solution)/shard_map/ppermute | solution.py:589
  20.7 12.5 %collective-permute-start.9 = (bf16[512,768]{1,0:T(8,128)(2,1)S(1)}, bf16[512,768]{1,0:T(8,128)(2,1)S(1)}, u32[]{:S(2)}, u32[]{:S(2)}) collective-permute-start(bf16[512,768]{1,0:T(8,128)(2,1)S(1)} %pad_maximum_fusion.wa_ref.refs_0_), channel_id=1, source_target_pairs={{0,32},{4,12},{8,40},{12,20},{16,48},{20,28},{24,56},{28,4},{32,64... | collective-permute-start | bytes 2359304 | tf_op jit(solution)/shard_map/ppermute | solution.py:589
  23.7 11.7 %collective-permute-start.8 = (bf16[512,768]{1,0:T(8,128)(2,1)S(1)}, bf16[512,768]{1,0:T(8,128)(2,1)S(1)}, u32[]{:S(2)}, u32[]{:S(2)}) collective-permute-start(bf16[512,768]{1,0:T(8,128)(2,1)S(1)} %constant_dynamic-update-slice_fusion.wb_ref.refs_1_), channel_id=1, source_target_pairs={{0,96},{4,28},{8,104},{12,4},{16,112},{20,12},{24,120},{28,20},{32... | collective-permute-start | bytes 2359304 | tf_op jit(solution)/shard_map/ppermute | solution.py:589
  26.5 22.7 %collective-permute-start.7 = (bf16[512,768]{1,0:T(8,128)(2,1)S(1)}, bf16[512,768]{1,0:T(8,128)(2,1)S(1)}, u32[]{:S(2)}, u32[]{:S(2)}) collective-permute-start(bf16[512,768]{1,0:T(8,128)(2,1)S(1)} %pad_maximum_fusion.wa_ref.refs_0_), channel_id=1, source_target_pairs={{0,96},{4,28},{8,104},{12,4},{16,112},{20,12},{24,120},{28,20},{32... | collective-permute-start | bytes 2359304 | tf_op jit(solution)/shard_map/ppermute | solution.py:589
  26.7 22.5 %collective-permute-start.10 = (bf16[512,768]{1,0:T(8,128)(2,1)S(1)}, bf16[512,768]{1,0:T(8,128)(2,1)S(1)}, u32[]{:S(2)}, u32[]{:S(2)}) collective-permute-start(bf16[512,768]{1,0:T(8,128)(2,1)S(1)} %constant_dynamic-update-slice_fusion.wb_ref.refs_1_), channel_id=1, source_target_pairs={{0,32},{4,12},{8,40},{12,20},{16,48},{20,28},{24,56},{28,4},{32,64... | collective-permute-start | bytes 2359304 | tf_op jit(solution)/shard_map/ppermute | solution.py:589
  33.2 20.1 %collective-permute-start.11 = (bf16[512,768]{1,0:T(8,128)(2,1)S(1)}, bf16[512,768]{1,0:T(8,128)(2,1)S(1)}, u32[]{:S(2)}, u32[]{:S(2)}) collective-permute-start(bf16[512,768]{1,0:T(8,128)(2,1)S(1)} %collective-permute-done.9.rest_2_.refs_6_), channel_id=1, source_target_pairs={{0,32},{4,12},{8,40},{12,20},{16,48},{20,28},{24,56},{28,4},{32,64... | collective-permute-start | bytes 2359304 | tf_op jit(solution)/shard_map/ppermute | solution.py:589
  35.4 17.8 %collective-permute-start.12 = (bf16[512,768]{1,0:T(8,128)(2,1)S(1)}, bf16[512,768]{1,0:T(8,128)(2,1)S(1)}, u32[]{:S(2)}, u32[]{:S(2)}) collective-permute-start(bf16[512,768]{1,0:T(8,128)(2,1)S(1)} %collective-permute-done.8.rest_1_.refs_3_), channel_id=1, source_target_pairs={{0,96},{4,28},{8,104},{12,4},{16,112},{20,12},{24,120},{28,20},{32... | collective-permute-start | bytes 2359304 | tf_op jit(solution)/shard_map/ppermute | solution.py:589
  58.3 5.6 %collective-permute-start.13 = (bf16[2,144,256]{2,1,0:T(8,128)(2,1)S(1)}, bf16[2,144,256]{2,1,0:T(8,128)(2,1)S(1)}, u32[]{:S(2)}, u32[]{:S(2)}) collective-permute-start(bf16[2,144,256]{2,1,0:T(8,128)(2,1)S(1)} %get-tuple-element.80), channel_id=1, source_target_pairs={{0,8},{4,36},{8,16},{12,44},{16,24},{20,52},{24,0},{28,60},{32,40}... | collective-permute-start | bytes 442376 | tf_op jit(solution)/shard_map/ppermute | solution.py:589
  58.3 5.5 %collective-permute-start.14 = (bf16[2,144,256]{2,1,0:T(8,128)(2,1)S(1)}, bf16[2,144,256]{2,1,0:T(8,128)(2,1)S(1)}, u32[]{:S(2)}, u32[]{:S(2)}) collective-permute-start(bf16[2,144,256]{2,1,0:T(8,128)(2,1)S(1)} %get-tuple-element.80), channel_id=1, source_target_pairs={{0,24},{4,100},{8,0},{12,108},{16,8},{20,116},{24,16},{28,124},{32... | collective-permute-start | bytes 442376 | tf_op jit(solution)/shard_map/ppermute | solution.py:589
  61.4 5.5 %collective-permute-start.15 = (bf16[2,144,256]{2,1,0:T(8,128)(2,1)S(1)}, bf16[2,144,256]{2,1,0:T(8,128)(2,1)S(1)}, u32[]{:S(2)}, u32[]{:S(2)}) collective-permute-start(bf16[2,144,256]{2,1,0:T(8,128)(2,1)S(1)} %get-tuple-element.80), channel_id=1, source_target_pairs={{0,16},{4,68},{8,24},{12,76},{16,0},{20,84},{24,8},{28,92},{32,48}... | collective-permute-start | bytes 442376 | tf_op jit(solution)/shard_map/ppermute | solution.py:589
  67.1 17.4 %collective-permute-start.17 = (bf16[2,144,256]{2,1,0:T(8,128)(2,1)S(1)}, bf16[2,144,256]{2,1,0:T(8,128)(2,1)S(1)}, u32[]{:S(2)}, u32[]{:S(2)}) collective-permute-start(bf16[2,144,256]{2,1,0:T(8,128)(2,1)S(1)} %get-tuple-element.140), channel_id=1, source_target_pairs={{0,96},{4,28},{8,104},{12,4},{16,112},{20,12},{24,120},{28,20},{32... | collective-permute-start | bytes 442376 | tf_op jit(solution)/shard_map/ppermute | solution.py:589
  69.6 14.9 %collective-permute-start.18 = (bf16[2,144,256]{2,1,0:T(8,128)(2,1)S(1)}, bf16[2,144,256]{2,1,0:T(8,128)(2,1)S(1)}, u32[]{:S(2)}, u32[]{:S(2)}) collective-permute-start(bf16[2,144,256]{2,1,0:T(8,128)(2,1)S(1)} %get-tuple-element.141), channel_id=1, source_target_pairs={{0,64},{4,20},{8,72},{12,28},{16,80},{20,4},{24,88},{28,12},{32,96... | collective-permute-start | bytes 442376 | tf_op jit(solution)/shard_map/ppermute | solution.py:589
  69.6 14.9 %collective-permute-start.16 = (bf16[2,144,256]{2,1,0:T(8,128)(2,1)S(1)}, bf16[2,144,256]{2,1,0:T(8,128)(2,1)S(1)}, u32[]{:S(2)}, u32[]{:S(2)}) collective-permute-start(bf16[2,144,256]{2,1,0:T(8,128)(2,1)S(1)} %get-tuple-element.117), channel_id=1, source_target_pairs={{0,32},{4,12},{8,40},{12,20},{16,48},{20,28},{24,56},{28,4},{32,64... | collective-permute-start | bytes 442376 | tf_op jit(solution)/shard_map/ppermute | solution.py:589
  74.4 83.9 %collective-permute-start.27 = (bf16[4096,768]{1,0:T(8,128)(2,1)S(1)}, bf16[4096,768]{1,0:T(8,128)(2,1)S(1)}, u32[]{:S(2)}, u32[]{:S(2)}) collective-permute-start(bf16[4096,768]{1,0:T(8,128)(2,1)S(1)} %collect.1.wm_ref), channel_id=1, source_target_pairs={{0,4},{4,0},{1,5},{5,1},{2,6},{6,2},{3,7},{7,3},{8,12},{12,8},{9,1... | collective-permute-start | bytes 18874376 | tf_op jit(solution)/shard_map/ppermute | solution.py:574
  87.7 4.9 %collective-permute-start.19 = (bf16[2,144,256]{2,1,0:T(8,128)(2,1)S(1)}, bf16[2,144,256]{2,1,0:T(8,128)(2,1)S(1)}, u32[]{:S(2)}, u32[]{:S(2)}) collective-permute-start(bf16[2,144,256]{2,1,0:T(8,128)(2,1)S(1)} %get-tuple-element.91), channel_id=1, source_target_pairs={{0,24},{4,100},{8,0},{12,108},{16,8},{20,116},{24,16},{28,124},{32... | collective-permute-start | bytes 442376 | tf_op jit(solution)/shard_map/ppermute | solution.py:589
  89.8 7.1 %collective-permute-start.20 = (bf16[2,144,256]{2,1,0:T(8,128)(2,1)S(1)}, bf16[2,144,256]{2,1,0:T(8,128)(2,1)S(1)}, u32[]{:S(2)}, u32[]{:S(2)}) collective-permute-start(bf16[2,144,256]{2,1,0:T(8,128)(2,1)S(1)} %get-tuple-element.91), channel_id=1, source_target_pairs={{0,8},{4,36},{8,16},{12,44},{16,24},{20,52},{24,0},{28,60},{32,40}... | collective-permute-start | bytes 442376 | tf_op jit(solution)/shard_map/ppermute | solution.py:589
  90.1 6.7 %collective-permute-start.21 = (bf16[2,144,256]{2,1,0:T(8,128)(2,1)S(1)}, bf16[2,144,256]{2,1,0:T(8,128)(2,1)S(1)}, u32[]{:S(2)}, u32[]{:S(2)}) collective-permute-start(bf16[2,144,256]{2,1,0:T(8,128)(2,1)S(1)} %get-tuple-element.91), channel_id=1, source_target_pairs={{0,16},{4,68},{8,24},{12,76},{16,0},{20,84},{24,8},{28,92},{32,48}... | collective-permute-start | bytes 442376 | tf_op jit(solution)/shard_map/ppermute | solution.py:589
  97.1 9.2 %collective-permute-start.23 = (bf16[2,144,256]{2,1,0:T(8,128)(2,1)S(1)}, bf16[2,144,256]{2,1,0:T(8,128)(2,1)S(1)}, u32[]{:S(2)}, u32[]{:S(2)}) collective-permute-start(bf16[2,144,256]{2,1,0:T(8,128)(2,1)S(1)} %get-tuple-element.138), channel_id=1, source_target_pairs={{0,32},{4,12},{8,40},{12,20},{16,48},{20,28},{24,56},{28,4},{32,64... | collective-permute-start | bytes 442376 | tf_op jit(solution)/shard_map/ppermute | solution.py:589
  97.1 9.1 %collective-permute-start.24 = (bf16[2,144,256]{2,1,0:T(8,128)(2,1)S(1)}, bf16[2,144,256]{2,1,0:T(8,128)(2,1)S(1)}, u32[]{:S(2)}, u32[]{:S(2)}) collective-permute-start(bf16[2,144,256]{2,1,0:T(8,128)(2,1)S(1)} %get-tuple-element.139), channel_id=1, source_target_pairs={{0,64},{4,20},{8,72},{12,28},{16,80},{20,4},{24,88},{28,12},{32,96... | collective-permute-start | bytes 442376 | tf_op jit(solution)/shard_map/ppermute | solution.py:589
  101.5 4.8 %collective-permute-start.22 = (bf16[2,144,256]{2,1,0:T(8,128)(2,1)S(1)}, bf16[2,144,256]{2,1,0:T(8,128)(2,1)S(1)}, u32[]{:S(2)}, u32[]{:S(2)}) collective-permute-start(bf16[2,144,256]{2,1,0:T(8,128)(2,1)S(1)} %get-tuple-element.114), channel_id=1, source_target_pairs={{0,96},{4,28},{8,104},{12,4},{16,112},{20,12},{24,120},{28,20},{32... | collective-permute-start | bytes 442376 | tf_op jit(solution)/shard_map/ppermute | solution.py:589
  111.7 12.4 %collective-permute-start.34 = (bf16[512,768]{1,0:T(8,128)(2,1)S(1)}, bf16[512,768]{1,0:T(8,128)(2,1)S(1)}, u32[]{:S(2)}, u32[]{:S(2)}) collective-permute-start(bf16[512,768]{1,0:T(8,128)(2,1)S(1)} %get-tuple-element.126), channel_id=1, source_target_pairs={{0,32},{4,12},{8,40},{12,20},{16,48},{20,28},{24,56},{28,4},{32,64... | collective-permute-start | bytes 2359304 | tf_op jit(solution)/shard_map/ppermute | solution.py:589
  113.2 11.4 %collective-permute-start.38 = (bf16[512,768]{1,0:T(8,128)(2,1)S(1)}, bf16[512,768]{1,0:T(8,128)(2,1)S(1)}, u32[]{:S(2)}, u32[]{:S(2)}) collective-permute-start(bf16[512,768]{1,0:T(8,128)(2,1)S(1)} %get-tuple-element.125), channel_id=1, source_target_pairs={{0,96},{4,28},{8,104},{12,4},{16,112},{20,12},{24,120},{28,20},{32... | collective-permute-start | bytes 2359304 | tf_op jit(solution)/shard_map/ppermute | solution.py:589
  116.8 15.7 %collective-permute-start.37 = (bf16[512,768]{1,0:T(8,128)(2,1)S(1)}, bf16[512,768]{1,0:T(8,128)(2,1)S(1)}, u32[]{:S(2)}, u32[]{:S(2)}) collective-permute-start(bf16[512,768]{1,0:T(8,128)(2,1)S(1)} %slice.269), channel_id=1, source_target_pairs={{0,32},{4,12},{8,40},{12,20},{16,48},{20,28},{24,56},{28,4},{32,64... | collective-permute-start | bytes 2359304 | tf_op jit(solution)/shard_map/ppermute | solution.py:589
  119.6 13.2 %collective-permute-start.36 = (bf16[512,768]{1,0:T(8,128)(2,1)S(1)}, bf16[512,768]{1,0:T(8,128)(2,1)S(1)}, u32[]{:S(2)}, u32[]{:S(2)}) collective-permute-start(bf16[512,768]{1,0:T(8,128)(2,1)S(1)} %slice.270), channel_id=1, source_target_pairs={{0,96},{4,28},{8,104},{12,4},{16,112},{20,12},{24,120},{28,20},{32... | collective-permute-start | bytes 2359304 | tf_op jit(solution)/shard_map/ppermute | solution.py:589
  124.3 16.7 %collective-permute-start.35 = (bf16[512,768]{1,0:T(8,128)(2,1)S(1)}, bf16[512,768]{1,0:T(8,128)(2,1)S(1)}, u32[]{:S(2)}, u32[]{:S(2)}) collective-permute-start(bf16[512,768]{1,0:T(8,128)(2,1)S(1)} %fusion.2), channel_id=1, source_target_pairs={{0,32},{4,12},{8,40},{12,20},{16,48},{20,28},{24,56},{28,4},{32,64... | collective-permute-start | bytes 2359304 | tf_op jit(solution)/shard_map/ppermute | solution.py:589
  124.8 16.4 %collective-permute-start.39 = (bf16[512,768]{1,0:T(8,128)(2,1)S(1)}, bf16[512,768]{1,0:T(8,128)(2,1)S(1)}, u32[]{:S(2)}, u32[]{:S(2)}) collective-permute-start(bf16[512,768]{1,0:T(8,128)(2,1)S(1)} %fusion), channel_id=1, source_target_pairs={{0,96},{4,28},{8,104},{12,4},{16,112},{20,12},{24,120},{28,20},{32... | collective-permute-start | bytes 2359304 | tf_op jit(solution)/shard_map/ppermute | solution.py:589
  141.7 5.8 %collective-permute-start.40 = (bf16[128,768]{1,0:T(8,128)(2,1)S(1)}, bf16[128,768]{1,0:T(8,128)(2,1)S(1)}, u32[]{:S(2)}, u32[]{:S(2)}) collective-permute-start(bf16[128,768]{1,0:T(8,128)(2,1)S(1)} %get-tuple-element.129), channel_id=1, source_target_pairs={{0,8},{4,36},{8,16},{12,44},{16,24},{20,52},{24,0},{28,60},{32,40}... | collective-permute-start | bytes 589832 | tf_op jit(solution)/shard_map/ppermute | solution.py:589
  141.9 5.7 %collective-permute-start.42 = (bf16[128,768]{1,0:T(8,128)(2,1)S(1)}, bf16[128,768]{1,0:T(8,128)(2,1)S(1)}, u32[]{:S(2)}, u32[]{:S(2)}) collective-permute-start(bf16[128,768]{1,0:T(8,128)(2,1)S(1)} %get-tuple-element.130), channel_id=1, source_target_pairs={{0,24},{4,100},{8,0},{12,108},{16,8},{20,116},{24,16},{28,124},{32... | collective-permute-start | bytes 589832 | tf_op jit(solution)/shard_map/ppermute | solution.py:589
  147.5 9.0 %collective-permute-start.41 = (bf16[256,768]{1,0:T(8,128)(2,1)S(1)}, bf16[256,768]{1,0:T(8,128)(2,1)S(1)}, u32[]{:S(2)}, u32[]{:S(2)}) collective-permute-start(bf16[256,768]{1,0:T(8,128)(2,1)S(1)} %pad_maximum_fusion.3), channel_id=1, source_target_pairs={{0,8},{4,36},{8,16},{12,44},{16,24},{20,52},{24,0},{28,60},{32,40}... | collective-permute-start | bytes 1179656 | tf_op jit(solution)/shard_map/ppermute | solution.py:589
  147.7 8.8 %collective-permute-start.43 = (bf16[256,768]{1,0:T(8,128)(2,1)S(1)}, bf16[256,768]{1,0:T(8,128)(2,1)S(1)}, u32[]{:S(2)}, u32[]{:S(2)}) collective-permute-start(bf16[256,768]{1,0:T(8,128)(2,1)S(1)} %pad_maximum_fusion.4), channel_id=1, source_target_pairs={{0,24},{4,100},{8,0},{12,108},{16,8},{20,116},{24,16},{28,124},{32... | collective-permute-start | bytes 1179656 | tf_op jit(solution)/shard_map/ppermute | solution.py:589
  150.7 7.6 %collective-permute-start.25 = (bf16[512,512]{1,0:T(8,128)(2,1)S(1)}, bf16[512,512]{1,0:T(8,128)(2,1)S(1)}, u32[]{:S(2)}, u32[]{:S(2)}) collective-permute-start(bf16[512,512]{1,0:T(8,128)(2,1)S(1)} %slice_select_fusion), channel_id=1, source_target_pairs={{0,4},{4,0},{1,5},{5,1},{2,6},{6,2},{3,7},{7,3},{8,12},{12,8},{9,1... | collective-permute-start | bytes 1572872 | tf_op jit(solution)/shard_map/ppermute | solution.py:574
  156.4 1.9 collective-permute-start.26
  161.1 11.3 %collective-permute-start.28 = (bf16[512,512]{1,0:T(8,128)(2,1)S(1)}, bf16[512,512]{1,0:T(8,128)(2,1)S(1)}, u32[]{:S(2)}, u32[]{:S(2)}) collective-permute-start(bf16[512,512]{1,0:T(8,128)(2,1)S(1)} %get-tuple-element.128), channel_id=1, source_target_pairs={{0,1},{1,2},{2,3},{3,0},{4,5},{5,6},{6,7},{7,4},{8,9},{9,10},{10,1... | collective-permute-start | bytes 1572872 | tf_op jit(solution)/shard_map/ppermute | solution.py:578
  162.4 10.0 %collective-permute-start.32 = (bf16[512,512]{1,0:T(8,128)(2,1)S(1)}, bf16[512,512]{1,0:T(8,128)(2,1)S(1)}, u32[]{:S(2)}, u32[]{:S(2)}) collective-permute-start(bf16[512,512]{1,0:T(8,128)(2,1)S(1)} %get-tuple-element.127), channel_id=1, source_target_pairs={{0,3},{1,0},{2,1},{3,2},{4,7},{5,4},{6,5},{7,6},{8,11},{9,8},{10,9... | collective-permute-start | bytes 1572872 | tf_op jit(solution)/shard_map/ppermute | solution.py:578
  168.8 20.6 %collective-permute-start.30 = (bf16[512,512]{1,0:T(8,128)(2,1)S(1)}, bf16[512,512]{1,0:T(8,128)(2,1)S(1)}, u32[]{:S(2)}, u32[]{:S(2)}) collective-permute-start(bf16[512,512]{1,0:T(8,128)(2,1)S(1)} %get-tuple-element.124), channel_id=1, source_target_pairs={{0,1},{1,2},{2,3},{3,0},{4,5},{5,6},{6,7},{7,4},{8,9},{9,10},{10,1... | collective-permute-start | bytes 1572872 | tf_op jit(solution)/shard_map/ppermute | solution.py:578
  168.9 20.5 %collective-permute-start.31 = (bf16[512,512]{1,0:T(8,128)(2,1)S(1)}, bf16[512,512]{1,0:T(8,128)(2,1)S(1)}, u32[]{:S(2)}, u32[]{:S(2)}) collective-permute-start(bf16[512,512]{1,0:T(8,128)(2,1)S(1)} %get-tuple-element.123), channel_id=1, source_target_pairs={{0,3},{1,0},{2,1},{3,2},{4,7},{5,4},{6,5},{7,6},{8,11},{9,8},{10,9... | collective-permute-start | bytes 1572872 | tf_op jit(solution)/shard_map/ppermute | solution.py:578
  172.8 22.5 %collective-permute-start.29 = (bf16[512,512]{1,0:T(8,128)(2,1)S(1)}, bf16[512,512]{1,0:T(8,128)(2,1)S(1)}, u32[]{:S(2)}, u32[]{:S(2)}) collective-permute-start(bf16[512,512]{1,0:T(8,128)(2,1)S(1)} %get-tuple-element.121), channel_id=1, source_target_pairs={{0,1},{1,2},{2,3},{3,0},{4,5},{5,6},{6,7},{7,4},{8,9},{9,10},{10,1... | collective-permute-start | bytes 1572872 | tf_op jit(solution)/shard_map/ppermute | solution.py:578
  173.8 21.4 %collective-permute-start.33 = (bf16[512,512]{1,0:T(8,128)(2,1)S(1)}, bf16[512,512]{1,0:T(8,128)(2,1)S(1)}, u32[]{:S(2)}, u32[]{:S(2)}) collective-permute-start(bf16[512,512]{1,0:T(8,128)(2,1)S(1)} %get-tuple-element.120), channel_id=1, source_target_pairs={{0,3},{1,0},{2,1},{3,2},{4,7},{5,4},{6,5},{7,6},{8,11},{9,8},{10,9... | collective-permute-start | bytes 1572872 | tf_op jit(solution)/shard_map/ppermute | solution.py:578
  175.6 10.3 %collective-permute-start.44 = (bf16[128,768]{1,0:T(8,128)(2,1)S(1)}, bf16[128,768]{1,0:T(8,128)(2,1)S(1)}, u32[]{:S(2)}, u32[]{:S(2)}) collective-permute-start(bf16[128,768]{1,0:T(8,128)(2,1)S(1)} %get-tuple-element.134), channel_id=1, source_target_pairs={{0,4},{4,0},{1,5},{5,1},{2,6},{6,2},{3,7},{7,3},{8,12},{12,8},{9,1... | collective-permute-start | bytes 589832 | tf_op jit(solution)/shard_map/ppermute | solution.py:574
where the time goes:
time: 200 us; the launch traced here: 197 us
  starting transfers between devices  78.7 us (39%)
  Pallas kernels  58.5 us (29%)
  waiting for transfers between devices  51.9 us (26%)
  other arithmetic  6.12 us (3%)
    ppermute x32, starting transfers between devices, along(): return lax.ppermute(a, ('z', 'y', 'c'), pairs)  46 us
    ppermute x32, waiting for transfers between devices, along(): return lax.ppermute(a, ('z', 'y', 'c'), pairs)  40.3 us
    ppermute x7, starting transfers between devices, swap(): return lax.ppermute(a, 'c', SWAP)  24.4 us
    pallas_call x3, Pallas kernels, back(): pl.pallas_call(back_body, out_shape=jax.ShapeDtypeStruct((n * width, rows...  9.75 us
    pallas_call x4, Pallas kernels, wgrad(): pl.pallas_call(wgrad_body, grid=(depth // size,), in_specs=[pl.BlockSpec(...  9.34 us
    pallas_call x3, Pallas kernels, project(): pl.pallas_call(body, grid=(tok // size,), in_specs=[tall(a) for a in acc...  8.75 us
    ppermute x6, starting transfers between devices, ring(): return lax.ppermute(a, axis, [(i, (i + by) % 4) for i in range(4)])  8.23 us
    pallas_call x4, Pallas kernels, arrange(): pl.pallas_call(arrange_body, out_shape=[jax.ShapeDtypeStruct((2 * size, 4...  7.89 us
  transfers between devices with their start and end apart: 45, of which 20 were waited for; matrix products, arithmetic and copies ran while one was open for 2% of the time, Pallas kernels for 25%

commit v1 on v0

--- a/solution.py
+++ b/solution.py
@@ -35,6 +35,37 @@
     return pl.CostEstimate(flops=flops, bytes_accessed=nbytes, transcendentals=0)
 
 
+def halve_body(core_ref, *refs):
+    *sources, mine_ref, give_ref = refs
+    core = core_ref[0]
+    half = sources[0].shape[1] // 2
+    mine = pl.ds(pl.multiple_of(core * half, half), half)
+    give = pl.ds(pl.multiple_of((1 - core) * half, half), half)
+    for i, ref in enumerate(sources):
+        cols = slice(half * i, half * i + half)
+        mine_ref[:, cols] = ref[:, mine]
+        give_ref[:, cols] = ref[:, give]
+
+
+def halve(core, sources):
+    size, columns = sources[0].shape
+    whole = pl.BlockSpec((size, columns), lambda i, core: (0, 0))
+    shape = (size, len(sources) * columns // 2)
+    return pl.pallas_call(
+        halve_body,
+        out_shape=[jax.ShapeDtypeStruct(shape, BF16)] * 2,
+        grid_spec=pltpu.PrefetchScalarGridSpec(
+            num_scalar_prefetch=1,
+            grid=(1,),
+            in_specs=[whole] * len(sources),
+            out_specs=[pl.BlockSpec(shape, lambda i, core: (0, 0))] * 2,
+        ),
+        compiler_params=params(56),
+        cost_estimate=cost(MIB, MIB),
+        name="halve",
+    )(core, *sources)
+
+
 def arrange_body(idx_ref, own_ref, other_ref, rows_ref, columns_ref):
     core = idx_ref[16]
     size = own_ref.shape[0]
@@ -89,8 +120,13 @@
     out_ref[...] = total
 
 
-def end_body(acc_ref, x_ref, wa_ref, wb_ref, out_ref):
-    out_ref[...] = (acc_ref[...] + halves_dot(x_ref, wa_ref, wb_ref)).astype(BF16)
+def top_body(acc_ref, x_ref, w_ref, out_ref):
+    out_ref[...] = acc_ref[...] + dot(x_ref[:, : w_ref.shape[0]], w_ref[...], NN)
+
+
+def end_body(acc_ref, x_ref, w_ref, out_ref):
+    out = acc_ref[...] + dot(x_ref[:, w_ref.shape[0] :], w_ref[...], NN)
+    out_ref[...] = out.astype(BF16)
 
 
 def project(body, acc, xs, ws, dtype):
@@ -139,26 +175,38 @@
     )
 
 
-def keys_body(k_ref, v_ref, seed_ref, kf_ref, before_ref, total_ref, carry_ref):
-    step = pl.program_id(0)
-
-    @pl.when(step == 0)
-    def _():
-        carry_ref[...] = jnp.zeros_like(carry_ref)
-
-    before_ref[0] = carry_ref[...]
-    for head in range(2):
-        cols = slice(128 * head, 128 * head + 128)
-        kf = features(k_ref[:, cols], seed_ref[head]).astype(BF16)
-        kf_ref[:, 256 * head : 256 * head + 256] = kf
-        main = dot(v_ref[:, cols], kf, TN)
-        row = jnp.sum(kf.astype(F32), 0, keepdims=True)
-        pad = jnp.zeros((STATE_ROWS - 129, 256), F32)
-        carry_ref[head] += jnp.concatenate([main, row, pad], 0)
-
-    @pl.when(step == pl.num_programs(0) - 1)
-    def _():
-        total_ref[...] = carry_ref[...].astype(BF16)
+PER_STEP = 2
+
+
+VMEM = pl.BlockSpec(memory_space=pltpu.VMEM)
+
+
+def over_chunks(n, body):
+    def step(i, _):
+        for part in range(PER_STEP):
+            start = (i * PER_STEP + part) * CHUNK
+            body(i * PER_STEP + part, pl.ds(pl.multiple_of(start, CHUNK), CHUNK))
+
+    lax.fori_loop(0, n // PER_STEP, step, None)
+
+
+def keys_body(kvq_ref, seed_ref, kf_ref, before_ref, total_ref, carry_ref):
+    carry_ref[...] = jnp.zeros_like(carry_ref)
+    pad = jnp.zeros((STATE_ROWS - 129, 256), F32)
+
+    def chunk(i, rows):
+        for head in range(2):
+            state = carry_ref[head]
+            before_ref[i, head] = state
+            kf = features(kvq_ref[rows, 128 * head : 128 * head + 128], seed_ref[head])
+            kf = kf.astype(BF16)
+            kf_ref[rows, 256 * head : 256 * head + 256] = kf
+            main = dot(kvq_ref[rows, 256 + 128 * head : 384 + 128 * head], kf, TN)
+            row = jnp.sum(kf.astype(F32), 0, keepdims=True)
+            carry_ref[head] = state + jnp.concatenate([main, row, pad], 0)
+
+    over_chunks(kvq_ref.shape[0] // CHUNK, chunk)
+    total_ref[...] = carry_ref[...].astype(BF16)
 
 
 def keys_stage(kvq, seed):
@@ -167,17 +215,8 @@
     state = (2, STATE_ROWS, 256)
     return pl.pallas_call(
         keys_body,
-        grid=(n,),
-        in_specs=[
-            pl.BlockSpec((CHUNK, 256), lambda i: (i, 0)),
-            pl.BlockSpec((CHUNK, 256), lambda i: (i, 1)),
-            pl.BlockSpec((2, 128, 256), lambda i: (0, 0, 0)),
-        ],
-        out_specs=[
-            pl.BlockSpec((CHUNK, 512), lambda i: (i, 0)),
-            pl.BlockSpec((1,) + state, lambda i: (i, 0, 0, 0)),
-            pl.BlockSpec(state, lambda i: (0, 0, 0)),
-        ],
+        in_specs=[VMEM] * 2,
+        out_specs=[VMEM] * 3,
         out_shape=[
             jax.ShapeDtypeStruct((tok, 512), BF16),
             jax.ShapeDtypeStruct((n,) + state, F32),
@@ -187,7 +226,7 @@
         compiler_params=params(),
         cost_estimate=cost(n * 2 * 4 * 256 * 256 * 128, 4 * MIB),
         name="keys_stage",
-    )(kvq, kvq, seed)
+    )(kvq, seed)
 
 
 def local_body(q_ref, v_ref, kf_ref, seed_ref, before_ref, qf_ref, s_ref, num_ref, den_ref):
@@ -240,33 +279,28 @@
 
 
 def ratio_body(qf_ref, num_ref, den_ref, g_ref, prefix_ref, gn_ref, gd_ref, total_ref, carry_ref):
-    step = pl.program_id(0)
-
-    @pl.when(step == 0)
-    def _():
-        carry_ref[...] = jnp.zeros_like(carry_ref)
-
-    for head in range(2):
-        cols = slice(128 * head, 128 * head + 128)
-        wide = slice(256 * head, 256 * head + 256)
-        qf = qf_ref[:, wide]
-        qf32 = qf.astype(F32)
-        main = prefix_ref[head, :128, :].astype(BF16)
-        row = prefix_ref[head, 128:129, :]
-        num = num_ref[:, cols] + dot(qf, main, NT)
-        den = den_ref[head] + jnp.sum(qf32 * row, -1, keepdims=True)
-        inverse = 1.0 / den
-        g = g_ref[:, cols].astype(F32)
-        gn = (g * inverse).astype(BF16)
-        gd = -jnp.sum(g * num, -1, keepdims=True) * inverse * inverse
-        gn_ref[:, cols] = gn
-        gd_ref[head] = gd
-        carry_ref[head, :128, :] += dot(gn, qf, TN)
-        carry_ref[head, 128:129, :] += jnp.sum(qf32 * gd, 0, keepdims=True)
-
-    @pl.when(step == pl.num_programs(0) - 1)
-    def _():
-        total_ref[...] = carry_ref[...].astype(BF16)
+    carry_ref[...] = jnp.zeros_like(carry_ref)
+
+    def chunk(i, rows):
+        for head in range(2):
+            cols = slice(128 * head, 128 * head + 128)
+            main = prefix_ref[head, :128, :].astype(BF16)
+            row = prefix_ref[head, 128:129, :]
+            qf = qf_ref[rows, 256 * head : 256 * head + 256]
+            qf32 = qf.astype(F32)
+            num = num_ref[rows, cols] + dot(qf, main, NT)
+            den = den_ref[head, rows] + jnp.sum(qf32 * row, -1, keepdims=True)
+            inverse = 1.0 / den
+            g = g_ref[rows, cols].astype(F32)
+            gn = (g * inverse).astype(BF16)
+            gd = -jnp.sum(g * num, -1, keepdims=True) * inverse * inverse
+            gn_ref[rows, cols] = gn
+            gd_ref[head, rows] = gd
+            carry_ref[head, :128, :] += dot(gn, qf, TN)
+            carry_ref[head, 128:129, :] += jnp.sum(qf32 * gd, 0, keepdims=True)
+
+    over_chunks(qf_ref.shape[0] // CHUNK, chunk)
+    total_ref[...] = carry_ref[...].astype(BF16)
 
 
 def ratio_stage(qf, num, den, g, prefix):
@@ -275,19 +309,8 @@
     state = (2, STATE_ROWS, 256)
     return pl.pallas_call(
         ratio_body,
-        grid=(n,),
-        in_specs=[
-            pl.BlockSpec((CHUNK, 512), lambda i: (i, 0)),
-            pl.BlockSpec((CHUNK, 256), lambda i: (i, 0)),
-            pl.BlockSpec((2, CHUNK, 1), lambda i: (0, i, 0)),
-            pl.BlockSpec((CHUNK, 256), lambda i: (i, 0)),
-            pl.BlockSpec(state, lambda i: (0, 0, 0)),
-        ],
-        out_specs=[
-            pl.BlockSpec((CHUNK, 256), lambda i: (i, 0)),
-            pl.BlockSpec((2, CHUNK, 1), lambda i: (0, i, 0)),
-            pl.BlockSpec(state, lambda i: (0, 0, 0)),
-        ],
+        in_specs=[VMEM] * 5,
+        out_specs=[VMEM] * 3,
         out_shape=[
             jax.ShapeDtypeStruct((tok, 256), BF16),
             jax.ShapeDtypeStruct((2, tok, 1), F32),
@@ -370,43 +393,34 @@
     )(kvq, kvq, kf, qf, s, gn, gd, seed, before, prefix)
 
 
-def last_body(k_ref, v_ref, kf_ref, dkf_ref, dv_ref, seed_ref, suffix_ref, out_ref, outt_ref):
-    for head in range(2):
-        cols = slice(128 * head, 128 * head + 128)
-        wide = slice(256 * head, 256 * head + 256)
-        kf = kf_ref[:, wide]
-        main = suffix_ref[head, :128, :].astype(BF16)
-        row = suffix_ref[head, 128:129, :]
-        dkf = dkf_ref[:, wide] + dot(v_ref[:, cols], main, NN) + row
-        dk = feature_grad(dkf * kf.astype(F32), k_ref[:, cols], seed_ref[head]).astype(BF16)
-        dv = (dv_ref[:, cols] + dot(kf, main, NT)).astype(BF16)
-        dv_cols = slice(256 + 128 * head, 384 + 128 * head)
-        out_ref[:, cols] = dk
-        out_ref[:, dv_cols] = dv
-        outt_ref[cols, :] = dk.T
-        outt_ref[dv_cols, :] = dv.T
+def last_body(kvq_ref, kf_ref, dkf_ref, dv_ref, seed_ref, suffix_ref, out_ref, outt_ref):
+    def chunk(i, rows):
+        for head in range(2):
+            cols = slice(128 * head, 128 * head + 128)
+            wide = slice(256 * head, 256 * head + 256)
+            dv_cols = slice(256 + 128 * head, 384 + 128 * head)
+            main = suffix_ref[head, :128, :].astype(BF16)
+            row = suffix_ref[head, 128:129, :]
+            kf = kf_ref[rows, wide]
+            dkf = dkf_ref[rows, wide] + dot(kvq_ref[rows, dv_cols], main, NN) + row
+            dk = feature_grad(dkf * kf.astype(F32), kvq_ref[rows, cols], seed_ref[head])
+            dk = dk.astype(BF16)
+            dv = (dv_ref[rows, cols] + dot(kf, main, NT)).astype(BF16)
+            out_ref[rows, cols] = dk
+            out_ref[rows, dv_cols] = dv
+            outt_ref[cols, rows] = dk.T
+            outt_ref[dv_cols, rows] = dv.T
+
+    over_chunks(kvq_ref.shape[0] // CHUNK, chunk)
 
 
 def last_stage(kvq, kf, dkf, dv, seed, suffix):
     tok = kf.shape[0]
     n = tok // CHUNK
-    state = (2, STATE_ROWS, 256)
     return pl.pallas_call(
         last_body,
-        grid=(n,),
-        in_specs=[
-            pl.BlockSpec((CHUNK, 256), lambda i: (i, 0)),
-            pl.BlockSpec((CHUNK, 256), lambda i: (i, 1)),
-            pl.BlockSpec((CHUNK, 512), lambda i: (i, 0)),
-            pl.BlockSpec((CHUNK, 512), lambda i: (i, 0)),
-            pl.BlockSpec((CHUNK, 256), lambda i: (i, 0)),
-            pl.BlockSpec((2, 128, 256), lambda i: (0, 0, 0)),
-            pl.BlockSpec(state, lambda i: (0, 0, 0)),
-        ],
-        out_specs=[
-            pl.BlockSpec((CHUNK, 512), lambda i: (i, 0)),
-            pl.BlockSpec((512, CHUNK), lambda i: (0, i)),
-        ],
+        in_specs=[VMEM] * 6,
+        out_specs=[VMEM] * 2,
         out_shape=[
             jax.ShapeDtypeStruct((tok, 512), BF16),
             jax.ShapeDtypeStruct((512, tok), BF16),
@@ -414,33 +428,33 @@
         compiler_params=params(),
         cost_estimate=cost(n * 2 * 6 * 256 * 256 * 128, 6 * MIB),
         name="last_stage",
-    )(kvq, kvq, kf, dkf, dv, seed, suffix)
-
-
-def wgrad_body(x_ref, dkv_ref, dq_ref, out_ref):
-    x = x_ref[...]
-    out_ref[:, :512] = dot(x, dkv_ref[...], NN)
-    out_ref[:, 512:] = dot(x, dq_ref[...], NN)
-
-
-def wgrad(x, dkv, dq):
+    )(kvq, kf, dkf, dv, seed, suffix)
+
+
+def early_body(x_ref, d_ref, out_ref):
+    out_ref[...] = dot(x_ref[...], d_ref[...], NN)
+
+
+def wgrad_body(x_ref, dkv_ref, early_ref, out_ref):
+    out_ref[:, :512] = dot(x_ref[...], dkv_ref[...], NN)
+    out_ref[:, 512:] = early_ref[...]
+
+
+def wgrad_call(body, x, d, early, columns):
     depth, tok = x.shape
-    columns = dkv.shape[1] + dq.shape[1]
     size = 256
-    return pl.pallas_call(
-        wgrad_body,
+    specs = [pl.BlockSpec((size, tok), lambda i: (i, 0)), pl.BlockSpec(d.shape, lambda i: (0, 0))]
+    specs += [pl.BlockSpec((size, a.shape[1]), lambda i: (i, 0)) for a in early]
+
+    return pl.pallas_call(
+        body,
         grid=(depth // size,),
-        in_specs=[
-            pl.BlockSpec((size, tok), lambda i: (i, 0)),
-            pl.BlockSpec(dkv.shape, lambda i: (0, 0)),
-            pl.BlockSpec(dq.shape, lambda i: (0, 0)),
-        ],
+        in_specs=specs,
         out_specs=pl.BlockSpec((size, columns), lambda i: (i, 0)),
         out_shape=jax.ShapeDtypeStruct((depth, columns), F32),
         compiler_params=params(),
         cost_estimate=cost(2 * tok * depth * columns, 6 * MIB),
-        name="wgrad",
-    )(x, dkv, dq)
+    )(x, d, *early)
 
 
 def finish_body(core_ref, keep_ref, got_ref, q_ref, k_ref, v_ref):
@@ -699,19 +713,11 @@
     )
     first, idx, chip, core, far_place, side_place, own_place, ahead_flags, behind_flags = where
 
-    def heads_of(*arrays):
-        pairs = [half_of(first, a, 1) for a in arrays]
-        return [jnp.concatenate([p[i] for p in pairs], 1) for i in range(2)]
-
-    w_mine, w_give = heads_of(w_key, w_value, w_query)
-    w_got = swap(w_give)
-    w_chip = in_order(first, w_mine, w_got)
-    g_mine, g_give = heads_of(grad_out)
-    g_give, _ = lax.optimization_barrier((g_give, w_got))
-    g_got = swap(g_give)
-    g = in_order(first, g_mine, g_got)
-    tokens_late, _ = lax.optimization_barrier((tokens, g_got))
-    other = swap(tokens_late)
+    w_mine, w_give = halve(core, (w_key, w_value, w_query))
+    w_chip = in_order(first, w_mine, swap(w_give))
+    g_got = swap(grad_out)
+    g = in_order(first, half_of(first, grad_out, 1)[0], half_of(first, g_got, 1)[0])
+    other = swap(tokens)
     seed = half_of(first, omega_seed, 0)[0].astype(BF16)
 
     w0, w1, w2_top, w2_bottom, w3 = gather_ring(w_chip)
@@ -723,7 +729,9 @@
     acc = project(first_body, [], [xs[0]], list(w_groups[0]), F32)
     pieces = list(w_groups[1] + w_groups[3])
     acc = project(more_body, [acc], [xs[1], xs[3]], pieces, F32)
-    kvq = project(end_body, [acc], [xs[2]], list(w_groups[2]), BF16)
+    top, bottom = w_groups[2]
+    acc = project(top_body, [acc], [xs[2]], [top], F32)
+    kvq = project(end_body, [acc], [xs[2]], [bottom], BF16)
 
     kf, before, total = keys_stage(kvq, seed)
     prefix = scan_chips(total, first, ahead_flags, 1)
@@ -739,7 +747,9 @@
     theirs_kv = swap(half_of(first, dkvt, 1)[1])
 
     def group(a):
-        return wgrad(arranged[a][1], dkv, dq)
+        x_rows = arranged[a][1]
+        early = wgrad_call(early_body, x_rows, dq, [], 256)
+        return wgrad_call(wgrad_body, x_rows, dkv, [early], 768)
 
     def quarters(place):
         return back(place, dkvt, dqt, theirs_kv, theirs_q, weights, weights_theirs)

time: 200 us -> 203 us (1.015)
  Pallas kernels: 58.5 us -> 62.6 us
    pallas_call x7 -> x12, Pallas kernels: 17.5 us -> 20.8 us  [the longest x8 12.3 us: wgrad_call(): pl.pallas_call(body, grid=(depth // size,), in_specs=specs, out_specs=pl....]
    ppermute x7, waiting for transfers between devices: 4.91 us -> 8.16 us  [swap(): return lax.ppermute(a, 'c', SWAP)]
    ppermute x32, starting transfers between devices: 46 us -> 43 us  [along(): return lax.ppermute(a, ('z', 'y', 'c'), pairs)]
    select_n x7 -> x3, other arithmetic: 2.8 us -> 0.11 us  [half_of(): return (jnp.where(first, low, high), jnp.where(first, high, low))]
    pallas_call x3 -> x4, Pallas kernels: 8.75 us -> 9.47 us  [project(): pl.pallas_call(body, grid=(tok // size,), in_specs=[tall(a) for a in acc...]
  transfers between devices with their start and end apart: 45 -> 45, of which waited for: 20 -> 19; matrix products, arithmetic and copies ran while one was open for 2% -> 2% of each run, Pallas kernels for 25% -> 29%
where the time goes in v1:
time: 203 us; the launch traced here: 200 us
  starting transfers between devices  77.2 us (38%)
  Pallas kernels  62.6 us (31%)
  waiting for transfers between devices  53.8 us (27%)
  other arithmetic  4.31 us (2%)
    ppermute x32, starting transfers between devices, along(): return lax.ppermute(a, ('z', 'y', 'c'), pairs)  43 us
    ppermute x32, waiting for transfers between devices, along(): return lax.ppermute(a, ('z', 'y', 'c'), pairs)  39 us
    ppermute x7, starting transfers between devices, swap(): return lax.ppermute(a, 'c', SWAP)  26 us
    pallas_call x8, Pallas kernels, wgrad_call(): pl.pallas_call(body, grid=(depth // size,), in_specs=specs, out_specs=pl....  12.3 us
    pallas_call x3, Pallas kernels, back(): pl.pallas_call(back_body, out_shape=jax.ShapeDtypeStruct((n * width, rows...  9.75 us
    pallas_call x4, Pallas kernels, project(): pl.pallas_call(body, grid=(tok // size,), in_specs=[tall(a) for a in acc...  9.47 us
    ppermute x6, starting transfers between devices, ring(): return lax.ppermute(a, axis, [(i, (i + by) % 4) for i in range(4)])  8.23 us
    ppermute x7, waiting for transfers between devices, swap(): return lax.ppermute(a, 'c', SWAP)  8.16 us
  transfers between devices with their start and end apart: 45, of which 19 were waited for; matrix products, arithmetic and copies ran while one was open for 2% of the time, Pallas kernels for 29%

profile of v1, /device:TPU:1, one launch (start us, length us, event | category | flops | bytes accessed | tf_op | source)
XLA Modules:
  0.0 200.0 jit_solution(4383353599928383374)
XLA Ops:
  1.1 1.4 collective-permute-start
  2.5 1.8 halve.1
  4.3 5.5 %collective-permute-done.1 = bf16[128,768]{1,0:T(8,128)(2,1)S(1)} collective-permute-done((bf16[128,768]{1,0:T(8,128)(2,1)}, bf16[128,768]{1,0:T(8,128)(2,1)S(1)}, u32[]{:S(2)}, u32[]{:S(2)}) %collective-permute-start.1) | collective-permute-done | bytes 196640 | tf_op jit(solution)/shard_map/ppermute | solution.py:588
  10.8 1.8 collective-permute-start.3
  12.6 2.2 %collective-permute-start.2 = (bf16[256,768]{1,0:T(8,128)(2,1)S(1)}, bf16[256,768]{1,0:T(8,128)(2,1)S(1)}, u32[]{:S(2)}, u32[]{:S(2)}) collective-permute-start(bf16[256,768]{1,0:T(8,128)(2,1)S(1)} %pad_maximum_fusion.2), channel_id=1, source_target_pairs={{0,24},{4,100},{8,0},{12,108},{16,8},{20,116},{24,16},{28,124},{32... | collective-permute-start | bytes 1179656 | tf_op jit(solution)/shard_map/ppermute | solution.py:603
  14.9 5.1 %collective-permute-done.3 = bf16[256,768]{1,0:T(8,128)(2,1)S(1)} collective-permute-done((bf16[256,768]{1,0:T(8,128)(2,1)S(1)}, bf16[256,768]{1,0:T(8,128)(2,1)S(1)}, u32[]{:S(2)}, u32[]{:S(2)}) %collective-permute-start.3) | collective-permute-done | bytes 393248 | tf_op jit(solution)/shard_map/ppermute | solution.py:603
  20.1 3.0 %collective-permute-start.5 = (bf16[128,768]{1,0:T(8,128)(2,1)S(1)}, bf16[128,768]{1,0:T(8,128)(2,1)S(1)}, u32[]{:S(2)}, u32[]{:S(2)}) collective-permute-start(bf16[128,768]{1,0:T(8,128)(2,1)S(1)} %slice.163), channel_id=1, source_target_pairs={{0,24},{4,100},{8,0},{12,108},{16,8},{20,116},{24,16},{28,124},{32... | collective-permute-start | bytes 589832 | tf_op jit(solution)/shard_map/ppermute | solution.py:603
  24.2 1.8 collective-permute-done.4
  26.1 3.0 %collective-permute-start.7 = (bf16[512,768]{1,0:T(8,128)(2,1)S(1)}, bf16[512,768]{1,0:T(8,128)(2,1)S(1)}, u32[]{:S(2)}, u32[]{:S(2)}) collective-permute-start(bf16[512,768]{1,0:T(8,128)(2,1)S(1)} %constant_dynamic-update-slice_fusion.wb_ref.refs_1_), channel_id=1, source_target_pairs={{0,96},{4,28},{8,104},{12,4},{16,112},{20,12},{24,120},{28,20},{32... | collective-permute-start | bytes 2359304 | tf_op jit(solution)/shard_map/ppermute | solution.py:603
  29.2 1.4 collective-permute-start.9
  30.6 5.0 %collective-permute-done.8.rest_2_.refs_6_ = bf16[512,768]{1,0:T(8,128)(2,1)S(1)} collective-permute-done((bf16[512,768]{1,0:T(8,128)(2,1)S(1)}, bf16[512,768]{1,0:T(8,128)(2,1)S(1)}, u32[]{:S(2)}, u32[]{:S(2)}) %collective-permute-start.8) | collective-permute-done | bytes 786464 | tf_op jit(solution)/shard_map/ppermute | solution.py:603
  35.6 2.4 %collective-permute-done.7.rest_1_.refs_3_ = bf16[512,768]{1,0:T(8,128)(2,1)S(1)} collective-permute-done((bf16[512,768]{1,0:T(8,128)(2,1)S(1)}, bf16[512,768]{1,0:T(8,128)(2,1)S(1)}, u32[]{:S(2)}, u32[]{:S(2)}) %collective-permute-start.7) | collective-permute-done | bytes 786464 | tf_op jit(solution)/shard_map/ppermute | solution.py:603
  38.0 3.4 %collective-permute-start.11 = (bf16[512,768]{1,0:T(8,128)(2,1)S(1)}, bf16[512,768]{1,0:T(8,128)(2,1)S(1)}, u32[]{:S(2)}, u32[]{:S(2)}) collective-permute-start(bf16[512,768]{1,0:T(8,128)(2,1)S(1)} %collective-permute-done.7.rest_1_.refs_3_), channel_id=1, source_target_pairs={{0,96},{4,28},{8,104},{12,4},{16,112},{20,12},{24,120},{28,20},{32... | collective-permute-start | bytes 2359304 | tf_op jit(solution)/shard_map/ppermute | solution.py:603
  41.5 5.5 %collective-permute-start.12 = (bf16[512,512]{1,0:T(8,128)(2,1)S(1)}, bf16[512,512]{1,0:T(8,128)(2,1)S(1)}, u32[]{:S(2)}, u32[]{:S(2)}) collective-permute-start(bf16[512,512]{1,0:T(8,128)(2,1)S(1)} %copy-done.2), channel_id=1, source_target_pairs={{0,4},{4,0},{1,5},{5,1},{2,6},{6,2},{3,7},{7,3},{8,12},{12,8},{9,1... | collective-permute-start | bytes 1572872 | tf_op jit(solution)/shard_map/ppermute | solution.py:588
  47.0 2.0 arrange.4
  49.0 2.0 arrange.5
  50.9 2.0 arrange.6
  52.9 2.0 arrange.7
  54.9 2.3 %shard_map.93.acc_ref = f32[1024,768]{1,0:T(8,128)S(1)} custom-call(bf16[1024,1024]{1,0:T(8,128)(2,1)S(1)} %get-tuple-element.61.x_ref, bf16[512,768]{1,0:T(8,128)(2,1)S(1)} %pad_maximum_fusion.wa_ref.refs_0_, bf16[512,768]{1,0:T(8,128)(2,1)S(1)} %constant_dynamic-update-slice_fusion.wb_ref.refs_1_), custom_call_target="tpu_custom_call" | custom-call | flops 1610612736 | bytes 8388608 | tf_op jit(solution)/shard_map/pallas_call | solution.py:145
  57.3 4.0 %shard_map.94.acc_ref = f32[1024,768]{1,0:T(8,128)S(1)} custom-call(f32[1024,768]{1,0:T(8,128)S(1)} %shard_map.93.acc_ref, bf16[1024,1024]{1,0:T(8,128)(2,1)S(1)} %get-tuple-element.69.xa_ref, bf16[1024,1024]{1,0:T(8,128)(2,1)S(1)} %get-tuple-element.70.xb_ref, bf16[512,768]{1,0:T(8,128)(2,1)S(1)} %collective-permute-done.6.rest_0_.refs_2_, ...), custom_call_target="tpu_custom_call" | custom-call | flops 3221225472 | bytes 8388608 | tf_op jit(solution)/shard_map/pallas_call | solution.py:145
  61.3 1.5 shard_map.95.acc_ref
  62.9 1.5 shard_map.96.kvq_ref.q_ref.v_ref
  64.4 2.2 %keys_stage.1 = (bf16[1024,512]{1,0:T(8,128)(2,1)S(1)}, f32[4,2,144,256]{3,2,1,0:T(8,128)S(1)}, bf16[2,144,256]{2,1,0:T(8,128)(2,1)S(1)}) custom-call(bf16[1024,768]{1,0:T(8,128)(2,1)S(1)} %shard_map.96.kvq_ref.q_ref.v_ref, bf16[2,128,256]{2,1,0:T(8,128)(2,1)S(1)} %select_convert_fusion.2.seed_ref), custom_call_target="tpu_custom_call" | custom-call | flops 268435456 | bytes 4194304 | tf_op jit(solution)/shard_map/keys_stage/pallas_call | solution.py:216
  66.7 2.7 %collective-permute-start.14 = (bf16[2,144,256]{2,1,0:T(8,128)(2,1)S(1)}, bf16[2,144,256]{2,1,0:T(8,128)(2,1)S(1)}, u32[]{:S(2)}, u32[]{:S(2)}) collective-permute-start(bf16[2,144,256]{2,1,0:T(8,128)(2,1)S(1)} %get-tuple-element.81), channel_id=1, source_target_pairs={{0,24},{4,100},{8,0},{12,108},{16,8},{20,116},{24,16},{28,124},{32... | collective-permute-start | bytes 442376 | tf_op jit(solution)/shard_map/ppermute | solution.py:603
  69.5 2.8 %collective-permute-done.13 = bf16[2,144,256]{2,1,0:T(8,128)(2,1)S(1)} collective-permute-done((bf16[2,144,256]{2,1,0:T(8,128)(2,1)S(1)}, bf16[2,144,256]{2,1,0:T(8,128)(2,1)S(1)}, u32[]{:S(2)}, u32[]{:S(2)}) %collective-permute-start.13) | collective-permute-done | bytes 147488 | tf_op jit(solution)/shard_map/ppermute | solution.py:603
  73.1 2.1 %collective-permute-done.15 = bf16[2,144,256]{2,1,0:T(8,128)(2,1)S(1)} collective-permute-done((bf16[2,144,256]{2,1,0:T(8,128)(2,1)S(1)}, bf16[2,144,256]{2,1,0:T(8,128)(2,1)S(1)}, u32[]{:S(2)}, u32[]{:S(2)}) %collective-permute-start.15) | collective-permute-done | bytes 147488 | tf_op jit(solution)/shard_map/ppermute | solution.py:603
  77.0 4.0 %collect.1.wm_ref = bf16[4096,768]{1,0:T(8,128)(2,1)S(1)} custom-call(s32[16]{0:T(128)S(1)} %select_n.211.place_ref, bf16[512,768]{1,0:T(8,128)(2,1)S(1)} %pad_maximum_fusion.wa_ref.refs_0_, bf16[512,768]{1,0:T(8,128)(2,1)S(1)} %constant_dynamic-update-slice_fusion.wb_ref.refs_1_, bf16[512,768]{1,0:T(8,128)(2,1)S(1)} %collective-permute-done.6.rest_0_.refs_2_, ...), custom_call_target="tpu_custom_call" | custom-call | flops 1048576 | bytes 12582912 | tf_op jit(solution)/shard_map/collect/pallas_call | solution.py:506
  81.0 2.2 %collective-permute-start.27 = (bf16[4096,768]{1,0:T(8,128)(2,1)S(1)}, bf16[4096,768]{1,0:T(8,128)(2,1)S(1)}, u32[]{:S(2)}, u32[]{:S(2)}) collective-permute-start(bf16[4096,768]{1,0:T(8,128)(2,1)S(1)} %collect.1.wm_ref), channel_id=1, source_target_pairs={{0,4},{4,0},{1,5},{5,1},{2,6},{6,2},{3,7},{7,3},{8,12},{12,8},{9,1... | collective-permute-start | bytes 18874376 | tf_op jit(solution)/shard_map/ppermute | solution.py:588
  83.3 3.0 %local_stage.1 = (bf16[1024,512]{1,0:T(8,128)(2,1)S(1)}, bf16[1024,512]{1,0:T(8,128)(2,1)S(1)}, f32[1024,256]{1,0:T(8,128)S(1)}, f32[2,1024,1]{2,1,0:T(8,128)S(1)}) custom-call(bf16[1024,768]{1,0:T(8,128)(2,1)S(1)} %shard_map.96.kvq_ref.q_ref.v_ref, bf16[1024,768]{1,0:T(8,128)(2,1)S(1)} %shard_map.96.kvq_ref.q_ref.v_ref, ...), custom_call_target="tpu_custom_call" | custom-call | flops 671088640 | bytes 6291456 | tf_op jit(solution)/shard_map/local_stage/pallas_call | solution.py:253
  86.5 2.5 %ratio_stage.1 = (bf16[1024,256]{1,0:T(8,128)(2,1)S(1)}, f32[2,1024,1]{2,1,0:T(8,128)S(1)}, bf16[2,144,256]{2,1,0:T(8,128)(2,1)S(1)}) custom-call(bf16[1024,512]{1,0:T(8,128)(2,1)S(1)} %get-tuple-element.75.qf_ref, f32[1024,256]{1,0:T(8,128)S(1)} %get-tuple-element.77.num_ref, f32[2,1024,1]{2,1,0:T(8,128)S(1)} %get-tuple-element.78.den_ref, ...), custom_call_target="tpu_custom_call" | custom-call | flops 268435456 | bytes 4194304 | tf_op jit(solution)/shard_map/ratio_stage/pallas_call | solution.py:310
  89.0 2.4 %collective-permute-start.19 = (bf16[2,144,256]{2,1,0:T(8,128)(2,1)S(1)}, bf16[2,144,256]{2,1,0:T(8,128)(2,1)S(1)}, u32[]{:S(2)}, u32[]{:S(2)}) collective-permute-start(bf16[2,144,256]{2,1,0:T(8,128)(2,1)S(1)} %get-tuple-element.92), channel_id=1, source_target_pairs={{0,24},{4,100},{8,0},{12,108},{16,8},{20,116},{24,16},{28,124},{32... | collective-permute-start | bytes 442376 | tf_op jit(solution)/shard_map/ppermute | solution.py:603
  91.4 2.9 %collective-permute-start.21 = (bf16[2,144,256]{2,1,0:T(8,128)(2,1)S(1)}, bf16[2,144,256]{2,1,0:T(8,128)(2,1)S(1)}, u32[]{:S(2)}, u32[]{:S(2)}) collective-permute-start(bf16[2,144,256]{2,1,0:T(8,128)(2,1)S(1)} %get-tuple-element.92), channel_id=1, source_target_pairs={{0,16},{4,68},{8,24},{12,76},{16,0},{20,84},{24,8},{28,92},{32,48}... | collective-permute-start | bytes 442376 | tf_op jit(solution)/shard_map/ppermute | solution.py:603
  94.3 2.6 %collective-permute-done.20 = bf16[2,144,256]{2,1,0:T(8,128)(2,1)S(1)} collective-permute-done((bf16[2,144,256]{2,1,0:T(8,128)(2,1)S(1)}, bf16[2,144,256]{2,1,0:T(8,128)(2,1)S(1)}, u32[]{:S(2)}, u32[]{:S(2)}) %collective-permute-start.20) | collective-permute-done | bytes 147488 | tf_op jit(solution)/shard_map/ppermute | solution.py:603
  96.9 1.5 collective-permute-done.21
  98.8 2.3 %collective-permute-start.24 = (bf16[2,144,256]{2,1,0:T(8,128)(2,1)S(1)}, bf16[2,144,256]{2,1,0:T(8,128)(2,1)S(1)}, u32[]{:S(2)}, u32[]{:S(2)}) collective-permute-start(bf16[2,144,256]{2,1,0:T(8,128)(2,1)S(1)} %get-tuple-element.139), channel_id=1, source_target_pairs={{0,64},{4,20},{8,72},{12,28},{16,80},{20,4},{24,88},{28,12},{32,96... | collective-permute-start | bytes 442376 | tf_op jit(solution)/shard_map/ppermute | solution.py:603
  101.4 4.8 %middle_stage.1 = (bf16[1024,256]{1,0:T(8,128)(2,1)S(1)}, bf16[256,1024]{1,0:T(8,128)(2,1)S(1)}, f32[1024,512]{1,0:T(8,128)S(1)}, f32[1024,256]{1,0:T(8,128)S(1)}) custom-call(bf16[1024,768]{1,0:T(8,128)(2,1)S(1)} %shard_map.96.kvq_ref.q_ref.v_ref, bf16[1024,768]{1,0:T(8,128)(2,1)S(1)} %shard_map.96.kvq_ref.q_ref.v_ref, ...), custom_call_target="tpu_custom_call" | custom-call | flops 1342177280 | bytes 10485760 | tf_op jit(solution)/shard_map/middle_stage/pallas_call | solution.py:367
  106.2 1.3 shard_map.101.early_ref
  107.7 2.0 last_stage.1
  109.6 1.8 shard_map.102
  112.9 1.6 collective-permute-start.38
  114.5 1.2 shard_map.99.early_ref
  115.7 1.3 shard_map.103.early_ref
  117.0 1.8 shard_map.100
  119.0 1.8 shard_map.104
  120.9 2.7 %collective-permute-start.36 = (bf16[512,768]{1,0:T(8,128)(2,1)S(1)}, bf16[512,768]{1,0:T(8,128)(2,1)S(1)}, u32[]{:S(2)}, u32[]{:S(2)}) collective-permute-start(bf16[512,768]{1,0:T(8,128)(2,1)S(1)} %slice.252), channel_id=1, source_target_pairs={{0,96},{4,28},{8,104},{12,4},{16,112},{20,12},{24,120},{28,20},{32... | collective-permute-start | bytes 2359304 | tf_op jit(solution)/shard_map/ppermute | solution.py:603
  124.6 2.7 %collective-permute-start.39 = (bf16[512,768]{1,0:T(8,128)(2,1)S(1)}, bf16[512,768]{1,0:T(8,128)(2,1)S(1)}, u32[]{:S(2)}, u32[]{:S(2)}) collective-permute-start(bf16[512,768]{1,0:T(8,128)(2,1)S(1)} %fusion), channel_id=1, source_target_pairs={{0,96},{4,28},{8,104},{12,4},{16,112},{20,12},{24,120},{28,20},{32... | collective-permute-start | bytes 2359304 | tf_op jit(solution)/shard_map/ppermute | solution.py:603
  127.4 1.2 shard_map.97.early_ref
  128.6 1.8 shard_map.98
  130.4 2.1 %collective-permute-done.37 = bf16[512,768]{1,0:T(8,128)(2,1)S(1)} collective-permute-done((bf16[512,768]{1,0:T(8,128)(2,1)S(1)}, bf16[512,768]{1,0:T(8,128)(2,1)S(1)}, u32[]{:S(2)}, u32[]{:S(2)}) %collective-permute-start.37) | collective-permute-done | bytes 786464 | tf_op jit(solution)/shard_map/ppermute | solution.py:603
  132.6 8.4 %collective-permute-done.35 = bf16[512,768]{1,0:T(8,128)(2,1)S(1)} collective-permute-done((bf16[512,768]{1,0:T(8,128)(2,1)S(1)}, bf16[512,768]{1,0:T(8,128)(2,1)S(1)}, u32[]{:S(2)}, u32[]{:S(2)}) %collective-permute-start.35) | collective-permute-done | bytes 786464 | tf_op jit(solution)/shard_map/ppermute | solution.py:603
  141.6 2.9 %collective-permute-start.42 = (bf16[128,768]{1,0:T(8,128)(2,1)S(1)}, bf16[128,768]{1,0:T(8,128)(2,1)S(1)}, u32[]{:S(2)}, u32[]{:S(2)}) collective-permute-start(bf16[128,768]{1,0:T(8,128)(2,1)S(1)} %get-tuple-element.132), channel_id=1, source_target_pairs={{0,24},{4,100},{8,0},{12,108},{16,8},{20,116},{24,16},{28,124},{32... | collective-permute-start | bytes 589832 | tf_op jit(solution)/shard_map/ppermute | solution.py:603
  144.6 2.7 %collective-permute-done.40 = bf16[128,768]{1,0:T(8,128)(2,1)S(1)} collective-permute-done((bf16[128,768]{1,0:T(8,128)(2,1)S(1)}, bf16[128,768]{1,0:T(8,128)(2,1)S(1)}, u32[]{:S(2)}, u32[]{:S(2)}) %collective-permute-start.40) | collective-permute-done | bytes 196640 | tf_op jit(solution)/shard_map/ppermute | solution.py:603
  148.5 3.2 %collective-permute-start.43 = (bf16[256,768]{1,0:T(8,128)(2,1)S(1)}, bf16[256,768]{1,0:T(8,128)(2,1)S(1)}, u32[]{:S(2)}, u32[]{:S(2)}) collective-permute-start(bf16[256,768]{1,0:T(8,128)(2,1)S(1)} %pad_maximum_fusion.4), channel_id=1, source_target_pairs={{0,24},{4,100},{8,0},{12,108},{16,8},{20,116},{24,16},{28,124},{32... | collective-permute-start | bytes 1179656 | tf_op jit(solution)/shard_map/ppermute | solution.py:603
  151.7 7.4 %collective-permute-start.25 = (bf16[512,512]{1,0:T(8,128)(2,1)S(1)}, bf16[512,512]{1,0:T(8,128)(2,1)S(1)}, u32[]{:S(2)}, u32[]{:S(2)}) collective-permute-start(bf16[512,512]{1,0:T(8,128)(2,1)S(1)} %slice_select_fusion), channel_id=1, source_target_pairs={{0,4},{4,0},{1,5},{5,1},{2,6},{6,2},{3,7},{7,3},{8,12},{12,8},{9,1... | collective-permute-start | bytes 1572872 | tf_op jit(solution)/shard_map/ppermute | solution.py:588
  159.4 1.6 collective-permute-done.26.tq_ref
  161.0 2.6 %back.5 = f32[1024,512]{1,0:T(8,128)S(1)} custom-call(s32[3]{0:T(128)S(1)} %get-tuple-element.102.place_ref, bf16[512,1024]{1,0:T(8,128)(2,1)S(1)} %get-tuple-element.98.mkv_ref, bf16[256,1024]{1,0:T(8,128)(2,1)S(1)} %get-tuple-element.99.mq_ref, bf16[512,512]{1,0:T(8,128)(2,1)S(1)} %collective-permute-done.25.tkv_ref, ...), custom_call_target="tpu_custom_call" | custom-call | flops 1610612736 | bytes 8388608 | tf_op jit(solution)/shard_map/back/pallas_call | solution.py:544
  165.1 1.5 collective-permute-start.32
  166.6 4.6 %back.4 = f32[2048,512]{1,0:T(8,128)S(1)} custom-call(s32[5]{0:T(128)S(1)} %stack.43.place_ref, bf16[512,1024]{1,0:T(8,128)(2,1)S(1)} %get-tuple-element.98.mkv_ref, bf16[256,1024]{1,0:T(8,128)(2,1)S(1)} %get-tuple-element.99.mq_ref, bf16[512,512]{1,0:T(8,128)(2,1)S(1)} %collective-permute-done.25.tkv_ref, ...), custom_call_target="tpu_custom_call" | custom-call | flops 3221225472 | bytes 8388608 | tf_op jit(solution)/shard_map/back/pallas_call | solution.py:544
  171.6 2.7 %collective-permute-start.31 = (bf16[512,512]{1,0:T(8,128)(2,1)S(1)}, bf16[512,512]{1,0:T(8,128)(2,1)S(1)}, u32[]{:S(2)}, u32[]{:S(2)}) collective-permute-start(bf16[512,512]{1,0:T(8,128)(2,1)S(1)} %get-tuple-element.123), channel_id=1, source_target_pairs={{0,3},{1,0},{2,1},{3,2},{4,7},{5,4},{6,5},{7,6},{8,11},{9,8},{10,9... | collective-permute-start | bytes 1572872 | tf_op jit(solution)/shard_map/ppermute | solution.py:592
  176.4 1.8 collective-permute-start.33
  178.2 9.3 %collective-permute-start.44 = (bf16[128,768]{1,0:T(8,128)(2,1)S(1)}, bf16[128,768]{1,0:T(8,128)(2,1)S(1)}, u32[]{:S(2)}, u32[]{:S(2)}) collective-permute-start(bf16[128,768]{1,0:T(8,128)(2,1)S(1)} %get-tuple-element.134), channel_id=1, source_target_pairs={{0,4},{4,0},{1,5},{5,1},{2,6},{6,2},{3,7},{7,3},{8,12},{12,8},{9,1... | collective-permute-start | bytes 589832 | tf_op jit(solution)/shard_map/ppermute | solution.py:588
  189.5 2.6 %back.3.own_ref = f32[1024,512]{1,0:T(8,128)S(1)} custom-call(s32[3]{0:T(128)S(1)} %get-tuple-element.58.place_ref, bf16[512,1024]{1,0:T(8,128)(2,1)S(1)} %get-tuple-element.98.mkv_ref, bf16[256,1024]{1,0:T(8,128)(2,1)S(1)} %get-tuple-element.99.mq_ref, bf16[512,512]{1,0:T(8,128)(2,1)S(1)} %collective-permute-done.25.tkv_ref, ...), custom_call_target="tpu_custom_call" | custom-call | flops 1610612736 | bytes 8388608 | tf_op jit(solution)/shard_map/back/pallas_call | solution.py:544
  192.1 5.9 %collective-permute-done.29.at_ref = bf16[512,512]{1,0:T(8,128)(2,1)S(1)} collective-permute-done((bf16[512,512]{1,0:T(8,128)(2,1)S(1)}, bf16[512,512]{1,0:T(8,128)(2,1)S(1)}, u32[]{:S(2)}, u32[]{:S(2)}) %collective-permute-start.29) | collective-permute-done | bytes 524320 | tf_op jit(solution)/shard_map/ppermute | solution.py:592
  198.0 2.0 %turn.1 = bf16[512,1024]{1,0:T(8,128)(2,1)} custom-call(f32[1024,512]{1,0:T(8,128)S(1)} %back.3.own_ref, bf16[512,512]{1,0:T(8,128)(2,1)S(1)} %collective-permute-done.29.at_ref, bf16[512,512]{1,0:T(8,128)(2,1)S(1)} %collective-permute-done.30.ab_ref, bf16[512,512]{1,0:T(8,128)(2,1)S(1)} %collective-permute-done.31.bt_ref, ...), custom_call_target="tpu_custom_call" | custom-call | flops 4194304 | bytes 6291456 | tf_op jit(solution)/shard_map/turn/pallas_call | solution.py:575
  (106 shorter events, 17.3 us)
Async XLA Ops:
  1.1 40.4 %collective-permute-start = (bf16[512,4096]{1,0:T(8,128)(2,1)}, bf16[512,4096]{1,0:T(8,128)(2,1)S(1)}, u32[]{:S(2)}, u32[]{:S(2)}) collective-permute-start(bf16[512,4096]{1,0:T(8,128)(2,1)} %own_ref.3), channel_id=1, source_target_pairs={{0,4},{4,0},{1,5},{5,1},{2,6},{6,2},{3,7},{7,3},{8,12},{12,8},{9,1... | collective-permute-start | bytes 12582920 | tf_op jit(solution)/shard_map/ppermute | solution.py:588
  4.3 5.5 %collective-permute-start.1 = (bf16[128,768]{1,0:T(8,128)(2,1)}, bf16[128,768]{1,0:T(8,128)(2,1)S(1)}, u32[]{:S(2)}, u32[]{:S(2)}) collective-permute-start(bf16[128,768]{1,0:T(8,128)(2,1)} %get-tuple-element.68), channel_id=1, source_target_pairs={{0,4},{4,0},{1,5},{5,1},{2,6},{6,2},{3,7},{7,3},{8,12},{12,8},{9,1... | collective-permute-start | bytes 589832 | tf_op jit(solution)/shard_map/ppermute | solution.py:588
  10.8 30.7 %copy-start.1 = (s32[4,128,256]{2,1,0:T(8,128)S(1)}, s32[4,128,256]{2,1,0:T(8,128)}, u32[]{:S(2)}) copy-start(s32[4,128,256]{2,1,0:T(8,128)} %param.10) | copy-start | bytes 1572868
  10.8 30.7 %copy-start.2 = (bf16[512,512]{1,0:T(8,128)(2,1)S(1)}, bf16[512,512]{1,0:T(8,128)(2,1)}, u32[]{:S(2)}) copy-start(bf16[512,512]{1,0:T(8,128)(2,1)} %param.11) | copy-start | bytes 1572868
  10.8 9.1 %collective-permute-start.3 = (bf16[256,768]{1,0:T(8,128)(2,1)S(1)}, bf16[256,768]{1,0:T(8,128)(2,1)S(1)}, u32[]{:S(2)}, u32[]{:S(2)}) collective-permute-start(bf16[256,768]{1,0:T(8,128)(2,1)S(1)} %pad_maximum_fusion.2), channel_id=1, source_target_pairs={{0,8},{4,36},{8,16},{12,44},{16,24},{20,52},{24,0},{28,60},{32,40}... | collective-permute-start | bytes 1179656 | tf_op jit(solution)/shard_map/ppermute | solution.py:603
  12.6 7.4 %collective-permute-start.2 = (bf16[256,768]{1,0:T(8,128)(2,1)S(1)}, bf16[256,768]{1,0:T(8,128)(2,1)S(1)}, u32[]{:S(2)}, u32[]{:S(2)}) collective-permute-start(bf16[256,768]{1,0:T(8,128)(2,1)S(1)} %pad_maximum_fusion.2), channel_id=1, source_target_pairs={{0,24},{4,100},{8,0},{12,108},{16,8},{20,116},{24,16},{28,124},{32... | collective-permute-start | bytes 1179656 | tf_op jit(solution)/shard_map/ppermute | solution.py:603
  20.0 6.1 %collective-permute-start.4 = (bf16[128,768]{1,0:T(8,128)(2,1)S(1)}, bf16[128,768]{1,0:T(8,128)(2,1)S(1)}, u32[]{:S(2)}, u32[]{:S(2)}) collective-permute-start(bf16[128,768]{1,0:T(8,128)(2,1)S(1)} %slice.162), channel_id=1, source_target_pairs={{0,8},{4,36},{8,16},{12,44},{16,24},{20,52},{24,0},{28,60},{32,40}... | collective-permute-start | bytes 589832 | tf_op jit(solution)/shard_map/ppermute | solution.py:603
  20.0 26.9 %copy-start = (bf16[512,4096]{1,0:T(8,128)(2,1)S(1)}, bf16[512,4096]{1,0:T(8,128)(2,1)}, u32[]{:S(2)}) copy-start(bf16[512,4096]{1,0:T(8,128)(2,1)} %own_ref.3) | copy-start | bytes 12582916
  20.1 6.0 %collective-permute-start.5 = (bf16[128,768]{1,0:T(8,128)(2,1)S(1)}, bf16[128,768]{1,0:T(8,128)(2,1)S(1)}, u32[]{:S(2)}, u32[]{:S(2)}) collective-permute-start(bf16[128,768]{1,0:T(8,128)(2,1)S(1)} %slice.163), channel_id=1, source_target_pairs={{0,24},{4,100},{8,0},{12,108},{16,8},{20,116},{24,16},{28,124},{32... | collective-permute-start | bytes 589832 | tf_op jit(solution)/shard_map/ppermute | solution.py:603
  23.1 12.5 %collective-permute-start.8 = (bf16[512,768]{1,0:T(8,128)(2,1)S(1)}, bf16[512,768]{1,0:T(8,128)(2,1)S(1)}, u32[]{:S(2)}, u32[]{:S(2)}) collective-permute-start(bf16[512,768]{1,0:T(8,128)(2,1)S(1)} %pad_maximum_fusion.wa_ref.refs_0_), channel_id=1, source_target_pairs={{0,32},{4,12},{8,40},{12,20},{16,48},{20,28},{24,56},{28,4},{32,64... | collective-permute-start | bytes 2359304 | tf_op jit(solution)/shard_map/ppermute | solution.py:603
  26.1 11.9 %collective-permute-start.7 = (bf16[512,768]{1,0:T(8,128)(2,1)S(1)}, bf16[512,768]{1,0:T(8,128)(2,1)S(1)}, u32[]{:S(2)}, u32[]{:S(2)}) collective-permute-start(bf16[512,768]{1,0:T(8,128)(2,1)S(1)} %constant_dynamic-update-slice_fusion.wb_ref.refs_1_), channel_id=1, source_target_pairs={{0,96},{4,28},{8,104},{12,4},{16,112},{20,12},{24,120},{28,20},{32... | collective-permute-start | bytes 2359304 | tf_op jit(solution)/shard_map/ppermute | solution.py:603
  29.1 28.2 %collective-permute-start.6 = (bf16[512,768]{1,0:T(8,128)(2,1)S(1)}, bf16[512,768]{1,0:T(8,128)(2,1)S(1)}, u32[]{:S(2)}, u32[]{:S(2)}) collective-permute-start(bf16[512,768]{1,0:T(8,128)(2,1)S(1)} %pad_maximum_fusion.wa_ref.refs_0_), channel_id=1, source_target_pairs={{0,96},{4,28},{8,104},{12,4},{16,112},{20,12},{24,120},{28,20},{32... | collective-permute-start | bytes 2359304 | tf_op jit(solution)/shard_map/ppermute | solution.py:603
  29.2 28.1 %collective-permute-start.9 = (bf16[512,768]{1,0:T(8,128)(2,1)S(1)}, bf16[512,768]{1,0:T(8,128)(2,1)S(1)}, u32[]{:S(2)}, u32[]{:S(2)}) collective-permute-start(bf16[512,768]{1,0:T(8,128)(2,1)S(1)} %constant_dynamic-update-slice_fusion.wb_ref.refs_1_), channel_id=1, source_target_pairs={{0,32},{4,12},{8,40},{12,20},{16,48},{20,28},{24,56},{28,4},{32,64... | collective-permute-start | bytes 2359304 | tf_op jit(solution)/shard_map/ppermute | solution.py:603
  35.6 25.7 %collective-permute-start.10 = (bf16[512,768]{1,0:T(8,128)(2,1)S(1)}, bf16[512,768]{1,0:T(8,128)(2,1)S(1)}, u32[]{:S(2)}, u32[]{:S(2)}) collective-permute-start(bf16[512,768]{1,0:T(8,128)(2,1)S(1)} %collective-permute-done.8.rest_2_.refs_6_), channel_id=1, source_target_pairs={{0,32},{4,12},{8,40},{12,20},{16,48},{20,28},{24,56},{28,4},{32,64... | collective-permute-start | bytes 2359304 | tf_op jit(solution)/shard_map/ppermute | solution.py:603
  38.0 24.9 %collective-permute-start.11 = (bf16[512,768]{1,0:T(8,128)(2,1)S(1)}, bf16[512,768]{1,0:T(8,128)(2,1)S(1)}, u32[]{:S(2)}, u32[]{:S(2)}) collective-permute-start(bf16[512,768]{1,0:T(8,128)(2,1)S(1)} %collective-permute-done.7.rest_1_.refs_3_), channel_id=1, source_target_pairs={{0,96},{4,28},{8,104},{12,4},{16,112},{20,12},{24,120},{28,20},{32... | collective-permute-start | bytes 2359304 | tf_op jit(solution)/shard_map/ppermute | solution.py:603
  41.5 27.9 %collective-permute-start.12 = (bf16[512,512]{1,0:T(8,128)(2,1)S(1)}, bf16[512,512]{1,0:T(8,128)(2,1)S(1)}, u32[]{:S(2)}, u32[]{:S(2)}) collective-permute-start(bf16[512,512]{1,0:T(8,128)(2,1)S(1)} %copy-done.2), channel_id=1, source_target_pairs={{0,4},{4,0},{1,5},{5,1},{2,6},{6,2},{3,7},{7,3},{8,12},{12,8},{9,1... | collective-permute-start | bytes 1572872 | tf_op jit(solution)/shard_map/ppermute | solution.py:588
  66.6 5.6 %collective-permute-start.13 = (bf16[2,144,256]{2,1,0:T(8,128)(2,1)S(1)}, bf16[2,144,256]{2,1,0:T(8,128)(2,1)S(1)}, u32[]{:S(2)}, u32[]{:S(2)}) collective-permute-start(bf16[2,144,256]{2,1,0:T(8,128)(2,1)S(1)} %get-tuple-element.81), channel_id=1, source_target_pairs={{0,8},{4,36},{8,16},{12,44},{16,24},{20,52},{24,0},{28,60},{32,40}... | collective-permute-start | bytes 442376 | tf_op jit(solution)/shard_map/ppermute | solution.py:603
  66.7 6.3 %collective-permute-start.14 = (bf16[2,144,256]{2,1,0:T(8,128)(2,1)S(1)}, bf16[2,144,256]{2,1,0:T(8,128)(2,1)S(1)}, u32[]{:S(2)}, u32[]{:S(2)}) collective-permute-start(bf16[2,144,256]{2,1,0:T(8,128)(2,1)S(1)} %get-tuple-element.81), channel_id=1, source_target_pairs={{0,24},{4,100},{8,0},{12,108},{16,8},{20,116},{24,16},{28,124},{32... | collective-permute-start | bytes 442376 | tf_op jit(solution)/shard_map/ppermute | solution.py:603
  69.4 5.8 %collective-permute-start.15 = (bf16[2,144,256]{2,1,0:T(8,128)(2,1)S(1)}, bf16[2,144,256]{2,1,0:T(8,128)(2,1)S(1)}, u32[]{:S(2)}, u32[]{:S(2)}) collective-permute-start(bf16[2,144,256]{2,1,0:T(8,128)(2,1)S(1)} %get-tuple-element.81), channel_id=1, source_target_pairs={{0,16},{4,68},{8,24},{12,76},{16,0},{20,84},{24,8},{28,92},{32,48}... | collective-permute-start | bytes 442376 | tf_op jit(solution)/shard_map/ppermute | solution.py:603
  75.4 10.9 %collective-permute-start.17 = (bf16[2,144,256]{2,1,0:T(8,128)(2,1)S(1)}, bf16[2,144,256]{2,1,0:T(8,128)(2,1)S(1)}, u32[]{:S(2)}, u32[]{:S(2)}) collective-permute-start(bf16[2,144,256]{2,1,0:T(8,128)(2,1)S(1)} %get-tuple-element.140), channel_id=1, source_target_pairs={{0,96},{4,28},{8,104},{12,4},{16,112},{20,12},{24,120},{28,20},{32... | collective-permute-start | bytes 442376 | tf_op jit(solution)/shard_map/ppermute | solution.py:603
  76.3 10.0 %collective-permute-start.18 = (bf16[2,144,256]{2,1,0:T(8,128)(2,1)S(1)}, bf16[2,144,256]{2,1,0:T(8,128)(2,1)S(1)}, u32[]{:S(2)}, u32[]{:S(2)}) collective-permute-start(bf16[2,144,256]{2,1,0:T(8,128)(2,1)S(1)} %get-tuple-element.141), channel_id=1, source_target_pairs={{0,64},{4,20},{8,72},{12,28},{16,80},{20,4},{24,88},{28,12},{32,96... | collective-permute-start | bytes 442376 | tf_op jit(solution)/shard_map/ppermute | solution.py:603
  76.3 10.0 %collective-permute-start.16 = (bf16[2,144,256]{2,1,0:T(8,128)(2,1)S(1)}, bf16[2,144,256]{2,1,0:T(8,128)(2,1)S(1)}, u32[]{:S(2)}, u32[]{:S(2)}) collective-permute-start(bf16[2,144,256]{2,1,0:T(8,128)(2,1)S(1)} %get-tuple-element.117), channel_id=1, source_target_pairs={{0,32},{4,12},{8,40},{12,20},{16,48},{20,28},{24,56},{28,4},{32,64... | collective-permute-start | bytes 442376 | tf_op jit(solution)/shard_map/ppermute | solution.py:603
  81.0 80.0 %collective-permute-start.27 = (bf16[4096,768]{1,0:T(8,128)(2,1)S(1)}, bf16[4096,768]{1,0:T(8,128)(2,1)S(1)}, u32[]{:S(2)}, u32[]{:S(2)}) collective-permute-start(bf16[4096,768]{1,0:T(8,128)(2,1)S(1)} %collect.1.wm_ref), channel_id=1, source_target_pairs={{0,4},{4,0},{1,5},{5,1},{2,6},{6,2},{3,7},{7,3},{8,12},{12,8},{9,1... | collective-permute-start | bytes 18874376 | tf_op jit(solution)/shard_map/ppermute | solution.py:588
  89.0 5.4 %collective-permute-start.19 = (bf16[2,144,256]{2,1,0:T(8,128)(2,1)S(1)}, bf16[2,144,256]{2,1,0:T(8,128)(2,1)S(1)}, u32[]{:S(2)}, u32[]{:S(2)}) collective-permute-start(bf16[2,144,256]{2,1,0:T(8,128)(2,1)S(1)} %get-tuple-element.92), channel_id=1, source_target_pairs={{0,24},{4,100},{8,0},{12,108},{16,8},{20,116},{24,16},{28,124},{32... | collective-permute-start | bytes 442376 | tf_op jit(solution)/shard_map/ppermute | solution.py:603
  91.4 5.5 %collective-permute-start.20 = (bf16[2,144,256]{2,1,0:T(8,128)(2,1)S(1)}, bf16[2,144,256]{2,1,0:T(8,128)(2,1)S(1)}, u32[]{:S(2)}, u32[]{:S(2)}) collective-permute-start(bf16[2,144,256]{2,1,0:T(8,128)(2,1)S(1)} %get-tuple-element.92), channel_id=1, source_target_pairs={{0,8},{4,36},{8,16},{12,44},{16,24},{20,52},{24,0},{28,60},{32,40}... | collective-permute-start | bytes 442376 | tf_op jit(solution)/shard_map/ppermute | solution.py:603
  91.4 7.0 %collective-permute-start.21 = (bf16[2,144,256]{2,1,0:T(8,128)(2,1)S(1)}, bf16[2,144,256]{2,1,0:T(8,128)(2,1)S(1)}, u32[]{:S(2)}, u32[]{:S(2)}) collective-permute-start(bf16[2,144,256]{2,1,0:T(8,128)(2,1)S(1)} %get-tuple-element.92), channel_id=1, source_target_pairs={{0,16},{4,68},{8,24},{12,76},{16,0},{20,84},{24,8},{28,92},{32,48}... | collective-permute-start | bytes 442376 | tf_op jit(solution)/shard_map/ppermute | solution.py:603
  98.7 8.8 %collective-permute-start.23 = (bf16[2,144,256]{2,1,0:T(8,128)(2,1)S(1)}, bf16[2,144,256]{2,1,0:T(8,128)(2,1)S(1)}, u32[]{:S(2)}, u32[]{:S(2)}) collective-permute-start(bf16[2,144,256]{2,1,0:T(8,128)(2,1)S(1)} %get-tuple-element.138), channel_id=1, source_target_pairs={{0,32},{4,12},{8,40},{12,20},{16,48},{20,28},{24,56},{28,4},{32,64... | collective-permute-start | bytes 442376 | tf_op jit(solution)/shard_map/ppermute | solution.py:603
  98.8 8.7 %collective-permute-start.24 = (bf16[2,144,256]{2,1,0:T(8,128)(2,1)S(1)}, bf16[2,144,256]{2,1,0:T(8,128)(2,1)S(1)}, u32[]{:S(2)}, u32[]{:S(2)}) collective-permute-start(bf16[2,144,256]{2,1,0:T(8,128)(2,1)S(1)} %get-tuple-element.139), channel_id=1, source_target_pairs={{0,64},{4,20},{8,72},{12,28},{16,80},{20,4},{24,88},{28,12},{32,96... | collective-permute-start | bytes 442376 | tf_op jit(solution)/shard_map/ppermute | solution.py:603
  101.0 6.5 %collective-permute-start.22 = (bf16[2,144,256]{2,1,0:T(8,128)(2,1)S(1)}, bf16[2,144,256]{2,1,0:T(8,128)(2,1)S(1)}, u32[]{:S(2)}, u32[]{:S(2)}) collective-permute-start(bf16[2,144,256]{2,1,0:T(8,128)(2,1)S(1)} %get-tuple-element.114), channel_id=1, source_target_pairs={{0,96},{4,28},{8,104},{12,4},{16,112},{20,12},{24,120},{28,20},{32... | collective-permute-start | bytes 442376 | tf_op jit(solution)/shard_map/ppermute | solution.py:603
  111.7 12.4 %collective-permute-start.34 = (bf16[512,768]{1,0:T(8,128)(2,1)S(1)}, bf16[512,768]{1,0:T(8,128)(2,1)S(1)}, u32[]{:S(2)}, u32[]{:S(2)}) collective-permute-start(bf16[512,768]{1,0:T(8,128)(2,1)S(1)} %get-tuple-element.126), channel_id=1, source_target_pairs={{0,32},{4,12},{8,40},{12,20},{16,48},{20,28},{24,56},{28,4},{32,64... | collective-permute-start | bytes 2359304 | tf_op jit(solution)/shard_map/ppermute | solution.py:603
  112.9 11.6 %collective-permute-start.38 = (bf16[512,768]{1,0:T(8,128)(2,1)S(1)}, bf16[512,768]{1,0:T(8,128)(2,1)S(1)}, u32[]{:S(2)}, u32[]{:S(2)}) collective-permute-start(bf16[512,768]{1,0:T(8,128)(2,1)S(1)} %get-tuple-element.125), channel_id=1, source_target_pairs={{0,96},{4,28},{8,104},{12,4},{16,112},{20,12},{24,120},{28,20},{32... | collective-permute-start | bytes 2359304 | tf_op jit(solution)/shard_map/ppermute | solution.py:603
  118.9 13.7 %collective-permute-start.37 = (bf16[512,768]{1,0:T(8,128)(2,1)S(1)}, bf16[512,768]{1,0:T(8,128)(2,1)S(1)}, u32[]{:S(2)}, u32[]{:S(2)}) collective-permute-start(bf16[512,768]{1,0:T(8,128)(2,1)S(1)} %slice.251), channel_id=1, source_target_pairs={{0,32},{4,12},{8,40},{12,20},{16,48},{20,28},{24,56},{28,4},{32,64... | collective-permute-start | bytes 2359304 | tf_op jit(solution)/shard_map/ppermute | solution.py:603
  120.9 11.7 %collective-permute-start.36 = (bf16[512,768]{1,0:T(8,128)(2,1)S(1)}, bf16[512,768]{1,0:T(8,128)(2,1)S(1)}, u32[]{:S(2)}, u32[]{:S(2)}) collective-permute-start(bf16[512,768]{1,0:T(8,128)(2,1)S(1)} %slice.252), channel_id=1, source_target_pairs={{0,96},{4,28},{8,104},{12,4},{16,112},{20,12},{24,120},{28,20},{32... | collective-permute-start | bytes 2359304 | tf_op jit(solution)/shard_map/ppermute | solution.py:603
  124.4 16.6 %collective-permute-start.35 = (bf16[512,768]{1,0:T(8,128)(2,1)S(1)}, bf16[512,768]{1,0:T(8,128)(2,1)S(1)}, u32[]{:S(2)}, u32[]{:S(2)}) collective-permute-start(bf16[512,768]{1,0:T(8,128)(2,1)S(1)} %fusion.2), channel_id=1, source_target_pairs={{0,32},{4,12},{8,40},{12,20},{16,48},{20,28},{24,56},{28,4},{32,64... | collective-permute-start | bytes 2359304 | tf_op jit(solution)/shard_map/ppermute | solution.py:603
  124.6 16.4 %collective-permute-start.39 = (bf16[512,768]{1,0:T(8,128)(2,1)S(1)}, bf16[512,768]{1,0:T(8,128)(2,1)S(1)}, u32[]{:S(2)}, u32[]{:S(2)}) collective-permute-start(bf16[512,768]{1,0:T(8,128)(2,1)S(1)} %fusion), channel_id=1, source_target_pairs={{0,96},{4,28},{8,104},{12,4},{16,112},{20,12},{24,120},{28,20},{32... | collective-permute-start | bytes 2359304 | tf_op jit(solution)/shard_map/ppermute | solution.py:603
  141.5 5.8 %collective-permute-start.40 = (bf16[128,768]{1,0:T(8,128)(2,1)S(1)}, bf16[128,768]{1,0:T(8,128)(2,1)S(1)}, u32[]{:S(2)}, u32[]{:S(2)}) collective-permute-start(bf16[128,768]{1,0:T(8,128)(2,1)S(1)} %get-tuple-element.131), channel_id=1, source_target_pairs={{0,8},{4,36},{8,16},{12,44},{16,24},{20,52},{24,0},{28,60},{32,40}... | collective-permute-start | bytes 589832 | tf_op jit(solution)/shard_map/ppermute | solution.py:603
  141.6 6.8 %collective-permute-start.42 = (bf16[128,768]{1,0:T(8,128)(2,1)S(1)}, bf16[128,768]{1,0:T(8,128)(2,1)S(1)}, u32[]{:S(2)}, u32[]{:S(2)}) collective-permute-start(bf16[128,768]{1,0:T(8,128)(2,1)S(1)} %get-tuple-element.132), channel_id=1, source_target_pairs={{0,24},{4,100},{8,0},{12,108},{16,8},{20,116},{24,16},{28,124},{32... | collective-permute-start | bytes 589832 | tf_op jit(solution)/shard_map/ppermute | solution.py:603
  147.4 11.9 %collective-permute-start.41 = (bf16[256,768]{1,0:T(8,128)(2,1)S(1)}, bf16[256,768]{1,0:T(8,128)(2,1)S(1)}, u32[]{:S(2)}, u32[]{:S(2)}) collective-permute-start(bf16[256,768]{1,0:T(8,128)(2,1)S(1)} %pad_maximum_fusion.3), channel_id=1, source_target_pairs={{0,8},{4,36},{8,16},{12,44},{16,24},{20,52},{24,0},{28,60},{32,40}... | collective-permute-start | bytes 1179656 | tf_op jit(solution)/shard_map/ppermute | solution.py:603
  148.5 10.8 %collective-permute-start.43 = (bf16[256,768]{1,0:T(8,128)(2,1)S(1)}, bf16[256,768]{1,0:T(8,128)(2,1)S(1)}, u32[]{:S(2)}, u32[]{:S(2)}) collective-permute-start(bf16[256,768]{1,0:T(8,128)(2,1)S(1)} %pad_maximum_fusion.4), channel_id=1, source_target_pairs={{0,24},{4,100},{8,0},{12,108},{16,8},{20,116},{24,16},{28,124},{32... | collective-permute-start | bytes 1179656 | tf_op jit(solution)/shard_map/ppermute | solution.py:603
  151.7 9.3 %collective-permute-start.25 = (bf16[512,512]{1,0:T(8,128)(2,1)S(1)}, bf16[512,512]{1,0:T(8,128)(2,1)S(1)}, u32[]{:S(2)}, u32[]{:S(2)}) collective-permute-start(bf16[512,512]{1,0:T(8,128)(2,1)S(1)} %slice_select_fusion), channel_id=1, source_target_pairs={{0,4},{4,0},{1,5},{5,1},{2,6},{6,2},{3,7},{7,3},{8,12},{12,8},{9,1... | collective-permute-start | bytes 1572872 | tf_op jit(solution)/shard_map/ppermute | solution.py:588
  159.2 1.9 collective-permute-start.26
  163.9 11.2 %collective-permute-start.28 = (bf16[512,512]{1,0:T(8,128)(2,1)S(1)}, bf16[512,512]{1,0:T(8,128)(2,1)S(1)}, u32[]{:S(2)}, u32[]{:S(2)}) collective-permute-start(bf16[512,512]{1,0:T(8,128)(2,1)S(1)} %get-tuple-element.128), channel_id=1, source_target_pairs={{0,1},{1,2},{2,3},{3,0},{4,5},{5,6},{6,7},{7,4},{8,9},{9,10},{10,1... | collective-permute-start | bytes 1572872 | tf_op jit(solution)/shard_map/ppermute | solution.py:592
  165.1 10.0 %collective-permute-start.32 = (bf16[512,512]{1,0:T(8,128)(2,1)S(1)}, bf16[512,512]{1,0:T(8,128)(2,1)S(1)}, u32[]{:S(2)}, u32[]{:S(2)}) collective-permute-start(bf16[512,512]{1,0:T(8,128)(2,1)S(1)} %get-tuple-element.127), channel_id=1, source_target_pairs={{0,3},{1,0},{2,1},{3,2},{4,7},{5,4},{6,5},{7,6},{8,11},{9,8},{10,9... | collective-permute-start | bytes 1572872 | tf_op jit(solution)/shard_map/ppermute | solution.py:592
  171.5 20.6 %collective-permute-start.30 = (bf16[512,512]{1,0:T(8,128)(2,1)S(1)}, bf16[512,512]{1,0:T(8,128)(2,1)S(1)}, u32[]{:S(2)}, u32[]{:S(2)}) collective-permute-start(bf16[512,512]{1,0:T(8,128)(2,1)S(1)} %get-tuple-element.124), channel_id=1, source_target_pairs={{0,1},{1,2},{2,3},{3,0},{4,5},{5,6},{6,7},{7,4},{8,9},{9,10},{10,1... | collective-permute-start | bytes 1572872 | tf_op jit(solution)/shard_map/ppermute | solution.py:592
  171.6 20.5 %collective-permute-start.31 = (bf16[512,512]{1,0:T(8,128)(2,1)S(1)}, bf16[512,512]{1,0:T(8,128)(2,1)S(1)}, u32[]{:S(2)}, u32[]{:S(2)}) collective-permute-start(bf16[512,512]{1,0:T(8,128)(2,1)S(1)} %get-tuple-element.123), channel_id=1, source_target_pairs={{0,3},{1,0},{2,1},{3,2},{4,7},{5,4},{6,5},{7,6},{8,11},{9,8},{10,9... | collective-permute-start | bytes 1572872 | tf_op jit(solution)/shard_map/ppermute | solution.py:592
  175.4 22.6 %collective-permute-start.29 = (bf16[512,512]{1,0:T(8,128)(2,1)S(1)}, bf16[512,512]{1,0:T(8,128)(2,1)S(1)}, u32[]{:S(2)}, u32[]{:S(2)}) collective-permute-start(bf16[512,512]{1,0:T(8,128)(2,1)S(1)} %get-tuple-element.121), channel_id=1, source_target_pairs={{0,1},{1,2},{2,3},{3,0},{4,5},{5,6},{6,7},{7,4},{8,9},{9,10},{10,1... | collective-permute-start | bytes 1572872 | tf_op jit(solution)/shard_map/ppermute | solution.py:592
  176.4 21.6 %collective-permute-start.33 = (bf16[512,512]{1,0:T(8,128)(2,1)S(1)}, bf16[512,512]{1,0:T(8,128)(2,1)S(1)}, u32[]{:S(2)}, u32[]{:S(2)}) collective-permute-start(bf16[512,512]{1,0:T(8,128)(2,1)S(1)} %get-tuple-element.120), channel_id=1, source_target_pairs={{0,3},{1,0},{2,1},{3,2},{4,7},{5,4},{6,5},{7,6},{8,11},{9,8},{10,9... | collective-permute-start | bytes 1572872 | tf_op jit(solution)/shard_map/ppermute | solution.py:592
  178.2 10.4 %collective-permute-start.44 = (bf16[128,768]{1,0:T(8,128)(2,1)S(1)}, bf16[128,768]{1,0:T(8,128)(2,1)S(1)}, u32[]{:S(2)}, u32[]{:S(2)}) collective-permute-start(bf16[128,768]{1,0:T(8,128)(2,1)S(1)} %get-tuple-element.134), channel_id=1, source_target_pairs={{0,4},{4,0},{1,5},{5,1},{2,6},{6,2},{3,7},{7,3},{8,12},{12,8},{9,1... | collective-permute-start | bytes 589832 | tf_op jit(solution)/shard_map/ppermute | solution.py:588

commit v2 on v1

--- a/solution.py
+++ b/solution.py
@@ -25,6 +25,17 @@
 
 
 GRANT = 12
+
+
+VMEM = pl.BlockSpec(memory_space=pltpu.VMEM)
+SMEM = pl.BlockSpec(memory_space=pltpu.SMEM)
+
+
+def over_rows(count, size, body):
+    def step(i, _):
+        body(i, pl.ds(pl.multiple_of(i * size, size), size))
+
+    lax.fori_loop(0, count // size, step, None)
 
 
 def params(vmem=GRANT):
@@ -103,52 +114,56 @@
     )(idx, own, other)
 
 
-def halves_dot(x_ref, wa_ref, wb_ref):
+def halves_dot(x_ref, rows, wa_ref, wb_ref):
     half = wa_ref.shape[0]
-    return dot(x_ref[:, :half], wa_ref[...], NN) + dot(x_ref[:, half:], wb_ref[...], NN)
+    return dot(x_ref[rows, :half], wa_ref[...], NN) + dot(x_ref[rows, half:], wb_ref[...], NN)
 
 
 def first_body(x_ref, wa_ref, wb_ref, out_ref):
-    out_ref[...] = halves_dot(x_ref, wa_ref, wb_ref)
+    def block(_, rows):
+        out_ref[rows, :] = halves_dot(x_ref, rows, wa_ref, wb_ref)
+
+    over_rows(out_ref.shape[0], CHUNK, block)
 
 
 def more_body(acc_ref, xa_ref, xb_ref, *rest):
     *w_refs, out_ref = rest
-    total = acc_ref[...]
-    for x_ref, pair in ((xa_ref, w_refs[:2]), (xb_ref, w_refs[2:])):
-        total += halves_dot(x_ref, *pair)
-    out_ref[...] = total
+
+    def block(_, rows):
+        total = acc_ref[rows, :]
+        for x_ref, pair in ((xa_ref, w_refs[:2]), (xb_ref, w_refs[2:])):
+            total += halves_dot(x_ref, rows, *pair)
+        out_ref[rows, :] = total
+
+    over_rows(out_ref.shape[0], CHUNK, block)
 
 
 def top_body(acc_ref, x_ref, w_ref, out_ref):
-    out_ref[...] = acc_ref[...] + dot(x_ref[:, : w_ref.shape[0]], w_ref[...], NN)
+    def block(_, rows):
+        out_ref[rows, :] = acc_ref[rows, :] + dot(x_ref[rows, : w_ref.shape[0]], w_ref[...], NN)
+
+    over_rows(out_ref.shape[0], CHUNK, block)
 
 
 def end_body(acc_ref, x_ref, w_ref, out_ref):
-    out = acc_ref[...] + dot(x_ref[:, w_ref.shape[0] :], w_ref[...], NN)
-    out_ref[...] = out.astype(BF16)
+    def block(_, rows):
+        out = acc_ref[rows, :] + dot(x_ref[rows, w_ref.shape[0] :], w_ref[...], NN)
+        out_ref[rows, :] = out.astype(BF16)
+
+    over_rows(out_ref.shape[0], CHUNK, block)
 
 
 def project(body, acc, xs, ws, dtype):
     tok = xs[0].shape[0]
     columns = ws[0].shape[1]
-    size = 256
-
-    def tall(a):
-        return pl.BlockSpec((size, a.shape[1]), lambda i: (i, 0))
-
-    def whole(a):
-        return pl.BlockSpec(a.shape, lambda i: (0, 0))
-
     ops = acc + xs + ws
-    depth = sum(x.shape[1] for x in xs)
+    depth = sum(w.shape[0] for w in ws)
     return pl.pallas_call(
         body,
-        grid=(tok // size,),
-        in_specs=[tall(a) for a in acc + xs] + [whole(w) for w in ws],
-        out_specs=pl.BlockSpec((size, columns), lambda i: (i, 0)),
+        in_specs=[VMEM] * len(ops),
+        out_specs=VMEM,
         out_shape=jax.ShapeDtypeStruct((tok, columns), dtype),
-        compiler_params=params(16),
+        compiler_params=params(),
         cost_estimate=cost(2 * tok * depth * columns, 8 * MIB),
     )(*ops)
 
@@ -176,9 +191,6 @@
 
 
 PER_STEP = 2
-
-
-VMEM = pl.BlockSpec(memory_space=pltpu.VMEM)
 
 
 def over_chunks(n, body):
@@ -432,25 +444,26 @@
 
 
 def early_body(x_ref, d_ref, out_ref):
-    out_ref[...] = dot(x_ref[...], d_ref[...], NN)
+    def block(_, rows):
+        out_ref[rows, :] = dot(x_ref[rows, :], d_ref[...], NN)
+
+    over_rows(out_ref.shape[0], 512, block)
 
 
 def wgrad_body(x_ref, dkv_ref, early_ref, out_ref):
-    out_ref[:, :512] = dot(x_ref[...], dkv_ref[...], NN)
-    out_ref[:, 512:] = early_ref[...]
+    def block(_, rows):
+        out_ref[rows, :512] = dot(x_ref[rows, :], dkv_ref[...], NN)
+        out_ref[rows, 512:] = early_ref[rows, :]
+
+    over_rows(out_ref.shape[0], 512, block)
 
 
 def wgrad_call(body, x, d, early, columns):
     depth, tok = x.shape
-    size = 256
-    specs = [pl.BlockSpec((size, tok), lambda i: (i, 0)), pl.BlockSpec(d.shape, lambda i: (0, 0))]
-    specs += [pl.BlockSpec((size, a.shape[1]), lambda i: (i, 0)) for a in early]
-
     return pl.pallas_call(
         body,
-        grid=(depth // size,),
-        in_specs=specs,
-        out_specs=pl.BlockSpec((size, columns), lambda i: (i, 0)),
+        in_specs=[VMEM] * (2 + len(early)),
+        out_specs=VMEM,
         out_shape=jax.ShapeDtypeStruct((depth, columns), F32),
         compiler_params=params(),
         cost_estimate=cost(2 * tok * depth * columns, 6 * MIB),
@@ -520,76 +533,79 @@
 
 
 def back_body(place_ref, mkv_ref, mq_ref, tkv_ref, tq_ref, wm_ref, wt_ref, out_ref):
-    out_ref[...] = (
-        dot(wm_ref[:, :512], mkv_ref[...], NN)
-        + dot(wm_ref[:, 512:], mq_ref[...], NN)
-        + dot(wt_ref[:, :512], tkv_ref[...], NN)
-        + dot(wt_ref[:, 512:], tq_ref[...], NN)
-    )
+    def block(i, rows):
+        source = pl.ds(pl.multiple_of(place_ref[i] * 512, 512), 512)
+        out_ref[rows, :] = (
+            dot(wm_ref[source, :512], mkv_ref[...], NN)
+            + dot(wm_ref[source, 512:], mq_ref[...], NN)
+            + dot(wt_ref[source, :512], tkv_ref[...], NN)
+            + dot(wt_ref[source, 512:], tq_ref[...], NN)
+        )
+
+    over_rows(out_ref.shape[0], 512, block)
 
 
 def back(place, dkvt, dqt, theirs_kv, theirs_q, w_mine, w_theirs):
-    rows = theirs_kv.shape[1]
+    tok = dkvt.shape[1]
     depth = w_mine.shape[1]
-    width = 512
-    n = place.shape[0] - 1
-
-    def half_of(a):
-        return pl.BlockSpec((a.shape[0], rows), lambda k, p: (0, p[0]))
-
-    def whole(a):
-        return pl.BlockSpec(a.shape, lambda k, p: (0, 0))
-
-    weights = pl.BlockSpec((width, depth), lambda k, p: (p[1 + k], 0))
+    columns = 512 * place.shape[0]
     return pl.pallas_call(
         back_body,
-        out_shape=jax.ShapeDtypeStruct((n * width, rows), F32),
-        grid_spec=pltpu.PrefetchScalarGridSpec(
-            num_scalar_prefetch=1,
-            grid=(n,),
-            in_specs=[
-                half_of(dkvt), half_of(dqt), whole(theirs_kv), whole(theirs_q), weights, weights,
-            ],
-            out_specs=pl.BlockSpec((width, rows), lambda k, p: (k, 0)),
-        ),
-        compiler_params=params(),
-        cost_estimate=cost(4 * rows * n * width * depth, 8 * MIB),
+        in_specs=[SMEM] + [VMEM] * 6,
+        out_specs=VMEM,
+        out_shape=jax.ShapeDtypeStruct((columns, tok), F32),
+        compiler_params=params(),
+        cost_estimate=cost(4 * tok * columns * depth, 8 * MIB),
         name="back",
     )(place, dkvt, dqt, theirs_kv, theirs_q, w_mine, w_theirs)
 
 
-def turn_body(own_ref, at_ref, ab_ref, bt_ref, bb_ref, out_ref):
-    upper = pl.program_id(0) < pl.num_programs(0) // 2
-    after = jnp.where(upper, at_ref[...].astype(F32), ab_ref[...].astype(F32))
-    before = jnp.where(upper, bt_ref[...].astype(F32), bb_ref[...].astype(F32))
-    out_ref[...] = (own_ref[...] + after + before).astype(BF16).T
-
-
-def turn(own, after, before):
-    columns, rows = own.shape
-    size = 256
-    n = columns // size
-    part = pl.BlockSpec((size, rows), lambda i: (i, 0))
-    top = pl.BlockSpec((size, rows), lambda i: (jnp.minimum(i, n // 2 - 1), 0))
-    bottom = pl.BlockSpec((size, rows), lambda i: (jnp.maximum(i - n // 2, 0), 0))
+def turn_body(core_ref, own_ref, a_ref, b_ref, keep_ref, give_ref):
+    core = core_ref[0]
+    size = keep_ref.shape[0]
+    mine = pl.ds(pl.multiple_of(core * size, size), size)
+    theirs = pl.ds(pl.multiple_of((1 - core) * size, size), size)
+    for tokens, ref in ((theirs, give_ref), (mine, keep_ref)):
+        total = own_ref[:, tokens] + a_ref[:, tokens].astype(F32) + b_ref[:, tokens].astype(F32)
+        ref[...] = total.astype(BF16).T
+
+
+def turn(core, own, a, b):
+    columns, tok = own.shape
+    part = jax.ShapeDtypeStruct((tok // 2, columns), BF16)
     return pl.pallas_call(
         turn_body,
-        grid=(n,),
-        in_specs=[part, top, bottom, top, bottom],
-        out_specs=pl.BlockSpec((rows, size), lambda i: (0, i)),
-        out_shape=jax.ShapeDtypeStruct((rows, columns), BF16),
+        in_specs=[SMEM] + [VMEM] * 3,
+        out_specs=[VMEM] * 2,
+        out_shape=[part, part],
         compiler_params=params(),
         cost_estimate=cost(4 * MIB, 6 * MIB),
         name="turn",
-    )(own, *after, *before)
+    )(core, own, a, b)
+
+
+def join_body(core_ref, keep_ref, got_ref, out_ref):
+    core = core_ref[0]
+    size = keep_ref.shape[1]
+    out_ref[:, pl.ds(pl.multiple_of(core * size, size), size)] = keep_ref[...]
+    out_ref[:, pl.ds(pl.multiple_of((1 - core) * size, size), size)] = got_ref[...]
+
+
+def join(core, keep, got):
+    rows, columns = keep.shape
+    return pl.pallas_call(
+        join_body,
+        in_specs=[SMEM] + [VMEM] * 2,
+        out_specs=VMEM,
+        out_shape=jax.ShapeDtypeStruct((rows, 2 * columns), BF16),
+        compiler_params=params(),
+        cost_estimate=cost(MIB, 2 * MIB),
+        name="join",
+    )(core, keep, got)
 
 
 def swap(a):
     return lax.ppermute(a, "c", SWAP)
-
-
-def ring(a, axis, by):
-    return lax.ppermute(a, axis, [(i, (i + by) % 4) for i in range(4)])
 
 
 def along(a, by, inner):
@@ -601,6 +617,13 @@
                 to = (z, (y + by) % 4) if over_y else ((z + by) % 4, y)
                 pairs.append(((z * 4 + y) * 2 + c, (to[0] * 4 + to[1]) * 2 + c))
     return lax.ppermute(a, ("z", "y", "c"), pairs)
+
+
+def across(a, by):
+    pairs = [
+        (4 * c + x, 4 * c + (x + (by if c == 0 else -by)) % 4) for c in range(2) for x in range(4)
+    ]
+    return lax.ppermute(a, ("c", "x"), pairs)
 
 
 def gather_ring(a):
@@ -693,9 +716,10 @@
         along_inner[None, :] * 4 + along_outer[:, None],
     ).reshape(16)
 
+    way = 1 - 2 * core
+
     def place_of(*steps):
-        rows = [2 * lax.rem(x + by, 4) + i for by in steps for i in range(2)]
-        return jnp.stack([core] + rows)
+        return jnp.stack([2 * ((x + way * by) % 4) + core for by in steps])
 
     where = (
         core == 0,
@@ -703,7 +727,7 @@
         chip,
         core[None],
         place_of(2),
-        place_of(1, 3),
+        place_of(1, -1),
         place_of(0),
         scan_flags(inner, outer, 1),
         scan_flags(inner, outer, -1),
@@ -743,8 +767,8 @@
     dq, dqt, dkf, dv = middle_stage(kvq, kf, qf, s, gn, gd, seed, before, prefix)
     dkv, dkvt = last_stage(kvq, kf, dkf, dv, seed, suffix)
 
-    theirs_q = swap(half_of(first, dqt, 1)[1])
-    theirs_kv = swap(half_of(first, dkvt, 1)[1])
+    theirs_q = swap(dqt)
+    theirs_kv = swap(dkvt)
 
     def group(a):
         x_rows = arranged[a][1]
@@ -768,12 +792,13 @@
 
     total_w = scatter_small(strip_of).astype(BF16)
 
+    far = across(quarters(far_place).astype(BF16), 1)
     sides = quarters(side_place)
-    columns = sides.shape[0] // 2
-    after, before = scatter_ring(
-        quarters(far_place), sides[:columns], sides[columns:], lambda a, by: ring(a, "x", by)
-    )
-    input_grad = turn(quarters(own_place), after, before)
+    size = sides.shape[0] // 2
+    plain = across(sides[size:].astype(BF16), -1)
+    summed = across((sides[:size] + far.astype(F32)).astype(BF16), 1)
+    input_keep, input_give = turn(core, quarters(own_place), plain, summed)
+    input_grad = join(core, input_keep, swap(input_give))
 
     keep, give = half_of(first, total_w, 0)
     return input_grad, *finish(core, keep, swap(give))

time: 203 us -> 201 us (level); the launches traced: 200 us -> 201 us
  waiting for transfers between devices: 53.8 us -> 68.3 us
  starting transfers between devices: 77.2 us -> 69.4 us
  Pallas kernels: 62.6 us -> 56.8 us
    ppermute x32, waiting for transfers between devices: 39 us -> 49.1 us  [along(): return lax.ppermute(a, ('z', 'y', 'c'), pairs)]
    pallas_call x16 -> x17, Pallas kernels: 33.5 us -> 27.7 us  [the longest x4 9.38 us: project(): pl.pallas_call(body, in_specs=[VMEM] * len(ops), out_specs=VMEM, out_shap...]
    ppermute x6 -> x3, waiting for transfers between devices: 6.65 us -> 12.2 us  [across(): return lax.ppermute(a, ('c', 'x'), pairs)]
    ppermute x7 -> x8, starting transfers between devices: 26 us -> 22.1 us  [swap(): return lax.ppermute(a, 'c', SWAP)]
    ppermute x6 -> x3, starting transfers between devices: 8.23 us -> 5.37 us  [across(): return lax.ppermute(a, ('c', 'x'), pairs)]
    ppermute x7 -> x8, waiting for transfers between devices: 8.16 us -> 6.99 us  [swap(): return lax.ppermute(a, 'c', SWAP)]
  transfers between devices with their start and end apart: 45 -> 43, of which waited for: 19 -> 18; matrix products, arithmetic and copies ran while one was open for 2% -> 2% of each run, Pallas kernels for 29% -> 28%
where the time goes in v2:
time: 201 us
  starting transfers between devices  69.4 us (35%)
  waiting for transfers between devices  68.3 us (34%)
  Pallas kernels  56.8 us (28%)
  other arithmetic  4.01 us (2%)
    ppermute x32, waiting for transfers between devices, along(): return lax.ppermute(a, ('z', 'y', 'c'), pairs)  49.1 us
    ppermute x32, starting transfers between devices, along(): return lax.ppermute(a, ('z', 'y', 'c'), pairs)  41.9 us
    ppermute x8, starting transfers between devices, swap(): return lax.ppermute(a, 'c', SWAP)  22.1 us
    ppermute x3, waiting for transfers between devices, across(): return lax.ppermute(a, ('c', 'x'), pairs)  12.2 us
    pallas_call x4, Pallas kernels, project(): pl.pallas_call(body, in_specs=[VMEM] * len(ops), out_specs=VMEM, out_shap...  9.38 us
    pallas_call x8, Pallas kernels, wgrad_call(): pl.pallas_call(body, in_specs=[VMEM] * (2 + len(early)), out_specs=VMEM,...  9.18 us
    pallas_call x4, Pallas kernels, arrange(): pl.pallas_call(arrange_body, out_shape=[jax.ShapeDtypeStruct((2 * size, 4...  7.88 us
    pallas_call x3, Pallas kernels, back(): pl.pallas_call(back_body, in_specs=[SMEM] + [VMEM] * 6, out_specs=VMEM, o...  7.68 us
  transfers between devices with their start and end apart: 43, of which 18 were waited for; matrix products, arithmetic and copies ran while one was open for 2% of the time, Pallas kernels for 28%

profile of v2, /device:TPU:1, one launch (start us, length us, event | category | flops | bytes accessed | tf_op | source)
XLA Modules:
  0.0 200.6 jit_solution(606658139099294061)
XLA Ops:
  1.1 1.4 collective-permute-start
  2.5 1.8 halve.1
  4.3 5.5 %collective-permute-done.1 = bf16[128,768]{1,0:T(8,128)(2,1)S(1)} collective-permute-done((bf16[128,768]{1,0:T(8,128)(2,1)}, bf16[128,768]{1,0:T(8,128)(2,1)S(1)}, u32[]{:S(2)}, u32[]{:S(2)}) %collective-permute-start.1) | collective-permute-done | bytes 196640 | tf_op jit(solution)/shard_map/ppermute | solution.py:608
  10.8 1.8 collective-permute-start.3
  12.6 2.2 %collective-permute-start.2 = (bf16[256,768]{1,0:T(8,128)(2,1)S(1)}, bf16[256,768]{1,0:T(8,128)(2,1)S(1)}, u32[]{:S(2)}, u32[]{:S(2)}) collective-permute-start(bf16[256,768]{1,0:T(8,128)(2,1)S(1)} %pad_maximum_fusion.2), channel_id=1, source_target_pairs={{0,24},{4,100},{8,0},{12,108},{16,8},{20,116},{24,16},{28,124},{32... | collective-permute-start | bytes 1179656 | tf_op jit(solution)/shard_map/ppermute | solution.py:619
  14.8 5.1 %collective-permute-done.3 = bf16[256,768]{1,0:T(8,128)(2,1)S(1)} collective-permute-done((bf16[256,768]{1,0:T(8,128)(2,1)S(1)}, bf16[256,768]{1,0:T(8,128)(2,1)S(1)}, u32[]{:S(2)}, u32[]{:S(2)}) %collective-permute-start.3) | collective-permute-done | bytes 393248 | tf_op jit(solution)/shard_map/ppermute | solution.py:619
  20.0 3.0 %collective-permute-start.5 = (bf16[128,768]{1,0:T(8,128)(2,1)S(1)}, bf16[128,768]{1,0:T(8,128)(2,1)S(1)}, u32[]{:S(2)}, u32[]{:S(2)}) collective-permute-start(bf16[128,768]{1,0:T(8,128)(2,1)S(1)} %slice.124), channel_id=1, source_target_pairs={{0,24},{4,100},{8,0},{12,108},{16,8},{20,116},{24,16},{28,124},{32... | collective-permute-start | bytes 589832 | tf_op jit(solution)/shard_map/ppermute | solution.py:619
  23.1 1.1 collective-permute-start.8
  24.2 1.8 collective-permute-done.4
  26.1 3.0 %collective-permute-start.7 = (bf16[512,768]{1,0:T(8,128)(2,1)S(1)}, bf16[512,768]{1,0:T(8,128)(2,1)S(1)}, u32[]{:S(2)}, u32[]{:S(2)}) collective-permute-start(bf16[512,768]{1,0:T(8,128)(2,1)S(1)} %constant_dynamic-update-slice_fusion.wb_ref.refs_1_), channel_id=1, source_target_pairs={{0,96},{4,28},{8,104},{12,4},{16,112},{20,12},{24,120},{28,20},{32... | collective-permute-start | bytes 2359304 | tf_op jit(solution)/shard_map/ppermute | solution.py:619
  29.2 1.4 collective-permute-start.9
  30.5 5.0 %collective-permute-done.8.rest_2_.refs_6_ = bf16[512,768]{1,0:T(8,128)(2,1)S(1)} collective-permute-done((bf16[512,768]{1,0:T(8,128)(2,1)S(1)}, bf16[512,768]{1,0:T(8,128)(2,1)S(1)}, u32[]{:S(2)}, u32[]{:S(2)}) %collective-permute-start.8) | collective-permute-done | bytes 786464 | tf_op jit(solution)/shard_map/ppermute | solution.py:619
  35.6 2.4 %collective-permute-done.7.rest_1_.refs_3_ = bf16[512,768]{1,0:T(8,128)(2,1)S(1)} collective-permute-done((bf16[512,768]{1,0:T(8,128)(2,1)S(1)}, bf16[512,768]{1,0:T(8,128)(2,1)S(1)}, u32[]{:S(2)}, u32[]{:S(2)}) %collective-permute-start.7) | collective-permute-done | bytes 786464 | tf_op jit(solution)/shard_map/ppermute | solution.py:619
  38.0 3.4 %collective-permute-start.11 = (bf16[512,768]{1,0:T(8,128)(2,1)S(1)}, bf16[512,768]{1,0:T(8,128)(2,1)S(1)}, u32[]{:S(2)}, u32[]{:S(2)}) collective-permute-start(bf16[512,768]{1,0:T(8,128)(2,1)S(1)} %collective-permute-done.7.rest_1_.refs_3_), channel_id=1, source_target_pairs={{0,96},{4,28},{8,104},{12,4},{16,112},{20,12},{24,120},{28,20},{32... | collective-permute-start | bytes 2359304 | tf_op jit(solution)/shard_map/ppermute | solution.py:619
  41.4 5.0 %collective-permute-done.6.rest_0_.refs_2_ = bf16[512,768]{1,0:T(8,128)(2,1)S(1)} collective-permute-done((bf16[512,768]{1,0:T(8,128)(2,1)S(1)}, bf16[512,768]{1,0:T(8,128)(2,1)S(1)}, u32[]{:S(2)}, u32[]{:S(2)}) %collective-permute-start.6) | collective-permute-done | bytes 786464 | tf_op jit(solution)/shard_map/ppermute | solution.py:619
  46.4 6.0 %collective-permute-done.10.w_ref.refs_4_ = bf16[512,768]{1,0:T(8,128)(2,1)S(1)} collective-permute-done((bf16[512,768]{1,0:T(8,128)(2,1)S(1)}, bf16[512,768]{1,0:T(8,128)(2,1)S(1)}, u32[]{:S(2)}, u32[]{:S(2)}) %collective-permute-start.10) | collective-permute-done | bytes 786464 | tf_op jit(solution)/shard_map/ppermute | solution.py:619
  52.4 2.4 %collective-permute-done.11.w_ref.refs_5_ = bf16[512,768]{1,0:T(8,128)(2,1)S(1)} collective-permute-done((bf16[512,768]{1,0:T(8,128)(2,1)S(1)}, bf16[512,768]{1,0:T(8,128)(2,1)S(1)}, u32[]{:S(2)}, u32[]{:S(2)}) %collective-permute-start.11) | collective-permute-done | bytes 786464 | tf_op jit(solution)/shard_map/ppermute | solution.py:619
  54.9 4.0 %collect.1.wm_ref = bf16[4096,768]{1,0:T(8,128)(2,1)S(1)} custom-call(s32[16]{0:T(128)S(1)} %select_n.213.place_ref, bf16[512,768]{1,0:T(8,128)(2,1)S(1)} %pad_maximum_fusion.wa_ref.refs_0_, bf16[512,768]{1,0:T(8,128)(2,1)S(1)} %constant_dynamic-update-slice_fusion.wb_ref.refs_1_, bf16[512,768]{1,0:T(8,128)(2,1)S(1)} %collective-permute-done.6.rest_0_.refs_2_, ...), custom_call_target="tpu_custom_call" | custom-call | flops 1048576 | bytes 12582912 | tf_op jit(solution)/shard_map/collect/pallas_call | solution.py:519
  58.9 5.2 %collective-permute-start.27 = (bf16[4096,768]{1,0:T(8,128)(2,1)S(1)}, bf16[4096,768]{1,0:T(8,128)(2,1)S(1)}, u32[]{:S(2)}, u32[]{:S(2)}) collective-permute-start(bf16[4096,768]{1,0:T(8,128)(2,1)S(1)} %collect.1.wm_ref), channel_id=1, source_target_pairs={{0,4},{4,0},{1,5},{5,1},{2,6},{6,2},{3,7},{7,3},{8,12},{12,8},{9,1... | collective-permute-start | bytes 18874376 | tf_op jit(solution)/shard_map/ppermute | solution.py:608
  64.3 2.0 arrange.4
  66.2 2.3 %shard_map.93.acc_ref = f32[1024,768]{1,0:T(8,128)S(1)} custom-call(bf16[1024,1024]{1,0:T(8,128)(2,1)S(1)} %get-tuple-element.64.x_ref, bf16[512,768]{1,0:T(8,128)(2,1)S(1)} %pad_maximum_fusion.wa_ref.refs_0_, bf16[512,768]{1,0:T(8,128)(2,1)S(1)} %constant_dynamic-update-slice_fusion.wb_ref.refs_1_), custom_call_target="tpu_custom_call" | custom-call | flops 1610612736 | bytes 8388608 | tf_op jit(solution)/shard_map/pallas_call | solution.py:161
  68.6 2.0 arrange.5
  70.6 2.0 arrange.6
  72.5 2.0 arrange.7
  74.5 4.0 %shard_map.94.acc_ref = f32[1024,768]{1,0:T(8,128)S(1)} custom-call(f32[1024,768]{1,0:T(8,128)S(1)} %shard_map.93.acc_ref, bf16[1024,1024]{1,0:T(8,128)(2,1)S(1)} %get-tuple-element.71.xa_ref, bf16[1024,1024]{1,0:T(8,128)(2,1)S(1)} %get-tuple-element.72.xb_ref, bf16[512,768]{1,0:T(8,128)(2,1)S(1)} %collective-permute-done.6.rest_0_.refs_2_, ...), custom_call_target="tpu_custom_call" | custom-call | flops 3221225472 | bytes 8388608 | tf_op jit(solution)/shard_map/pallas_call | solution.py:161
  78.6 1.5 shard_map.95.acc_ref
  80.1 1.5 shard_map.96.kvq_ref.q_ref.v_ref
  81.6 2.2 %keys_stage.1 = (bf16[1024,512]{1,0:T(8,128)(2,1)S(1)}, f32[4,2,144,256]{3,2,1,0:T(8,128)S(1)}, bf16[2,144,256]{2,1,0:T(8,128)(2,1)S(1)}) custom-call(bf16[1024,768]{1,0:T(8,128)(2,1)S(1)} %shard_map.96.kvq_ref.q_ref.v_ref, bf16[2,128,256]{2,1,0:T(8,128)(2,1)S(1)} %select_convert_fusion.2.seed_ref), custom_call_target="tpu_custom_call" | custom-call | flops 268435456 | bytes 4194304 | tf_op jit(solution)/shard_map/keys_stage/pallas_call | solution.py:228
  83.9 3.4 %collective-permute-start.14 = (bf16[2,144,256]{2,1,0:T(8,128)(2,1)S(1)}, bf16[2,144,256]{2,1,0:T(8,128)(2,1)S(1)}, u32[]{:S(2)}, u32[]{:S(2)}) collective-permute-start(bf16[2,144,256]{2,1,0:T(8,128)(2,1)S(1)} %get-tuple-element.83), channel_id=1, source_target_pairs={{0,24},{4,100},{8,0},{12,108},{16,8},{20,116},{24,16},{28,124},{32... | collective-permute-start | bytes 442376 | tf_op jit(solution)/shard_map/ppermute | solution.py:619
  87.3 1.1 collective-permute-start.15
  88.5 1.6 collective-permute-done.13
  90.1 3.0 %collective-permute-done.15 = bf16[2,144,256]{2,1,0:T(8,128)(2,1)S(1)} collective-permute-done((bf16[2,144,256]{2,1,0:T(8,128)(2,1)S(1)}, bf16[2,144,256]{2,1,0:T(8,128)(2,1)S(1)}, u32[]{:S(2)}, u32[]{:S(2)}) %collective-permute-start.15) | collective-permute-done | bytes 147488 | tf_op jit(solution)/shard_map/ppermute | solution.py:619
  94.9 3.0 %local_stage.1 = (bf16[1024,512]{1,0:T(8,128)(2,1)S(1)}, bf16[1024,512]{1,0:T(8,128)(2,1)S(1)}, f32[1024,256]{1,0:T(8,128)S(1)}, f32[2,1024,1]{2,1,0:T(8,128)S(1)}) custom-call(bf16[1024,768]{1,0:T(8,128)(2,1)S(1)} %shard_map.96.kvq_ref.q_ref.v_ref, bf16[1024,768]{1,0:T(8,128)(2,1)S(1)} %shard_map.96.kvq_ref.q_ref.v_ref, ...), custom_call_target="tpu_custom_call" | custom-call | flops 671088640 | bytes 6291456 | tf_op jit(solution)/shard_map/local_stage/pallas_call | solution.py:265
  98.0 1.7 collective-permute-done.18
  99.6 1.5 collective-permute-done.16
  101.3 2.5 %ratio_stage.1 = (bf16[1024,256]{1,0:T(8,128)(2,1)S(1)}, f32[2,1024,1]{2,1,0:T(8,128)S(1)}, bf16[2,144,256]{2,1,0:T(8,128)(2,1)S(1)}) custom-call(bf16[1024,512]{1,0:T(8,128)(2,1)S(1)} %get-tuple-element.77.qf_ref, f32[1024,256]{1,0:T(8,128)S(1)} %get-tuple-element.79.num_ref, f32[2,1024,1]{2,1,0:T(8,128)S(1)} %get-tuple-element.80.den_ref, ...), custom_call_target="tpu_custom_call" | custom-call | flops 268435456 | bytes 4194304 | tf_op jit(solution)/shard_map/ratio_stage/pallas_call | solution.py:322
  103.8 1.8 collective-permute-start.19
  105.5 1.3 collective-permute-start.21
  107.8 4.5 %collective-permute-done.20 = bf16[2,144,256]{2,1,0:T(8,128)(2,1)S(1)} collective-permute-done((bf16[2,144,256]{2,1,0:T(8,128)(2,1)S(1)}, bf16[2,144,256]{2,1,0:T(8,128)(2,1)S(1)}, u32[]{:S(2)}, u32[]{:S(2)}) %collective-permute-start.20) | collective-permute-done | bytes 147488 | tf_op jit(solution)/shard_map/ppermute | solution.py:619
  112.6 1.8 collective-permute-start.24
  115.3 4.8 %middle_stage.1 = (bf16[1024,256]{1,0:T(8,128)(2,1)S(1)}, bf16[256,1024]{1,0:T(8,128)(2,1)S(1)}, f32[1024,512]{1,0:T(8,128)S(1)}, f32[1024,256]{1,0:T(8,128)S(1)}) custom-call(bf16[1024,768]{1,0:T(8,128)(2,1)S(1)} %shard_map.96.kvq_ref.q_ref.v_ref, bf16[1024,768]{1,0:T(8,128)(2,1)S(1)} %shard_map.96.kvq_ref.q_ref.v_ref, ...), custom_call_target="tpu_custom_call" | custom-call | flops 1342177280 | bytes 10485760 | tf_op jit(solution)/shard_map/middle_stage/pallas_call | solution.py:379
  121.2 2.0 last_stage.1
  123.1 1.4 shard_map.102
  125.5 2.1 %collective-permute-start.36 = (bf16[512,768]{1,0:T(8,128)(2,1)S(1)}, bf16[512,768]{1,0:T(8,128)(2,1)S(1)}, u32[]{:S(2)}, u32[]{:S(2)}) collective-permute-start(bf16[512,768]{1,0:T(8,128)(2,1)S(1)} %get-tuple-element.125), channel_id=1, source_target_pairs={{0,96},{4,28},{8,104},{12,4},{16,112},{20,12},{24,120},{28,20},{32... | collective-permute-start | bytes 2359304 | tf_op jit(solution)/shard_map/ppermute | solution.py:619
  127.6 8.1 %collective-permute-start.25 = (bf16[512,1024]{1,0:T(8,128)(2,1)S(1)}, bf16[512,1024]{1,0:T(8,128)(2,1)S(1)}, u32[]{:S(2)}, u32[]{:S(2)}) collective-permute-start(bf16[512,1024]{1,0:T(8,128)(2,1)S(1)} %get-tuple-element.100.mkv_ref), channel_id=1, source_target_pairs={{0,4},{4,0},{1,5},{5,1},{2,6},{6,2},{3,7},{7,3},{8,12},{12,8},{9,1... | collective-permute-start | bytes 3145736 | tf_op jit(solution)/shard_map/ppermute | solution.py:608
  137.5 1.4 shard_map.100
  139.0 1.4 shard_map.104
  140.8 2.7 %collective-permute-start.34 = (bf16[512,768]{1,0:T(8,128)(2,1)S(1)}, bf16[512,768]{1,0:T(8,128)(2,1)S(1)}, u32[]{:S(2)}, u32[]{:S(2)}) collective-permute-start(bf16[512,768]{1,0:T(8,128)(2,1)S(1)} %slice.204), channel_id=1, source_target_pairs={{0,96},{4,28},{8,104},{12,4},{16,112},{20,12},{24,120},{28,20},{32... | collective-permute-start | bytes 2359304 | tf_op jit(solution)/shard_map/ppermute | solution.py:619
  143.8 2.7 %collective-permute-start.37 = (bf16[512,768]{1,0:T(8,128)(2,1)S(1)}, bf16[512,768]{1,0:T(8,128)(2,1)S(1)}, u32[]{:S(2)}, u32[]{:S(2)}) collective-permute-start(bf16[512,768]{1,0:T(8,128)(2,1)S(1)} %fusion.1), channel_id=1, source_target_pairs={{0,96},{4,28},{8,104},{12,4},{16,112},{20,12},{24,120},{28,20},{32... | collective-permute-start | bytes 2359304 | tf_op jit(solution)/shard_map/ppermute | solution.py:619
  147.4 1.8 back.5
  149.3 2.6 %collective-permute-start.29 = (bf16[512,1024]{1,0:T(8,128)(2,1)S(1)}, bf16[512,1024]{1,0:T(8,128)(2,1)S(1)}, u32[]{:S(2)}, u32[]{:S(2)}) collective-permute-start(bf16[512,1024]{1,0:T(8,128)(2,1)S(1)} %convert_element_type.133), channel_id=1, source_target_pairs={{0,1},{1,2},{2,3},{3,0},{4,7},{5,4},{6,5},{7,6},{8,9},{9,10},{10,1... | collective-permute-start | bytes 3145736 | tf_op jit(solution)/shard_map/ppermute | solution.py:626
  151.9 1.4 shard_map.98
  153.3 8.0 %collective-permute-done.33 = bf16[512,768]{1,0:T(8,128)(2,1)S(1)} collective-permute-done((bf16[512,768]{1,0:T(8,128)(2,1)S(1)}, bf16[512,768]{1,0:T(8,128)(2,1)S(1)}, u32[]{:S(2)}, u32[]{:S(2)}) %collective-permute-start.33) | collective-permute-done | bytes 786464 | tf_op jit(solution)/shard_map/ppermute | solution.py:619
  161.9 2.7 %collective-permute-start.40 = (bf16[128,768]{1,0:T(8,128)(2,1)S(1)}, bf16[128,768]{1,0:T(8,128)(2,1)S(1)}, u32[]{:S(2)}, u32[]{:S(2)}) collective-permute-start(bf16[128,768]{1,0:T(8,128)(2,1)S(1)} %get-tuple-element.130), channel_id=1, source_target_pairs={{0,24},{4,100},{8,0},{12,108},{16,8},{20,116},{24,16},{28,124},{32... | collective-permute-start | bytes 589832 | tf_op jit(solution)/shard_map/ppermute | solution.py:619
  164.6 4.1 %back.4 = f32[1024,1024]{1,0:T(8,128)S(1)} custom-call(s32[2]{0:T(128)S(1)} %pad_add_fusion.1.place_ref, bf16[512,1024]{1,0:T(8,128)(2,1)S(1)} %get-tuple-element.100.mkv_ref, bf16[256,1024]{1,0:T(8,128)(2,1)S(1)} %get-tuple-element.101.mq_ref, bf16[512,1024]{1,0:T(8,128)(2,1)S(1)} %collective-permute-done.25.tkv_ref, ...), custom_call_target="tpu_custom_call" | custom-call | flops 3221225472 | bytes 8388608 | tf_op jit(solution)/shard_map/back/pallas_call | solution.py:552
  168.9 1.3 collective-permute-start.28
  170.6 1.5 collective-permute-start.30
  172.4 2.7 %collective-permute-start.41 = (bf16[256,768]{1,0:T(8,128)(2,1)S(1)}, bf16[256,768]{1,0:T(8,128)(2,1)S(1)}, u32[]{:S(2)}, u32[]{:S(2)}) collective-permute-start(bf16[256,768]{1,0:T(8,128)(2,1)S(1)} %pad_maximum_fusion.4), channel_id=1, source_target_pairs={{0,24},{4,100},{8,0},{12,108},{16,8},{20,116},{24,16},{28,124},{32... | collective-permute-start | bytes 1179656 | tf_op jit(solution)/shard_map/ppermute | solution.py:619
  175.1 1.8 back.3.own_ref
  176.9 7.0 %collective-permute-done.28.a_ref = bf16[512,1024]{1,0:T(8,128)(2,1)S(1)} collective-permute-done((bf16[512,1024]{1,0:T(8,128)(2,1)S(1)}, bf16[512,1024]{1,0:T(8,128)(2,1)S(1)}, u32[]{:S(2)}, u32[]{:S(2)}) %collective-permute-start.28) | collective-permute-done | bytes 1048608 | tf_op jit(solution)/shard_map/ppermute | solution.py:626
  183.9 5.3 %collective-permute-done.30.b_ref = bf16[512,1024]{1,0:T(8,128)(2,1)S(1)} collective-permute-done((bf16[512,1024]{1,0:T(8,128)(2,1)S(1)}, bf16[512,1024]{1,0:T(8,128)(2,1)S(1)}, u32[]{:S(2)}, u32[]{:S(2)}) %collective-permute-start.30) | collective-permute-done | bytes 1048608 | tf_op jit(solution)/shard_map/ppermute | solution.py:626
  189.6 7.2 %collective-permute-start.31 = (bf16[512,512]{1,0:T(8,128)(2,1)S(1)}, bf16[512,512]{1,0:T(8,128)(2,1)S(1)}, u32[]{:S(2)}, u32[]{:S(2)}) collective-permute-start(bf16[512,512]{1,0:T(8,128)(2,1)S(1)} %get-tuple-element.106), channel_id=1, source_target_pairs={{0,4},{4,0},{1,5},{5,1},{2,6},{6,2},{3,7},{7,3},{8,12},{12,8},{9,1... | collective-permute-start | bytes 1572872 | tf_op jit(solution)/shard_map/ppermute | solution.py:608
  197.1 1.5 collective-permute-done.42.got_ref
  199.5 1.1 join.1
  (98 shorter events, 14.6 us)
Async XLA Ops:
  1.1 63.1 %collective-permute-start = (bf16[512,4096]{1,0:T(8,128)(2,1)}, bf16[512,4096]{1,0:T(8,128)(2,1)S(1)}, u32[]{:S(2)}, u32[]{:S(2)}) collective-permute-start(bf16[512,4096]{1,0:T(8,128)(2,1)} %own_ref.3), channel_id=1, source_target_pairs={{0,4},{4,0},{1,5},{5,1},{2,6},{6,2},{3,7},{7,3},{8,12},{12,8},{9,1... | collective-permute-start | bytes 12582920 | tf_op jit(solution)/shard_map/ppermute | solution.py:608
  4.3 5.5 %collective-permute-start.1 = (bf16[128,768]{1,0:T(8,128)(2,1)}, bf16[128,768]{1,0:T(8,128)(2,1)S(1)}, u32[]{:S(2)}, u32[]{:S(2)}) collective-permute-start(bf16[128,768]{1,0:T(8,128)(2,1)} %get-tuple-element.70), channel_id=1, source_target_pairs={{0,4},{4,0},{1,5},{5,1},{2,6},{6,2},{3,7},{7,3},{8,12},{12,8},{9,1... | collective-permute-start | bytes 589832 | tf_op jit(solution)/shard_map/ppermute | solution.py:608
  10.8 9.1 %collective-permute-start.3 = (bf16[256,768]{1,0:T(8,128)(2,1)S(1)}, bf16[256,768]{1,0:T(8,128)(2,1)S(1)}, u32[]{:S(2)}, u32[]{:S(2)}) collective-permute-start(bf16[256,768]{1,0:T(8,128)(2,1)S(1)} %pad_maximum_fusion.2), channel_id=1, source_target_pairs={{0,8},{4,36},{8,16},{12,44},{16,24},{20,52},{24,0},{28,60},{32,40}... | collective-permute-start | bytes 1179656 | tf_op jit(solution)/shard_map/ppermute | solution.py:619
  12.6 7.4 %collective-permute-start.2 = (bf16[256,768]{1,0:T(8,128)(2,1)S(1)}, bf16[256,768]{1,0:T(8,128)(2,1)S(1)}, u32[]{:S(2)}, u32[]{:S(2)}) collective-permute-start(bf16[256,768]{1,0:T(8,128)(2,1)S(1)} %pad_maximum_fusion.2), channel_id=1, source_target_pairs={{0,24},{4,100},{8,0},{12,108},{16,8},{20,116},{24,16},{28,124},{32... | collective-permute-start | bytes 1179656 | tf_op jit(solution)/shard_map/ppermute | solution.py:619
  19.9 6.1 %collective-permute-start.4 = (bf16[128,768]{1,0:T(8,128)(2,1)S(1)}, bf16[128,768]{1,0:T(8,128)(2,1)S(1)}, u32[]{:S(2)}, u32[]{:S(2)}) collective-permute-start(bf16[128,768]{1,0:T(8,128)(2,1)S(1)} %slice.123), channel_id=1, source_target_pairs={{0,8},{4,36},{8,16},{12,44},{16,24},{20,52},{24,0},{28,60},{32,40}... | collective-permute-start | bytes 589832 | tf_op jit(solution)/shard_map/ppermute | solution.py:619
  20.0 6.0 %collective-permute-start.5 = (bf16[128,768]{1,0:T(8,128)(2,1)S(1)}, bf16[128,768]{1,0:T(8,128)(2,1)S(1)}, u32[]{:S(2)}, u32[]{:S(2)}) collective-permute-start(bf16[128,768]{1,0:T(8,128)(2,1)S(1)} %slice.124), channel_id=1, source_target_pairs={{0,24},{4,100},{8,0},{12,108},{16,8},{20,116},{24,16},{28,124},{32... | collective-permute-start | bytes 589832 | tf_op jit(solution)/shard_map/ppermute | solution.py:619
  23.1 12.5 %collective-permute-start.8 = (bf16[512,768]{1,0:T(8,128)(2,1)S(1)}, bf16[512,768]{1,0:T(8,128)(2,1)S(1)}, u32[]{:S(2)}, u32[]{:S(2)}) collective-permute-start(bf16[512,768]{1,0:T(8,128)(2,1)S(1)} %pad_maximum_fusion.wa_ref.refs_0_), channel_id=1, source_target_pairs={{0,32},{4,12},{8,40},{12,20},{16,48},{20,28},{24,56},{28,4},{32,64... | collective-permute-start | bytes 2359304 | tf_op jit(solution)/shard_map/ppermute | solution.py:619
  26.1 38.0 %copy-start.2 = (bf16[512,512]{1,0:T(8,128)(2,1)S(1)}, bf16[512,512]{1,0:T(8,128)(2,1)}, u32[]{:S(2)}) copy-start(bf16[512,512]{1,0:T(8,128)(2,1)} %param.11) | copy-start | bytes 1572868
  26.1 38.1 %copy-start.1 = (s32[4,128,256]{2,1,0:T(8,128)S(1)}, s32[4,128,256]{2,1,0:T(8,128)}, u32[]{:S(2)}) copy-start(s32[4,128,256]{2,1,0:T(8,128)} %param.10) | copy-start | bytes 1572868
  26.1 11.9 %collective-permute-start.7 = (bf16[512,768]{1,0:T(8,128)(2,1)S(1)}, bf16[512,768]{1,0:T(8,128)(2,1)S(1)}, u32[]{:S(2)}, u32[]{:S(2)}) collective-permute-start(bf16[512,768]{1,0:T(8,128)(2,1)S(1)} %constant_dynamic-update-slice_fusion.wb_ref.refs_1_), channel_id=1, source_target_pairs={{0,96},{4,28},{8,104},{12,4},{16,112},{20,12},{24,120},{28,20},{32... | collective-permute-start | bytes 2359304 | tf_op jit(solution)/shard_map/ppermute | solution.py:619
  29.1 17.4 %collective-permute-start.6 = (bf16[512,768]{1,0:T(8,128)(2,1)S(1)}, bf16[512,768]{1,0:T(8,128)(2,1)S(1)}, u32[]{:S(2)}, u32[]{:S(2)}) collective-permute-start(bf16[512,768]{1,0:T(8,128)(2,1)S(1)} %pad_maximum_fusion.wa_ref.refs_0_), channel_id=1, source_target_pairs={{0,96},{4,28},{8,104},{12,4},{16,112},{20,12},{24,120},{28,20},{32... | collective-permute-start | bytes 2359304 | tf_op jit(solution)/shard_map/ppermute | solution.py:619
  29.2 17.3 %collective-permute-start.9 = (bf16[512,768]{1,0:T(8,128)(2,1)S(1)}, bf16[512,768]{1,0:T(8,128)(2,1)S(1)}, u32[]{:S(2)}, u32[]{:S(2)}) collective-permute-start(bf16[512,768]{1,0:T(8,128)(2,1)S(1)} %constant_dynamic-update-slice_fusion.wb_ref.refs_1_), channel_id=1, source_target_pairs={{0,32},{4,12},{8,40},{12,20},{16,48},{20,28},{24,56},{28,4},{32,64... | collective-permute-start | bytes 2359304 | tf_op jit(solution)/shard_map/ppermute | solution.py:619
  35.6 16.9 %collective-permute-start.10 = (bf16[512,768]{1,0:T(8,128)(2,1)S(1)}, bf16[512,768]{1,0:T(8,128)(2,1)S(1)}, u32[]{:S(2)}, u32[]{:S(2)}) collective-permute-start(bf16[512,768]{1,0:T(8,128)(2,1)S(1)} %collective-permute-done.8.rest_2_.refs_6_), channel_id=1, source_target_pairs={{0,32},{4,12},{8,40},{12,20},{16,48},{20,28},{24,56},{28,4},{32,64... | collective-permute-start | bytes 2359304 | tf_op jit(solution)/shard_map/ppermute | solution.py:619
  38.0 16.9 %collective-permute-start.11 = (bf16[512,768]{1,0:T(8,128)(2,1)S(1)}, bf16[512,768]{1,0:T(8,128)(2,1)S(1)}, u32[]{:S(2)}, u32[]{:S(2)}) collective-permute-start(bf16[512,768]{1,0:T(8,128)(2,1)S(1)} %collective-permute-done.7.rest_1_.refs_3_), channel_id=1, source_target_pairs={{0,96},{4,28},{8,104},{12,4},{16,112},{20,12},{24,120},{28,20},{32... | collective-permute-start | bytes 2359304 | tf_op jit(solution)/shard_map/ppermute | solution.py:619
  54.9 9.4 %copy-start = (bf16[512,4096]{1,0:T(8,128)(2,1)S(1)}, bf16[512,4096]{1,0:T(8,128)(2,1)}, u32[]{:S(2)}) copy-start(bf16[512,4096]{1,0:T(8,128)(2,1)} %own_ref.3) | copy-start | bytes 12582916
  58.9 88.5 %collective-permute-start.27 = (bf16[4096,768]{1,0:T(8,128)(2,1)S(1)}, bf16[4096,768]{1,0:T(8,128)(2,1)S(1)}, u32[]{:S(2)}, u32[]{:S(2)}) collective-permute-start(bf16[4096,768]{1,0:T(8,128)(2,1)S(1)} %collect.1.wm_ref), channel_id=1, source_target_pairs={{0,4},{4,0},{1,5},{5,1},{2,6},{6,2},{3,7},{7,3},{8,12},{12,8},{9,1... | collective-permute-start | bytes 18874376 | tf_op jit(solution)/shard_map/ppermute | solution.py:608
  64.1 24.4 %collective-permute-start.12 = (bf16[512,512]{1,0:T(8,128)(2,1)S(1)}, bf16[512,512]{1,0:T(8,128)(2,1)S(1)}, u32[]{:S(2)}, u32[]{:S(2)}) collective-permute-start(bf16[512,512]{1,0:T(8,128)(2,1)S(1)} %copy-done.2), channel_id=1, source_target_pairs={{0,4},{4,0},{1,5},{5,1},{2,6},{6,2},{3,7},{7,3},{8,12},{12,8},{9,1... | collective-permute-start | bytes 1572872 | tf_op jit(solution)/shard_map/ppermute | solution.py:608
  83.8 6.3 %collective-permute-start.13 = (bf16[2,144,256]{2,1,0:T(8,128)(2,1)S(1)}, bf16[2,144,256]{2,1,0:T(8,128)(2,1)S(1)}, u32[]{:S(2)}, u32[]{:S(2)}) collective-permute-start(bf16[2,144,256]{2,1,0:T(8,128)(2,1)S(1)} %get-tuple-element.83), channel_id=1, source_target_pairs={{0,8},{4,36},{8,16},{12,44},{16,24},{20,52},{24,0},{28,60},{32,40}... | collective-permute-start | bytes 442376 | tf_op jit(solution)/shard_map/ppermute | solution.py:619
  83.9 6.2 %collective-permute-start.14 = (bf16[2,144,256]{2,1,0:T(8,128)(2,1)S(1)}, bf16[2,144,256]{2,1,0:T(8,128)(2,1)S(1)}, u32[]{:S(2)}, u32[]{:S(2)}) collective-permute-start(bf16[2,144,256]{2,1,0:T(8,128)(2,1)S(1)} %get-tuple-element.83), channel_id=1, source_target_pairs={{0,24},{4,100},{8,0},{12,108},{16,8},{20,116},{24,16},{28,124},{32... | collective-permute-start | bytes 442376 | tf_op jit(solution)/shard_map/ppermute | solution.py:619
  87.3 5.8 %collective-permute-start.15 = (bf16[2,144,256]{2,1,0:T(8,128)(2,1)S(1)}, bf16[2,144,256]{2,1,0:T(8,128)(2,1)S(1)}, u32[]{:S(2)}, u32[]{:S(2)}) collective-permute-start(bf16[2,144,256]{2,1,0:T(8,128)(2,1)S(1)} %get-tuple-element.83), channel_id=1, source_target_pairs={{0,16},{4,68},{8,24},{12,76},{16,0},{20,84},{24,8},{28,92},{32,48}... | collective-permute-start | bytes 442376 | tf_op jit(solution)/shard_map/ppermute | solution.py:619
  93.4 4.6 %collective-permute-start.17 = (bf16[2,144,256]{2,1,0:T(8,128)(2,1)S(1)}, bf16[2,144,256]{2,1,0:T(8,128)(2,1)S(1)}, u32[]{:S(2)}, u32[]{:S(2)}) collective-permute-start(bf16[2,144,256]{2,1,0:T(8,128)(2,1)S(1)} %get-tuple-element.138), channel_id=1, source_target_pairs={{0,96},{4,28},{8,104},{12,4},{16,112},{20,12},{24,120},{28,20},{32... | collective-permute-start | bytes 442376 | tf_op jit(solution)/shard_map/ppermute | solution.py:619
  94.0 5.6 %collective-permute-start.18 = (bf16[2,144,256]{2,1,0:T(8,128)(2,1)S(1)}, bf16[2,144,256]{2,1,0:T(8,128)(2,1)S(1)}, u32[]{:S(2)}, u32[]{:S(2)}) collective-permute-start(bf16[2,144,256]{2,1,0:T(8,128)(2,1)S(1)} %get-tuple-element.139), channel_id=1, source_target_pairs={{0,64},{4,20},{8,72},{12,28},{16,80},{20,4},{24,88},{28,12},{32,96... | collective-permute-start | bytes 442376 | tf_op jit(solution)/shard_map/ppermute | solution.py:619
  94.0 7.1 %collective-permute-start.16 = (bf16[2,144,256]{2,1,0:T(8,128)(2,1)S(1)}, bf16[2,144,256]{2,1,0:T(8,128)(2,1)S(1)}, u32[]{:S(2)}, u32[]{:S(2)}) collective-permute-start(bf16[2,144,256]{2,1,0:T(8,128)(2,1)S(1)} %get-tuple-element.121), channel_id=1, source_target_pairs={{0,32},{4,12},{8,40},{12,20},{16,48},{20,28},{24,56},{28,4},{32,64... | collective-permute-start | bytes 442376 | tf_op jit(solution)/shard_map/ppermute | solution.py:619
  103.8 4.1 %collective-permute-start.19 = (bf16[2,144,256]{2,1,0:T(8,128)(2,1)S(1)}, bf16[2,144,256]{2,1,0:T(8,128)(2,1)S(1)}, u32[]{:S(2)}, u32[]{:S(2)}) collective-permute-start(bf16[2,144,256]{2,1,0:T(8,128)(2,1)S(1)} %get-tuple-element.94), channel_id=1, source_target_pairs={{0,24},{4,100},{8,0},{12,108},{16,8},{20,116},{24,16},{28,124},{32... | collective-permute-start | bytes 442376 | tf_op jit(solution)/shard_map/ppermute | solution.py:619
  105.5 6.8 %collective-permute-start.20 = (bf16[2,144,256]{2,1,0:T(8,128)(2,1)S(1)}, bf16[2,144,256]{2,1,0:T(8,128)(2,1)S(1)}, u32[]{:S(2)}, u32[]{:S(2)}) collective-permute-start(bf16[2,144,256]{2,1,0:T(8,128)(2,1)S(1)} %get-tuple-element.94), channel_id=1, source_target_pairs={{0,8},{4,36},{8,16},{12,44},{16,24},{20,52},{24,0},{28,60},{32,40}... | collective-permute-start | bytes 442376 | tf_op jit(solution)/shard_map/ppermute | solution.py:619
  105.5 6.8 %collective-permute-start.21 = (bf16[2,144,256]{2,1,0:T(8,128)(2,1)S(1)}, bf16[2,144,256]{2,1,0:T(8,128)(2,1)S(1)}, u32[]{:S(2)}, u32[]{:S(2)}) collective-permute-start(bf16[2,144,256]{2,1,0:T(8,128)(2,1)S(1)} %get-tuple-element.94), channel_id=1, source_target_pairs={{0,16},{4,68},{8,24},{12,76},{16,0},{20,84},{24,8},{28,92},{32,48}... | collective-permute-start | bytes 442376 | tf_op jit(solution)/shard_map/ppermute | solution.py:619
  112.6 8.4 %collective-permute-start.23 = (bf16[2,144,256]{2,1,0:T(8,128)(2,1)S(1)}, bf16[2,144,256]{2,1,0:T(8,128)(2,1)S(1)}, u32[]{:S(2)}, u32[]{:S(2)}) collective-permute-start(bf16[2,144,256]{2,1,0:T(8,128)(2,1)S(1)} %get-tuple-element.136), channel_id=1, source_target_pairs={{0,32},{4,12},{8,40},{12,20},{16,48},{20,28},{24,56},{28,4},{32,64... | collective-permute-start | bytes 442376 | tf_op jit(solution)/shard_map/ppermute | solution.py:619
  112.6 8.4 %collective-permute-start.24 = (bf16[2,144,256]{2,1,0:T(8,128)(2,1)S(1)}, bf16[2,144,256]{2,1,0:T(8,128)(2,1)S(1)}, u32[]{:S(2)}, u32[]{:S(2)}) collective-permute-start(bf16[2,144,256]{2,1,0:T(8,128)(2,1)S(1)} %get-tuple-element.137), channel_id=1, source_target_pairs={{0,64},{4,20},{8,72},{12,28},{16,80},{20,4},{24,88},{28,12},{32,96... | collective-permute-start | bytes 442376 | tf_op jit(solution)/shard_map/ppermute | solution.py:619
  114.4 6.6 %collective-permute-start.22 = (bf16[2,144,256]{2,1,0:T(8,128)(2,1)S(1)}, bf16[2,144,256]{2,1,0:T(8,128)(2,1)S(1)}, u32[]{:S(2)}, u32[]{:S(2)}) collective-permute-start(bf16[2,144,256]{2,1,0:T(8,128)(2,1)S(1)} %get-tuple-element.118), channel_id=1, source_target_pairs={{0,96},{4,28},{8,104},{12,4},{16,112},{20,12},{24,120},{28,20},{32... | collective-permute-start | bytes 442376 | tf_op jit(solution)/shard_map/ppermute | solution.py:619
  124.8 15.6 %collective-permute-start.32 = (bf16[512,768]{1,0:T(8,128)(2,1)S(1)}, bf16[512,768]{1,0:T(8,128)(2,1)S(1)}, u32[]{:S(2)}, u32[]{:S(2)}) collective-permute-start(bf16[512,768]{1,0:T(8,128)(2,1)S(1)} %get-tuple-element.126), channel_id=1, source_target_pairs={{0,32},{4,12},{8,40},{12,20},{16,48},{20,28},{24,56},{28,4},{32,64... | collective-permute-start | bytes 2359304 | tf_op jit(solution)/shard_map/ppermute | solution.py:619
  125.5 15.3 %collective-permute-start.36 = (bf16[512,768]{1,0:T(8,128)(2,1)S(1)}, bf16[512,768]{1,0:T(8,128)(2,1)S(1)}, u32[]{:S(2)}, u32[]{:S(2)}) collective-permute-start(bf16[512,768]{1,0:T(8,128)(2,1)S(1)} %get-tuple-element.125), channel_id=1, source_target_pairs={{0,96},{4,28},{8,104},{12,4},{16,112},{20,12},{24,120},{28,20},{32... | collective-permute-start | bytes 2359304 | tf_op jit(solution)/shard_map/ppermute | solution.py:619
  127.6 16.2 %collective-permute-start.25 = (bf16[512,1024]{1,0:T(8,128)(2,1)S(1)}, bf16[512,1024]{1,0:T(8,128)(2,1)S(1)}, u32[]{:S(2)}, u32[]{:S(2)}) collective-permute-start(bf16[512,1024]{1,0:T(8,128)(2,1)S(1)} %get-tuple-element.100.mkv_ref), channel_id=1, source_target_pairs={{0,4},{4,0},{1,5},{5,1},{2,6},{6,2},{3,7},{7,3},{8,12},{12,8},{9,1... | collective-permute-start | bytes 3145736 | tf_op jit(solution)/shard_map/ppermute | solution.py:608
  135.7 8.1 %collective-permute-start.26 = (bf16[256,1024]{1,0:T(8,128)(2,1)S(1)}, bf16[256,1024]{1,0:T(8,128)(2,1)S(1)}, u32[]{:S(2)}, u32[]{:S(2)}) collective-permute-start(bf16[256,1024]{1,0:T(8,128)(2,1)S(1)} %get-tuple-element.101.mq_ref), channel_id=1, source_target_pairs={{0,4},{4,0},{1,5},{5,1},{2,6},{6,2},{3,7},{7,3},{8,12},{12,8},{9,1... | collective-permute-start | bytes 1572872 | tf_op jit(solution)/shard_map/ppermute | solution.py:608
  140.5 12.8 %collective-permute-start.35 = (bf16[512,768]{1,0:T(8,128)(2,1)S(1)}, bf16[512,768]{1,0:T(8,128)(2,1)S(1)}, u32[]{:S(2)}, u32[]{:S(2)}) collective-permute-start(bf16[512,768]{1,0:T(8,128)(2,1)S(1)} %slice.203), channel_id=1, source_target_pairs={{0,32},{4,12},{8,40},{12,20},{16,48},{20,28},{24,56},{28,4},{32,64... | collective-permute-start | bytes 2359304 | tf_op jit(solution)/shard_map/ppermute | solution.py:619
  140.8 12.5 %collective-permute-start.34 = (bf16[512,768]{1,0:T(8,128)(2,1)S(1)}, bf16[512,768]{1,0:T(8,128)(2,1)S(1)}, u32[]{:S(2)}, u32[]{:S(2)}) collective-permute-start(bf16[512,768]{1,0:T(8,128)(2,1)S(1)} %slice.204), channel_id=1, source_target_pairs={{0,96},{4,28},{8,104},{12,4},{16,112},{20,12},{24,120},{28,20},{32... | collective-permute-start | bytes 2359304 | tf_op jit(solution)/shard_map/ppermute | solution.py:619
  143.7 17.6 %collective-permute-start.33 = (bf16[512,768]{1,0:T(8,128)(2,1)S(1)}, bf16[512,768]{1,0:T(8,128)(2,1)S(1)}, u32[]{:S(2)}, u32[]{:S(2)}) collective-permute-start(bf16[512,768]{1,0:T(8,128)(2,1)S(1)} %fusion.3), channel_id=1, source_target_pairs={{0,32},{4,12},{8,40},{12,20},{16,48},{20,28},{24,56},{28,4},{32,64... | collective-permute-start | bytes 2359304 | tf_op jit(solution)/shard_map/ppermute | solution.py:619
  143.8 17.5 %collective-permute-start.37 = (bf16[512,768]{1,0:T(8,128)(2,1)S(1)}, bf16[512,768]{1,0:T(8,128)(2,1)S(1)}, u32[]{:S(2)}, u32[]{:S(2)}) collective-permute-start(bf16[512,768]{1,0:T(8,128)(2,1)S(1)} %fusion.1), channel_id=1, source_target_pairs={{0,96},{4,28},{8,104},{12,4},{16,112},{20,12},{24,120},{28,20},{32... | collective-permute-start | bytes 2359304 | tf_op jit(solution)/shard_map/ppermute | solution.py:619
  149.3 20.9 %collective-permute-start.29 = (bf16[512,1024]{1,0:T(8,128)(2,1)S(1)}, bf16[512,1024]{1,0:T(8,128)(2,1)S(1)}, u32[]{:S(2)}, u32[]{:S(2)}) collective-permute-start(bf16[512,1024]{1,0:T(8,128)(2,1)S(1)} %convert_element_type.133), channel_id=1, source_target_pairs={{0,1},{1,2},{2,3},{3,0},{4,7},{5,4},{6,5},{7,6},{8,9},{9,10},{10,1... | collective-permute-start | bytes 3145736 | tf_op jit(solution)/shard_map/ppermute | solution.py:626
  161.8 10.3 %collective-permute-start.38 = (bf16[128,768]{1,0:T(8,128)(2,1)S(1)}, bf16[128,768]{1,0:T(8,128)(2,1)S(1)}, u32[]{:S(2)}, u32[]{:S(2)}) collective-permute-start(bf16[128,768]{1,0:T(8,128)(2,1)S(1)} %get-tuple-element.129), channel_id=1, source_target_pairs={{0,8},{4,36},{8,16},{12,44},{16,24},{20,52},{24,0},{28,60},{32,40}... | collective-permute-start | bytes 589832 | tf_op jit(solution)/shard_map/ppermute | solution.py:619
  161.9 10.4 %collective-permute-start.40 = (bf16[128,768]{1,0:T(8,128)(2,1)S(1)}, bf16[128,768]{1,0:T(8,128)(2,1)S(1)}, u32[]{:S(2)}, u32[]{:S(2)}) collective-permute-start(bf16[128,768]{1,0:T(8,128)(2,1)S(1)} %get-tuple-element.130), channel_id=1, source_target_pairs={{0,24},{4,100},{8,0},{12,108},{16,8},{20,116},{24,16},{28,124},{32... | collective-permute-start | bytes 589832 | tf_op jit(solution)/shard_map/ppermute | solution.py:619
  168.9 14.9 %collective-permute-start.28 = (bf16[512,1024]{1,0:T(8,128)(2,1)S(1)}, bf16[512,1024]{1,0:T(8,128)(2,1)S(1)}, u32[]{:S(2)}, u32[]{:S(2)}) collective-permute-start(bf16[512,1024]{1,0:T(8,128)(2,1)S(1)} %slice.202), channel_id=1, source_target_pairs={{0,3},{1,0},{2,1},{3,2},{4,5},{5,6},{6,7},{7,4},{8,11},{9,8},{10,9... | collective-permute-start | bytes 3145736 | tf_op jit(solution)/shard_map/ppermute | solution.py:626
  170.6 18.5 %collective-permute-start.30 = (bf16[512,1024]{1,0:T(8,128)(2,1)S(1)}, bf16[512,1024]{1,0:T(8,128)(2,1)S(1)}, u32[]{:S(2)}, u32[]{:S(2)}) collective-permute-start(bf16[512,1024]{1,0:T(8,128)(2,1)S(1)} %fusion), channel_id=1, source_target_pairs={{0,1},{1,2},{2,3},{3,0},{4,7},{5,4},{6,5},{7,6},{8,9},{9,10},{10,1... | collective-permute-start | bytes 3145736 | tf_op jit(solution)/shard_map/ppermute | solution.py:626
  172.2 24.6 %collective-permute-start.39 = (bf16[256,768]{1,0:T(8,128)(2,1)S(1)}, bf16[256,768]{1,0:T(8,128)(2,1)S(1)}, u32[]{:S(2)}, u32[]{:S(2)}) collective-permute-start(bf16[256,768]{1,0:T(8,128)(2,1)S(1)} %pad_maximum_fusion.3), channel_id=1, source_target_pairs={{0,8},{4,36},{8,16},{12,44},{16,24},{20,52},{24,0},{28,60},{32,40}... | collective-permute-start | bytes 1179656 | tf_op jit(solution)/shard_map/ppermute | solution.py:619
  172.4 24.4 %collective-permute-start.41 = (bf16[256,768]{1,0:T(8,128)(2,1)S(1)}, bf16[256,768]{1,0:T(8,128)(2,1)S(1)}, u32[]{:S(2)}, u32[]{:S(2)}) collective-permute-start(bf16[256,768]{1,0:T(8,128)(2,1)S(1)} %pad_maximum_fusion.4), channel_id=1, source_target_pairs={{0,24},{4,100},{8,0},{12,108},{16,8},{20,116},{24,16},{28,124},{32... | collective-permute-start | bytes 1179656 | tf_op jit(solution)/shard_map/ppermute | solution.py:619
  189.6 9.9 %collective-permute-start.31 = (bf16[512,512]{1,0:T(8,128)(2,1)S(1)}, bf16[512,512]{1,0:T(8,128)(2,1)S(1)}, u32[]{:S(2)}, u32[]{:S(2)}) collective-permute-start(bf16[512,512]{1,0:T(8,128)(2,1)S(1)} %get-tuple-element.106), channel_id=1, source_target_pairs={{0,4},{4,0},{1,5},{5,1},{2,6},{6,2},{3,7},{7,3},{8,12},{12,8},{9,1... | collective-permute-start | bytes 1572872 | tf_op jit(solution)/shard_map/ppermute | solution.py:608
  197.0 1.6 collective-permute-start.42

commit v3 on v2

--- a/solution.py
+++ b/solution.py
@@ -16,7 +16,8 @@
 TN = (((0,), (0,)), ((), ()))
 NN = (((1,), (0,)), ((), ()))
 SWAP = ((0, 1), (1, 0))
-STATE_ROWS = 144
+STATE_ROWS = 136
+SENT_ROWS = 272
 MIB = 1 << 20
 
 
@@ -184,6 +185,18 @@
     return (projected - total * (rows.astype(F32) * scale)) * scale
 
 
+def send_state(ref, carry_ref):
+    for head in range(2):
+        ref[128 * head : 128 * head + 128, :] = carry_ref[head, :128, :].astype(BF16)
+    rest = jnp.zeros((SENT_ROWS - 258, 256), F32)
+    sums = [carry_ref[0, 128:129, :], carry_ref[1, 128:129, :], rest]
+    ref[256:, :] = jnp.concatenate(sums, 0).astype(BF16)
+
+
+def state_of(ref, head):
+    return ref[128 * head : 128 * head + 128, :], ref[256 + head : 257 + head, :]
+
+
 def mask_of(size):
     return lax.broadcasted_iota(jnp.int32, (size, size), 0) >= lax.broadcasted_iota(
         jnp.int32, (size, size), 1
@@ -218,7 +231,7 @@
             carry_ref[head] = state + jnp.concatenate([main, row, pad], 0)
 
     over_chunks(kvq_ref.shape[0] // CHUNK, chunk)
-    total_ref[...] = carry_ref[...].astype(BF16)
+    send_state(total_ref, carry_ref)
 
 
 def keys_stage(kvq, seed):
@@ -232,7 +245,7 @@
         out_shape=[
             jax.ShapeDtypeStruct((tok, 512), BF16),
             jax.ShapeDtypeStruct((n,) + state, F32),
-            jax.ShapeDtypeStruct(state, BF16),
+            jax.ShapeDtypeStruct((SENT_ROWS, 256), BF16),
         ],
         scratch_shapes=[pltpu.VMEM(state, F32)],
         compiler_params=params(),
@@ -296,8 +309,8 @@
     def chunk(i, rows):
         for head in range(2):
             cols = slice(128 * head, 128 * head + 128)
-            main = prefix_ref[head, :128, :].astype(BF16)
-            row = prefix_ref[head, 128:129, :]
+            main, row = state_of(prefix_ref, head)
+            main = main.astype(BF16)
             qf = qf_ref[rows, 256 * head : 256 * head + 256]
             qf32 = qf.astype(F32)
             num = num_ref[rows, cols] + dot(qf, main, NT)
@@ -312,7 +325,7 @@
             carry_ref[head, 128:129, :] += jnp.sum(qf32 * gd, 0, keepdims=True)
 
     over_chunks(qf_ref.shape[0] // CHUNK, chunk)
-    total_ref[...] = carry_ref[...].astype(BF16)
+    send_state(total_ref, carry_ref)
 
 
 def ratio_stage(qf, num, den, g, prefix):
@@ -326,7 +339,7 @@
         out_shape=[
             jax.ShapeDtypeStruct((tok, 256), BF16),
             jax.ShapeDtypeStruct((2, tok, 1), F32),
-            jax.ShapeDtypeStruct(state, BF16),
+            jax.ShapeDtypeStruct((SENT_ROWS, 256), BF16),
         ],
         scratch_shapes=[pltpu.VMEM(state, F32)],
         compiler_params=params(),
@@ -353,8 +366,9 @@
         v = v_ref[:, cols]
         qf32 = qf.astype(F32)
         pairs = jnp.where(mask, dot(gn, v, NT) + gd, 0.0).astype(BF16)
-        earlier = prefix_ref[head] + before_ref[0, head]
-        main, row = earlier[:128].astype(BF16), earlier[128:129]
+        main, row = state_of(prefix_ref, head)
+        main = (main + before_ref[0, head, :128, :]).astype(BF16)
+        row = row + before_ref[0, head, 128:129, :]
         dqf = dot(pairs, kf, NN) + dot(gn, main, NN) + gd * row
         dq = feature_grad(dqf * qf32, q_ref[:, cols], seed_ref[head]).astype(BF16)
         dq_ref[:, cols] = dq
@@ -384,7 +398,7 @@
             pl.BlockSpec((2, CHUNK, 1), lambda i: (0, n - 1 - i, 0)),
             pl.BlockSpec((2, 128, 256), lambda i: (0, 0, 0)),
             pl.BlockSpec((1,) + state, lambda i: (n - 1 - i, 0, 0, 0)),
-            pl.BlockSpec(state, lambda i: (0, 0, 0)),
+            pl.BlockSpec((SENT_ROWS, 256), lambda i: (0, 0)),
         ],
         out_specs=[
             narrow(0),
@@ -411,8 +425,8 @@
             cols = slice(128 * head, 128 * head + 128)
             wide = slice(256 * head, 256 * head + 256)
             dv_cols = slice(256 + 128 * head, 384 + 128 * head)
-            main = suffix_ref[head, :128, :].astype(BF16)
-            row = suffix_ref[head, 128:129, :]
+            main, row = state_of(suffix_ref, head)
+            main = main.astype(BF16)
             kf = kf_ref[rows, wide]
             dkf = dkf_ref[rows, wide] + dot(kvq_ref[rows, dv_cols], main, NN) + row
             dk = feature_grad(dkf * kf.astype(F32), kvq_ref[rows, cols], seed_ref[head])

time: 201 us -> 200 us (level)
  no operation moved by 1% of the time
where the time goes in v3:
time: 200 us
  starting transfers between devices  69.4 us (35%)
  waiting for transfers between devices  67.9 us (34%)
  Pallas kernels  56.8 us (28%)
  other arithmetic  3.99 us (2%)
    ppermute x32, waiting for transfers between devices, along(): return lax.ppermute(a, ('z', 'y', 'c'), pairs)  48.7 us
    ppermute x32, starting transfers between devices, along(): return lax.ppermute(a, ('z', 'y', 'c'), pairs)  41.9 us
    ppermute x8, starting transfers between devices, swap(): return lax.ppermute(a, 'c', SWAP)  22.2 us
    ppermute x3, waiting for transfers between devices, across(): return lax.ppermute(a, ('c', 'x'), pairs)  12.2 us
    pallas_call x4, Pallas kernels, project(): pl.pallas_call(body, in_specs=[VMEM] * len(ops), out_specs=VMEM, out_shap...  9.38 us
    pallas_call x8, Pallas kernels, wgrad_call(): pl.pallas_call(body, in_specs=[VMEM] * (2 + len(early)), out_specs=VMEM,...  9.18 us
    pallas_call x4, Pallas kernels, arrange(): pl.pallas_call(arrange_body, out_shape=[jax.ShapeDtypeStruct((2 * size, 4...  7.88 us
    pallas_call x3, Pallas kernels, back(): pl.pallas_call(back_body, in_specs=[SMEM] + [VMEM] * 6, out_specs=VMEM, o...  7.68 us
  transfers between devices with their start and end apart: 43, of which 18 were waited for; matrix products, arithmetic and copies ran while one was open for 2% of the time, Pallas kernels for 28%

profile of v3, /device:TPU:1, one launch (start us, length us, event | category | flops | bytes accessed | tf_op | source)
XLA Modules:
  0.0 200.1 jit_solution(2719964847296271302)
XLA Ops:
  1.1 1.4 collective-permute-start
  2.5 1.8 halve.1
  4.3 5.5 %collective-permute-done.1 = bf16[128,768]{1,0:T(8,128)(2,1)S(1)} collective-permute-done((bf16[128,768]{1,0:T(8,128)(2,1)}, bf16[128,768]{1,0:T(8,128)(2,1)S(1)}, u32[]{:S(2)}, u32[]{:S(2)}) %collective-permute-start.1) | collective-permute-done | bytes 196640 | tf_op jit(solution)/shard_map/ppermute | solution.py:622
  10.8 1.8 collective-permute-start.3
  12.6 2.2 %collective-permute-start.2 = (bf16[256,768]{1,0:T(8,128)(2,1)S(1)}, bf16[256,768]{1,0:T(8,128)(2,1)S(1)}, u32[]{:S(2)}, u32[]{:S(2)}) collective-permute-start(bf16[256,768]{1,0:T(8,128)(2,1)S(1)} %pad_maximum_fusion.2), channel_id=1, source_target_pairs={{0,24},{4,100},{8,0},{12,108},{16,8},{20,116},{24,16},{28,124},{32... | collective-permute-start | bytes 1179656 | tf_op jit(solution)/shard_map/ppermute | solution.py:633
  14.8 5.1 %collective-permute-done.3 = bf16[256,768]{1,0:T(8,128)(2,1)S(1)} collective-permute-done((bf16[256,768]{1,0:T(8,128)(2,1)S(1)}, bf16[256,768]{1,0:T(8,128)(2,1)S(1)}, u32[]{:S(2)}, u32[]{:S(2)}) %collective-permute-start.3) | collective-permute-done | bytes 393248 | tf_op jit(solution)/shard_map/ppermute | solution.py:633
  20.0 3.0 %collective-permute-start.5 = (bf16[128,768]{1,0:T(8,128)(2,1)S(1)}, bf16[128,768]{1,0:T(8,128)(2,1)S(1)}, u32[]{:S(2)}, u32[]{:S(2)}) collective-permute-start(bf16[128,768]{1,0:T(8,128)(2,1)S(1)} %slice.124), channel_id=1, source_target_pairs={{0,24},{4,100},{8,0},{12,108},{16,8},{20,116},{24,16},{28,124},{32... | collective-permute-start | bytes 589832 | tf_op jit(solution)/shard_map/ppermute | solution.py:633
  23.1 1.1 collective-permute-start.8
  24.2 1.8 collective-permute-done.4
  26.1 3.0 %collective-permute-start.7 = (bf16[512,768]{1,0:T(8,128)(2,1)S(1)}, bf16[512,768]{1,0:T(8,128)(2,1)S(1)}, u32[]{:S(2)}, u32[]{:S(2)}) collective-permute-start(bf16[512,768]{1,0:T(8,128)(2,1)S(1)} %constant_dynamic-update-slice_fusion.wb_ref.refs_1_), channel_id=1, source_target_pairs={{0,96},{4,28},{8,104},{12,4},{16,112},{20,12},{24,120},{28,20},{32... | collective-permute-start | bytes 2359304 | tf_op jit(solution)/shard_map/ppermute | solution.py:633
  29.2 1.4 collective-permute-start.9
  30.5 5.0 %collective-permute-done.8.rest_2_.refs_6_ = bf16[512,768]{1,0:T(8,128)(2,1)S(1)} collective-permute-done((bf16[512,768]{1,0:T(8,128)(2,1)S(1)}, bf16[512,768]{1,0:T(8,128)(2,1)S(1)}, u32[]{:S(2)}, u32[]{:S(2)}) %collective-permute-start.8) | collective-permute-done | bytes 786464 | tf_op jit(solution)/shard_map/ppermute | solution.py:633
  35.6 2.4 %collective-permute-done.7.rest_1_.refs_3_ = bf16[512,768]{1,0:T(8,128)(2,1)S(1)} collective-permute-done((bf16[512,768]{1,0:T(8,128)(2,1)S(1)}, bf16[512,768]{1,0:T(8,128)(2,1)S(1)}, u32[]{:S(2)}, u32[]{:S(2)}) %collective-permute-start.7) | collective-permute-done | bytes 786464 | tf_op jit(solution)/shard_map/ppermute | solution.py:633
  38.0 3.4 %collective-permute-start.11 = (bf16[512,768]{1,0:T(8,128)(2,1)S(1)}, bf16[512,768]{1,0:T(8,128)(2,1)S(1)}, u32[]{:S(2)}, u32[]{:S(2)}) collective-permute-start(bf16[512,768]{1,0:T(8,128)(2,1)S(1)} %collective-permute-done.7.rest_1_.refs_3_), channel_id=1, source_target_pairs={{0,96},{4,28},{8,104},{12,4},{16,112},{20,12},{24,120},{28,20},{32... | collective-permute-start | bytes 2359304 | tf_op jit(solution)/shard_map/ppermute | solution.py:633
  41.4 5.0 %collective-permute-done.6.rest_0_.refs_2_ = bf16[512,768]{1,0:T(8,128)(2,1)S(1)} collective-permute-done((bf16[512,768]{1,0:T(8,128)(2,1)S(1)}, bf16[512,768]{1,0:T(8,128)(2,1)S(1)}, u32[]{:S(2)}, u32[]{:S(2)}) %collective-permute-start.6) | collective-permute-done | bytes 786464 | tf_op jit(solution)/shard_map/ppermute | solution.py:633
  46.4 6.0 %collective-permute-done.10.w_ref.refs_4_ = bf16[512,768]{1,0:T(8,128)(2,1)S(1)} collective-permute-done((bf16[512,768]{1,0:T(8,128)(2,1)S(1)}, bf16[512,768]{1,0:T(8,128)(2,1)S(1)}, u32[]{:S(2)}, u32[]{:S(2)}) %collective-permute-start.10) | collective-permute-done | bytes 786464 | tf_op jit(solution)/shard_map/ppermute | solution.py:633
  52.4 2.4 %collective-permute-done.11.w_ref.refs_5_ = bf16[512,768]{1,0:T(8,128)(2,1)S(1)} collective-permute-done((bf16[512,768]{1,0:T(8,128)(2,1)S(1)}, bf16[512,768]{1,0:T(8,128)(2,1)S(1)}, u32[]{:S(2)}, u32[]{:S(2)}) %collective-permute-start.11) | collective-permute-done | bytes 786464 | tf_op jit(solution)/shard_map/ppermute | solution.py:633
  54.9 4.0 %collect.1.wm_ref = bf16[4096,768]{1,0:T(8,128)(2,1)S(1)} custom-call(s32[16]{0:T(128)S(1)} %select_n.213.place_ref, bf16[512,768]{1,0:T(8,128)(2,1)S(1)} %pad_maximum_fusion.wa_ref.refs_0_, bf16[512,768]{1,0:T(8,128)(2,1)S(1)} %constant_dynamic-update-slice_fusion.wb_ref.refs_1_, bf16[512,768]{1,0:T(8,128)(2,1)S(1)} %collective-permute-done.6.rest_0_.refs_2_, ...), custom_call_target="tpu_custom_call" | custom-call | flops 1048576 | bytes 12582912 | tf_op jit(solution)/shard_map/collect/pallas_call | solution.py:533
  58.9 5.2 %collective-permute-start.27 = (bf16[4096,768]{1,0:T(8,128)(2,1)S(1)}, bf16[4096,768]{1,0:T(8,128)(2,1)S(1)}, u32[]{:S(2)}, u32[]{:S(2)}) collective-permute-start(bf16[4096,768]{1,0:T(8,128)(2,1)S(1)} %collect.1.wm_ref), channel_id=1, source_target_pairs={{0,4},{4,0},{1,5},{5,1},{2,6},{6,2},{3,7},{7,3},{8,12},{12,8},{9,1... | collective-permute-start | bytes 18874376 | tf_op jit(solution)/shard_map/ppermute | solution.py:622
  64.3 2.0 arrange.4
  66.2 2.3 %shard_map.93.acc_ref = f32[1024,768]{1,0:T(8,128)S(1)} custom-call(bf16[1024,1024]{1,0:T(8,128)(2,1)S(1)} %get-tuple-element.64.x_ref, bf16[512,768]{1,0:T(8,128)(2,1)S(1)} %pad_maximum_fusion.wa_ref.refs_0_, bf16[512,768]{1,0:T(8,128)(2,1)S(1)} %constant_dynamic-update-slice_fusion.wb_ref.refs_1_), custom_call_target="tpu_custom_call" | custom-call | flops 1610612736 | bytes 8388608 | tf_op jit(solution)/shard_map/pallas_call | solution.py:162
  68.6 2.0 arrange.5
  70.6 2.0 arrange.6
  72.5 2.0 arrange.7
  74.5 4.0 %shard_map.94.acc_ref = f32[1024,768]{1,0:T(8,128)S(1)} custom-call(f32[1024,768]{1,0:T(8,128)S(1)} %shard_map.93.acc_ref, bf16[1024,1024]{1,0:T(8,128)(2,1)S(1)} %get-tuple-element.71.xa_ref, bf16[1024,1024]{1,0:T(8,128)(2,1)S(1)} %get-tuple-element.72.xb_ref, bf16[512,768]{1,0:T(8,128)(2,1)S(1)} %collective-permute-done.6.rest_0_.refs_2_, ...), custom_call_target="tpu_custom_call" | custom-call | flops 3221225472 | bytes 8388608 | tf_op jit(solution)/shard_map/pallas_call | solution.py:162
  78.6 1.5 shard_map.95.acc_ref
  80.1 1.5 shard_map.96.kvq_ref.q_ref.v_ref
  81.6 2.2 %keys_stage.1 = (bf16[1024,512]{1,0:T(8,128)(2,1)S(1)}, f32[4,2,136,256]{3,2,1,0:T(8,128)S(1)}, bf16[272,256]{1,0:T(8,128)(2,1)S(1)}) custom-call(bf16[1024,768]{1,0:T(8,128)(2,1)S(1)} %shard_map.96.kvq_ref.q_ref.v_ref, bf16[2,128,256]{2,1,0:T(8,128)(2,1)S(1)} %select_convert_fusion.2.seed_ref), custom_call_target="tpu_custom_call" | custom-call | flops 268435456 | bytes 4194304 | tf_op jit(solution)/shard_map/keys_stage/pallas_call | solution.py:241
  83.9 3.4 %collective-permute-start.14 = (bf16[272,256]{1,0:T(8,128)(2,1)S(1)}, bf16[272,256]{1,0:T(8,128)(2,1)S(1)}, u32[]{:S(2)}, u32[]{:S(2)}) collective-permute-start(bf16[272,256]{1,0:T(8,128)(2,1)S(1)} %get-tuple-element.83), channel_id=1, source_target_pairs={{0,24},{4,100},{8,0},{12,108},{16,8},{20,116},{24,16},{28,124},{32... | collective-permute-start | bytes 417800 | tf_op jit(solution)/shard_map/ppermute | solution.py:633
  87.3 1.1 collective-permute-start.15
  88.5 1.5 collective-permute-done.13
  90.0 3.0 %collective-permute-done.15 = bf16[272,256]{1,0:T(8,128)(2,1)S(1)} collective-permute-done((bf16[272,256]{1,0:T(8,128)(2,1)S(1)}, bf16[272,256]{1,0:T(8,128)(2,1)S(1)}, u32[]{:S(2)}, u32[]{:S(2)}) %collective-permute-start.15) | collective-permute-done | bytes 139296 | tf_op jit(solution)/shard_map/ppermute | solution.py:633
  94.8 3.0 %local_stage.1 = (bf16[1024,512]{1,0:T(8,128)(2,1)S(1)}, bf16[1024,512]{1,0:T(8,128)(2,1)S(1)}, f32[1024,256]{1,0:T(8,128)S(1)}, f32[2,1024,1]{2,1,0:T(8,128)S(1)}) custom-call(bf16[1024,768]{1,0:T(8,128)(2,1)S(1)} %shard_map.96.kvq_ref.q_ref.v_ref, bf16[1024,768]{1,0:T(8,128)(2,1)S(1)} %shard_map.96.kvq_ref.q_ref.v_ref, ...), custom_call_target="tpu_custom_call" | custom-call | flops 671088640 | bytes 6291456 | tf_op jit(solution)/shard_map/local_stage/pallas_call | solution.py:278
  97.8 1.6 collective-permute-done.18
  99.4 1.4 collective-permute-done.16
  101.0 2.5 %ratio_stage.1 = (bf16[1024,256]{1,0:T(8,128)(2,1)S(1)}, f32[2,1024,1]{2,1,0:T(8,128)S(1)}, bf16[272,256]{1,0:T(8,128)(2,1)S(1)}) custom-call(bf16[1024,512]{1,0:T(8,128)(2,1)S(1)} %get-tuple-element.77.qf_ref, f32[1024,256]{1,0:T(8,128)S(1)} %get-tuple-element.79.num_ref, f32[2,1024,1]{2,1,0:T(8,128)S(1)} %get-tuple-element.80.den_ref, ...), custom_call_target="tpu_custom_call" | custom-call | flops 268435456 | bytes 4194304 | tf_op jit(solution)/shard_map/ratio_stage/pallas_call | solution.py:335
  103.5 1.8 collective-permute-start.19
  105.3 1.3 collective-permute-start.21
  107.5 4.4 %collective-permute-done.20 = bf16[272,256]{1,0:T(8,128)(2,1)S(1)} collective-permute-done((bf16[272,256]{1,0:T(8,128)(2,1)S(1)}, bf16[272,256]{1,0:T(8,128)(2,1)S(1)}, u32[]{:S(2)}, u32[]{:S(2)}) %collective-permute-start.20) | collective-permute-done | bytes 139296 | tf_op jit(solution)/shard_map/ppermute | solution.py:633
  112.2 1.8 collective-permute-start.24
  114.8 4.8 %middle_stage.1 = (bf16[1024,256]{1,0:T(8,128)(2,1)S(1)}, bf16[256,1024]{1,0:T(8,128)(2,1)S(1)}, f32[1024,512]{1,0:T(8,128)S(1)}, f32[1024,256]{1,0:T(8,128)S(1)}) custom-call(bf16[1024,768]{1,0:T(8,128)(2,1)S(1)} %shard_map.96.kvq_ref.q_ref.v_ref, bf16[1024,768]{1,0:T(8,128)(2,1)S(1)} %shard_map.96.kvq_ref.q_ref.v_ref, ...), custom_call_target="tpu_custom_call" | custom-call | flops 1342177280 | bytes 10485760 | tf_op jit(solution)/shard_map/middle_stage/pallas_call | solution.py:393
  120.7 2.0 last_stage.1
  122.7 1.4 shard_map.102
  125.0 2.1 %collective-permute-start.36 = (bf16[512,768]{1,0:T(8,128)(2,1)S(1)}, bf16[512,768]{1,0:T(8,128)(2,1)S(1)}, u32[]{:S(2)}, u32[]{:S(2)}) collective-permute-start(bf16[512,768]{1,0:T(8,128)(2,1)S(1)} %get-tuple-element.125), channel_id=1, source_target_pairs={{0,96},{4,28},{8,104},{12,4},{16,112},{20,12},{24,120},{28,20},{32... | collective-permute-start | bytes 2359304 | tf_op jit(solution)/shard_map/ppermute | solution.py:633
  127.1 8.2 %collective-permute-start.25 = (bf16[512,1024]{1,0:T(8,128)(2,1)S(1)}, bf16[512,1024]{1,0:T(8,128)(2,1)S(1)}, u32[]{:S(2)}, u32[]{:S(2)}) collective-permute-start(bf16[512,1024]{1,0:T(8,128)(2,1)S(1)} %get-tuple-element.100.mkv_ref), channel_id=1, source_target_pairs={{0,4},{4,0},{1,5},{5,1},{2,6},{6,2},{3,7},{7,3},{8,12},{12,8},{9,1... | collective-permute-start | bytes 3145736 | tf_op jit(solution)/shard_map/ppermute | solution.py:622
  137.1 1.4 shard_map.100
  138.6 1.4 shard_map.104
  140.4 2.7 %collective-permute-start.34 = (bf16[512,768]{1,0:T(8,128)(2,1)S(1)}, bf16[512,768]{1,0:T(8,128)(2,1)S(1)}, u32[]{:S(2)}, u32[]{:S(2)}) collective-permute-start(bf16[512,768]{1,0:T(8,128)(2,1)S(1)} %slice.204), channel_id=1, source_target_pairs={{0,96},{4,28},{8,104},{12,4},{16,112},{20,12},{24,120},{28,20},{32... | collective-permute-start | bytes 2359304 | tf_op jit(solution)/shard_map/ppermute | solution.py:633
  143.4 2.7 %collective-permute-start.37 = (bf16[512,768]{1,0:T(8,128)(2,1)S(1)}, bf16[512,768]{1,0:T(8,128)(2,1)S(1)}, u32[]{:S(2)}, u32[]{:S(2)}) collective-permute-start(bf16[512,768]{1,0:T(8,128)(2,1)S(1)} %fusion.1), channel_id=1, source_target_pairs={{0,96},{4,28},{8,104},{12,4},{16,112},{20,12},{24,120},{28,20},{32... | collective-permute-start | bytes 2359304 | tf_op jit(solution)/shard_map/ppermute | solution.py:633
  147.0 1.8 back.5
  148.9 2.5 %collective-permute-start.29 = (bf16[512,1024]{1,0:T(8,128)(2,1)S(1)}, bf16[512,1024]{1,0:T(8,128)(2,1)S(1)}, u32[]{:S(2)}, u32[]{:S(2)}) collective-permute-start(bf16[512,1024]{1,0:T(8,128)(2,1)S(1)} %convert_element_type.133), channel_id=1, source_target_pairs={{0,1},{1,2},{2,3},{3,0},{4,7},{5,4},{6,5},{7,6},{8,9},{9,10},{10,1... | collective-permute-start | bytes 3145736 | tf_op jit(solution)/shard_map/ppermute | solution.py:640
  151.5 1.4 shard_map.98
  152.9 8.0 %collective-permute-done.33 = bf16[512,768]{1,0:T(8,128)(2,1)S(1)} collective-permute-done((bf16[512,768]{1,0:T(8,128)(2,1)S(1)}, bf16[512,768]{1,0:T(8,128)(2,1)S(1)}, u32[]{:S(2)}, u32[]{:S(2)}) %collective-permute-start.33) | collective-permute-done | bytes 786464 | tf_op jit(solution)/shard_map/ppermute | solution.py:633
  161.5 2.7 %collective-permute-start.40 = (bf16[128,768]{1,0:T(8,128)(2,1)S(1)}, bf16[128,768]{1,0:T(8,128)(2,1)S(1)}, u32[]{:S(2)}, u32[]{:S(2)}) collective-permute-start(bf16[128,768]{1,0:T(8,128)(2,1)S(1)} %get-tuple-element.130), channel_id=1, source_target_pairs={{0,24},{4,100},{8,0},{12,108},{16,8},{20,116},{24,16},{28,124},{32... | collective-permute-start | bytes 589832 | tf_op jit(solution)/shard_map/ppermute | solution.py:633
  164.2 4.1 %back.4 = f32[1024,1024]{1,0:T(8,128)S(1)} custom-call(s32[2]{0:T(128)S(1)} %pad_add_fusion.1.place_ref, bf16[512,1024]{1,0:T(8,128)(2,1)S(1)} %get-tuple-element.100.mkv_ref, bf16[256,1024]{1,0:T(8,128)(2,1)S(1)} %get-tuple-element.101.mq_ref, bf16[512,1024]{1,0:T(8,128)(2,1)S(1)} %collective-permute-done.25.tkv_ref, ...), custom_call_target="tpu_custom_call" | custom-call | flops 3221225472 | bytes 8388608 | tf_op jit(solution)/shard_map/back/pallas_call | solution.py:566
  168.5 1.3 collective-permute-start.28
  170.2 1.5 collective-permute-start.30
  172.0 2.7 %collective-permute-start.41 = (bf16[256,768]{1,0:T(8,128)(2,1)S(1)}, bf16[256,768]{1,0:T(8,128)(2,1)S(1)}, u32[]{:S(2)}, u32[]{:S(2)}) collective-permute-start(bf16[256,768]{1,0:T(8,128)(2,1)S(1)} %pad_maximum_fusion.4), channel_id=1, source_target_pairs={{0,24},{4,100},{8,0},{12,108},{16,8},{20,116},{24,16},{28,124},{32... | collective-permute-start | bytes 1179656 | tf_op jit(solution)/shard_map/ppermute | solution.py:633
  174.7 1.8 back.3.own_ref
  176.5 7.0 %collective-permute-done.28.a_ref = bf16[512,1024]{1,0:T(8,128)(2,1)S(1)} collective-permute-done((bf16[512,1024]{1,0:T(8,128)(2,1)S(1)}, bf16[512,1024]{1,0:T(8,128)(2,1)S(1)}, u32[]{:S(2)}, u32[]{:S(2)}) %collective-permute-start.28) | collective-permute-done | bytes 1048608 | tf_op jit(solution)/shard_map/ppermute | solution.py:640
  183.4 5.2 %collective-permute-done.30.b_ref = bf16[512,1024]{1,0:T(8,128)(2,1)S(1)} collective-permute-done((bf16[512,1024]{1,0:T(8,128)(2,1)S(1)}, bf16[512,1024]{1,0:T(8,128)(2,1)S(1)}, u32[]{:S(2)}, u32[]{:S(2)}) %collective-permute-start.30) | collective-permute-done | bytes 1048608 | tf_op jit(solution)/shard_map/ppermute | solution.py:640
  189.1 7.2 %collective-permute-start.31 = (bf16[512,512]{1,0:T(8,128)(2,1)S(1)}, bf16[512,512]{1,0:T(8,128)(2,1)S(1)}, u32[]{:S(2)}, u32[]{:S(2)}) collective-permute-start(bf16[512,512]{1,0:T(8,128)(2,1)S(1)} %get-tuple-element.106), channel_id=1, source_target_pairs={{0,4},{4,0},{1,5},{5,1},{2,6},{6,2},{3,7},{7,3},{8,12},{12,8},{9,1... | collective-permute-start | bytes 1572872 | tf_op jit(solution)/shard_map/ppermute | solution.py:622
  196.7 1.5 collective-permute-done.42.got_ref
  199.1 1.1 join.1
  (98 shorter events, 14.6 us)
Async XLA Ops:
  1.1 63.1 %collective-permute-start = (bf16[512,4096]{1,0:T(8,128)(2,1)}, bf16[512,4096]{1,0:T(8,128)(2,1)S(1)}, u32[]{:S(2)}, u32[]{:S(2)}) collective-permute-start(bf16[512,4096]{1,0:T(8,128)(2,1)} %own_ref.3), channel_id=1, source_target_pairs={{0,4},{4,0},{1,5},{5,1},{2,6},{6,2},{3,7},{7,3},{8,12},{12,8},{9,1... | collective-permute-start | bytes 12582920 | tf_op jit(solution)/shard_map/ppermute | solution.py:622
  4.3 5.5 %collective-permute-start.1 = (bf16[128,768]{1,0:T(8,128)(2,1)}, bf16[128,768]{1,0:T(8,128)(2,1)S(1)}, u32[]{:S(2)}, u32[]{:S(2)}) collective-permute-start(bf16[128,768]{1,0:T(8,128)(2,1)} %get-tuple-element.70), channel_id=1, source_target_pairs={{0,4},{4,0},{1,5},{5,1},{2,6},{6,2},{3,7},{7,3},{8,12},{12,8},{9,1... | collective-permute-start | bytes 589832 | tf_op jit(solution)/shard_map/ppermute | solution.py:622
  10.8 9.1 %collective-permute-start.3 = (bf16[256,768]{1,0:T(8,128)(2,1)S(1)}, bf16[256,768]{1,0:T(8,128)(2,1)S(1)}, u32[]{:S(2)}, u32[]{:S(2)}) collective-permute-start(bf16[256,768]{1,0:T(8,128)(2,1)S(1)} %pad_maximum_fusion.2), channel_id=1, source_target_pairs={{0,8},{4,36},{8,16},{12,44},{16,24},{20,52},{24,0},{28,60},{32,40}... | collective-permute-start | bytes 1179656 | tf_op jit(solution)/shard_map/ppermute | solution.py:633
  12.6 7.4 %collective-permute-start.2 = (bf16[256,768]{1,0:T(8,128)(2,1)S(1)}, bf16[256,768]{1,0:T(8,128)(2,1)S(1)}, u32[]{:S(2)}, u32[]{:S(2)}) collective-permute-start(bf16[256,768]{1,0:T(8,128)(2,1)S(1)} %pad_maximum_fusion.2), channel_id=1, source_target_pairs={{0,24},{4,100},{8,0},{12,108},{16,8},{20,116},{24,16},{28,124},{32... | collective-permute-start | bytes 1179656 | tf_op jit(solution)/shard_map/ppermute | solution.py:633
  19.9 6.1 %collective-permute-start.4 = (bf16[128,768]{1,0:T(8,128)(2,1)S(1)}, bf16[128,768]{1,0:T(8,128)(2,1)S(1)}, u32[]{:S(2)}, u32[]{:S(2)}) collective-permute-start(bf16[128,768]{1,0:T(8,128)(2,1)S(1)} %slice.123), channel_id=1, source_target_pairs={{0,8},{4,36},{8,16},{12,44},{16,24},{20,52},{24,0},{28,60},{32,40}... | collective-permute-start | bytes 589832 | tf_op jit(solution)/shard_map/ppermute | solution.py:633
  20.0 6.0 %collective-permute-start.5 = (bf16[128,768]{1,0:T(8,128)(2,1)S(1)}, bf16[128,768]{1,0:T(8,128)(2,1)S(1)}, u32[]{:S(2)}, u32[]{:S(2)}) collective-permute-start(bf16[128,768]{1,0:T(8,128)(2,1)S(1)} %slice.124), channel_id=1, source_target_pairs={{0,24},{4,100},{8,0},{12,108},{16,8},{20,116},{24,16},{28,124},{32... | collective-permute-start | bytes 589832 | tf_op jit(solution)/shard_map/ppermute | solution.py:633
  23.1 12.5 %collective-permute-start.8 = (bf16[512,768]{1,0:T(8,128)(2,1)S(1)}, bf16[512,768]{1,0:T(8,128)(2,1)S(1)}, u32[]{:S(2)}, u32[]{:S(2)}) collective-permute-start(bf16[512,768]{1,0:T(8,128)(2,1)S(1)} %pad_maximum_fusion.wa_ref.refs_0_), channel_id=1, source_target_pairs={{0,32},{4,12},{8,40},{12,20},{16,48},{20,28},{24,56},{28,4},{32,64... | collective-permute-start | bytes 2359304 | tf_op jit(solution)/shard_map/ppermute | solution.py:633
  26.1 38.0 %copy-start.2 = (bf16[512,512]{1,0:T(8,128)(2,1)S(1)}, bf16[512,512]{1,0:T(8,128)(2,1)}, u32[]{:S(2)}) copy-start(bf16[512,512]{1,0:T(8,128)(2,1)} %param.11) | copy-start | bytes 1572868
  26.1 38.1 %copy-start.1 = (s32[4,128,256]{2,1,0:T(8,128)S(1)}, s32[4,128,256]{2,1,0:T(8,128)}, u32[]{:S(2)}) copy-start(s32[4,128,256]{2,1,0:T(8,128)} %param.10) | copy-start | bytes 1572868
  26.1 11.9 %collective-permute-start.7 = (bf16[512,768]{1,0:T(8,128)(2,1)S(1)}, bf16[512,768]{1,0:T(8,128)(2,1)S(1)}, u32[]{:S(2)}, u32[]{:S(2)}) collective-permute-start(bf16[512,768]{1,0:T(8,128)(2,1)S(1)} %constant_dynamic-update-slice_fusion.wb_ref.refs_1_), channel_id=1, source_target_pairs={{0,96},{4,28},{8,104},{12,4},{16,112},{20,12},{24,120},{28,20},{32... | collective-permute-start | bytes 2359304 | tf_op jit(solution)/shard_map/ppermute | solution.py:633
  29.1 17.4 %collective-permute-start.6 = (bf16[512,768]{1,0:T(8,128)(2,1)S(1)}, bf16[512,768]{1,0:T(8,128)(2,1)S(1)}, u32[]{:S(2)}, u32[]{:S(2)}) collective-permute-start(bf16[512,768]{1,0:T(8,128)(2,1)S(1)} %pad_maximum_fusion.wa_ref.refs_0_), channel_id=1, source_target_pairs={{0,96},{4,28},{8,104},{12,4},{16,112},{20,12},{24,120},{28,20},{32... | collective-permute-start | bytes 2359304 | tf_op jit(solution)/shard_map/ppermute | solution.py:633
  29.2 17.3 %collective-permute-start.9 = (bf16[512,768]{1,0:T(8,128)(2,1)S(1)}, bf16[512,768]{1,0:T(8,128)(2,1)S(1)}, u32[]{:S(2)}, u32[]{:S(2)}) collective-permute-start(bf16[512,768]{1,0:T(8,128)(2,1)S(1)} %constant_dynamic-update-slice_fusion.wb_ref.refs_1_), channel_id=1, source_target_pairs={{0,32},{4,12},{8,40},{12,20},{16,48},{20,28},{24,56},{28,4},{32,64... | collective-permute-start | bytes 2359304 | tf_op jit(solution)/shard_map/ppermute | solution.py:633
  35.6 16.9 %collective-permute-start.10 = (bf16[512,768]{1,0:T(8,128)(2,1)S(1)}, bf16[512,768]{1,0:T(8,128)(2,1)S(1)}, u32[]{:S(2)}, u32[]{:S(2)}) collective-permute-start(bf16[512,768]{1,0:T(8,128)(2,1)S(1)} %collective-permute-done.8.rest_2_.refs_6_), channel_id=1, source_target_pairs={{0,32},{4,12},{8,40},{12,20},{16,48},{20,28},{24,56},{28,4},{32,64... | collective-permute-start | bytes 2359304 | tf_op jit(solution)/shard_map/ppermute | solution.py:633
  38.0 16.9 %collective-permute-start.11 = (bf16[512,768]{1,0:T(8,128)(2,1)S(1)}, bf16[512,768]{1,0:T(8,128)(2,1)S(1)}, u32[]{:S(2)}, u32[]{:S(2)}) collective-permute-start(bf16[512,768]{1,0:T(8,128)(2,1)S(1)} %collective-permute-done.7.rest_1_.refs_3_), channel_id=1, source_target_pairs={{0,96},{4,28},{8,104},{12,4},{16,112},{20,12},{24,120},{28,20},{32... | collective-permute-start | bytes 2359304 | tf_op jit(solution)/shard_map/ppermute | solution.py:633
  54.9 9.4 %copy-start = (bf16[512,4096]{1,0:T(8,128)(2,1)S(1)}, bf16[512,4096]{1,0:T(8,128)(2,1)}, u32[]{:S(2)}) copy-start(bf16[512,4096]{1,0:T(8,128)(2,1)} %own_ref.3) | copy-start | bytes 12582916
  58.9 88.1 %collective-permute-start.27 = (bf16[4096,768]{1,0:T(8,128)(2,1)S(1)}, bf16[4096,768]{1,0:T(8,128)(2,1)S(1)}, u32[]{:S(2)}, u32[]{:S(2)}) collective-permute-start(bf16[4096,768]{1,0:T(8,128)(2,1)S(1)} %collect.1.wm_ref), channel_id=1, source_target_pairs={{0,4},{4,0},{1,5},{5,1},{2,6},{6,2},{3,7},{7,3},{8,12},{12,8},{9,1... | collective-permute-start | bytes 18874376 | tf_op jit(solution)/shard_map/ppermute | solution.py:622
  64.1 24.4 %collective-permute-start.12 = (bf16[512,512]{1,0:T(8,128)(2,1)S(1)}, bf16[512,512]{1,0:T(8,128)(2,1)S(1)}, u32[]{:S(2)}, u32[]{:S(2)}) collective-permute-start(bf16[512,512]{1,0:T(8,128)(2,1)S(1)} %copy-done.2), channel_id=1, source_target_pairs={{0,4},{4,0},{1,5},{5,1},{2,6},{6,2},{3,7},{7,3},{8,12},{12,8},{9,1... | collective-permute-start | bytes 1572872 | tf_op jit(solution)/shard_map/ppermute | solution.py:622
  83.8 6.2 %collective-permute-start.13 = (bf16[272,256]{1,0:T(8,128)(2,1)S(1)}, bf16[272,256]{1,0:T(8,128)(2,1)S(1)}, u32[]{:S(2)}, u32[]{:S(2)}) collective-permute-start(bf16[272,256]{1,0:T(8,128)(2,1)S(1)} %get-tuple-element.83), channel_id=1, source_target_pairs={{0,8},{4,36},{8,16},{12,44},{16,24},{20,52},{24,0},{28,60},{32,40}... | collective-permute-start | bytes 417800 | tf_op jit(solution)/shard_map/ppermute | solution.py:633
  83.9 6.1 %collective-permute-start.14 = (bf16[272,256]{1,0:T(8,128)(2,1)S(1)}, bf16[272,256]{1,0:T(8,128)(2,1)S(1)}, u32[]{:S(2)}, u32[]{:S(2)}) collective-permute-start(bf16[272,256]{1,0:T(8,128)(2,1)S(1)} %get-tuple-element.83), channel_id=1, source_target_pairs={{0,24},{4,100},{8,0},{12,108},{16,8},{20,116},{24,16},{28,124},{32... | collective-permute-start | bytes 417800 | tf_op jit(solution)/shard_map/ppermute | solution.py:633
  87.3 5.7 %collective-permute-start.15 = (bf16[272,256]{1,0:T(8,128)(2,1)S(1)}, bf16[272,256]{1,0:T(8,128)(2,1)S(1)}, u32[]{:S(2)}, u32[]{:S(2)}) collective-permute-start(bf16[272,256]{1,0:T(8,128)(2,1)S(1)} %get-tuple-element.83), channel_id=1, source_target_pairs={{0,16},{4,68},{8,24},{12,76},{16,0},{20,84},{24,8},{28,92},{32,48}... | collective-permute-start | bytes 417800 | tf_op jit(solution)/shard_map/ppermute | solution.py:633
  93.3 4.6 %collective-permute-start.17 = (bf16[272,256]{1,0:T(8,128)(2,1)S(1)}, bf16[272,256]{1,0:T(8,128)(2,1)S(1)}, u32[]{:S(2)}, u32[]{:S(2)}) collective-permute-start(bf16[272,256]{1,0:T(8,128)(2,1)S(1)} %get-tuple-element.138), channel_id=1, source_target_pairs={{0,96},{4,28},{8,104},{12,4},{16,112},{20,12},{24,120},{28,20},{32... | collective-permute-start | bytes 417800 | tf_op jit(solution)/shard_map/ppermute | solution.py:633
  93.9 5.5 %collective-permute-start.18 = (bf16[272,256]{1,0:T(8,128)(2,1)S(1)}, bf16[272,256]{1,0:T(8,128)(2,1)S(1)}, u32[]{:S(2)}, u32[]{:S(2)}) collective-permute-start(bf16[272,256]{1,0:T(8,128)(2,1)S(1)} %get-tuple-element.139), channel_id=1, source_target_pairs={{0,64},{4,20},{8,72},{12,28},{16,80},{20,4},{24,88},{28,12},{32,96... | collective-permute-start | bytes 417800 | tf_op jit(solution)/shard_map/ppermute | solution.py:633
  93.9 6.9 %collective-permute-start.16 = (bf16[272,256]{1,0:T(8,128)(2,1)S(1)}, bf16[272,256]{1,0:T(8,128)(2,1)S(1)}, u32[]{:S(2)}, u32[]{:S(2)}) collective-permute-start(bf16[272,256]{1,0:T(8,128)(2,1)S(1)} %get-tuple-element.121), channel_id=1, source_target_pairs={{0,32},{4,12},{8,40},{12,20},{16,48},{20,28},{24,56},{28,4},{32,64... | collective-permute-start | bytes 417800 | tf_op jit(solution)/shard_map/ppermute | solution.py:633
  103.5 4.0 %collective-permute-start.19 = (bf16[272,256]{1,0:T(8,128)(2,1)S(1)}, bf16[272,256]{1,0:T(8,128)(2,1)S(1)}, u32[]{:S(2)}, u32[]{:S(2)}) collective-permute-start(bf16[272,256]{1,0:T(8,128)(2,1)S(1)} %get-tuple-element.94), channel_id=1, source_target_pairs={{0,24},{4,100},{8,0},{12,108},{16,8},{20,116},{24,16},{28,124},{32... | collective-permute-start | bytes 417800 | tf_op jit(solution)/shard_map/ppermute | solution.py:633
  105.3 6.6 %collective-permute-start.20 = (bf16[272,256]{1,0:T(8,128)(2,1)S(1)}, bf16[272,256]{1,0:T(8,128)(2,1)S(1)}, u32[]{:S(2)}, u32[]{:S(2)}) collective-permute-start(bf16[272,256]{1,0:T(8,128)(2,1)S(1)} %get-tuple-element.94), channel_id=1, source_target_pairs={{0,8},{4,36},{8,16},{12,44},{16,24},{20,52},{24,0},{28,60},{32,40}... | collective-permute-start | bytes 417800 | tf_op jit(solution)/shard_map/ppermute | solution.py:633
  105.3 6.6 %collective-permute-start.21 = (bf16[272,256]{1,0:T(8,128)(2,1)S(1)}, bf16[272,256]{1,0:T(8,128)(2,1)S(1)}, u32[]{:S(2)}, u32[]{:S(2)}) collective-permute-start(bf16[272,256]{1,0:T(8,128)(2,1)S(1)} %get-tuple-element.94), channel_id=1, source_target_pairs={{0,16},{4,68},{8,24},{12,76},{16,0},{20,84},{24,8},{28,92},{32,48}... | collective-permute-start | bytes 417800 | tf_op jit(solution)/shard_map/ppermute | solution.py:633
  112.1 8.4 %collective-permute-start.23 = (bf16[272,256]{1,0:T(8,128)(2,1)S(1)}, bf16[272,256]{1,0:T(8,128)(2,1)S(1)}, u32[]{:S(2)}, u32[]{:S(2)}) collective-permute-start(bf16[272,256]{1,0:T(8,128)(2,1)S(1)} %get-tuple-element.136), channel_id=1, source_target_pairs={{0,32},{4,12},{8,40},{12,20},{16,48},{20,28},{24,56},{28,4},{32,64... | collective-permute-start | bytes 417800 | tf_op jit(solution)/shard_map/ppermute | solution.py:633
  112.2 8.4 %collective-permute-start.24 = (bf16[272,256]{1,0:T(8,128)(2,1)S(1)}, bf16[272,256]{1,0:T(8,128)(2,1)S(1)}, u32[]{:S(2)}, u32[]{:S(2)}) collective-permute-start(bf16[272,256]{1,0:T(8,128)(2,1)S(1)} %get-tuple-element.137), channel_id=1, source_target_pairs={{0,64},{4,20},{8,72},{12,28},{16,80},{20,4},{24,88},{28,12},{32,96... | collective-permute-start | bytes 417800 | tf_op jit(solution)/shard_map/ppermute | solution.py:633
  113.9 6.6 %collective-permute-start.22 = (bf16[272,256]{1,0:T(8,128)(2,1)S(1)}, bf16[272,256]{1,0:T(8,128)(2,1)S(1)}, u32[]{:S(2)}, u32[]{:S(2)}) collective-permute-start(bf16[272,256]{1,0:T(8,128)(2,1)S(1)} %get-tuple-element.118), channel_id=1, source_target_pairs={{0,96},{4,28},{8,104},{12,4},{16,112},{20,12},{24,120},{28,20},{32... | collective-permute-start | bytes 417800 | tf_op jit(solution)/shard_map/ppermute | solution.py:633
  124.3 15.7 %collective-permute-start.32 = (bf16[512,768]{1,0:T(8,128)(2,1)S(1)}, bf16[512,768]{1,0:T(8,128)(2,1)S(1)}, u32[]{:S(2)}, u32[]{:S(2)}) collective-permute-start(bf16[512,768]{1,0:T(8,128)(2,1)S(1)} %get-tuple-element.126), channel_id=1, source_target_pairs={{0,32},{4,12},{8,40},{12,20},{16,48},{20,28},{24,56},{28,4},{32,64... | collective-permute-start | bytes 2359304 | tf_op jit(solution)/shard_map/ppermute | solution.py:633
  125.0 15.4 %collective-permute-start.36 = (bf16[512,768]{1,0:T(8,128)(2,1)S(1)}, bf16[512,768]{1,0:T(8,128)(2,1)S(1)}, u32[]{:S(2)}, u32[]{:S(2)}) collective-permute-start(bf16[512,768]{1,0:T(8,128)(2,1)S(1)} %get-tuple-element.125), channel_id=1, source_target_pairs={{0,96},{4,28},{8,104},{12,4},{16,112},{20,12},{24,120},{28,20},{32... | collective-permute-start | bytes 2359304 | tf_op jit(solution)/shard_map/ppermute | solution.py:633
  127.1 16.3 %collective-permute-start.25 = (bf16[512,1024]{1,0:T(8,128)(2,1)S(1)}, bf16[512,1024]{1,0:T(8,128)(2,1)S(1)}, u32[]{:S(2)}, u32[]{:S(2)}) collective-permute-start(bf16[512,1024]{1,0:T(8,128)(2,1)S(1)} %get-tuple-element.100.mkv_ref), channel_id=1, source_target_pairs={{0,4},{4,0},{1,5},{5,1},{2,6},{6,2},{3,7},{7,3},{8,12},{12,8},{9,1... | collective-permute-start | bytes 3145736 | tf_op jit(solution)/shard_map/ppermute | solution.py:622
  135.3 8.1 %collective-permute-start.26 = (bf16[256,1024]{1,0:T(8,128)(2,1)S(1)}, bf16[256,1024]{1,0:T(8,128)(2,1)S(1)}, u32[]{:S(2)}, u32[]{:S(2)}) collective-permute-start(bf16[256,1024]{1,0:T(8,128)(2,1)S(1)} %get-tuple-element.101.mq_ref), channel_id=1, source_target_pairs={{0,4},{4,0},{1,5},{5,1},{2,6},{6,2},{3,7},{7,3},{8,12},{12,8},{9,1... | collective-permute-start | bytes 1572872 | tf_op jit(solution)/shard_map/ppermute | solution.py:622
  140.1 12.8 %collective-permute-start.35 = (bf16[512,768]{1,0:T(8,128)(2,1)S(1)}, bf16[512,768]{1,0:T(8,128)(2,1)S(1)}, u32[]{:S(2)}, u32[]{:S(2)}) collective-permute-start(bf16[512,768]{1,0:T(8,128)(2,1)S(1)} %slice.203), channel_id=1, source_target_pairs={{0,32},{4,12},{8,40},{12,20},{16,48},{20,28},{24,56},{28,4},{32,64... | collective-permute-start | bytes 2359304 | tf_op jit(solution)/shard_map/ppermute | solution.py:633
  140.4 12.5 %collective-permute-start.34 = (bf16[512,768]{1,0:T(8,128)(2,1)S(1)}, bf16[512,768]{1,0:T(8,128)(2,1)S(1)}, u32[]{:S(2)}, u32[]{:S(2)}) collective-permute-start(bf16[512,768]{1,0:T(8,128)(2,1)S(1)} %slice.204), channel_id=1, source_target_pairs={{0,96},{4,28},{8,104},{12,4},{16,112},{20,12},{24,120},{28,20},{32... | collective-permute-start | bytes 2359304 | tf_op jit(solution)/shard_map/ppermute | solution.py:633
  143.3 17.6 %collective-permute-start.33 = (bf16[512,768]{1,0:T(8,128)(2,1)S(1)}, bf16[512,768]{1,0:T(8,128)(2,1)S(1)}, u32[]{:S(2)}, u32[]{:S(2)}) collective-permute-start(bf16[512,768]{1,0:T(8,128)(2,1)S(1)} %fusion.3), channel_id=1, source_target_pairs={{0,32},{4,12},{8,40},{12,20},{16,48},{20,28},{24,56},{28,4},{32,64... | collective-permute-start | bytes 2359304 | tf_op jit(solution)/shard_map/ppermute | solution.py:633
  143.4 17.5 %collective-permute-start.37 = (bf16[512,768]{1,0:T(8,128)(2,1)S(1)}, bf16[512,768]{1,0:T(8,128)(2,1)S(1)}, u32[]{:S(2)}, u32[]{:S(2)}) collective-permute-start(bf16[512,768]{1,0:T(8,128)(2,1)S(1)} %fusion.1), channel_id=1, source_target_pairs={{0,96},{4,28},{8,104},{12,4},{16,112},{20,12},{24,120},{28,20},{32... | collective-permute-start | bytes 2359304 | tf_op jit(solution)/shard_map/ppermute | solution.py:633
  148.9 20.9 %collective-permute-start.29 = (bf16[512,1024]{1,0:T(8,128)(2,1)S(1)}, bf16[512,1024]{1,0:T(8,128)(2,1)S(1)}, u32[]{:S(2)}, u32[]{:S(2)}) collective-permute-start(bf16[512,1024]{1,0:T(8,128)(2,1)S(1)} %convert_element_type.133), channel_id=1, source_target_pairs={{0,1},{1,2},{2,3},{3,0},{4,7},{5,4},{6,5},{7,6},{8,9},{9,10},{10,1... | collective-permute-start | bytes 3145736 | tf_op jit(solution)/shard_map/ppermute | solution.py:640
  161.4 10.3 %collective-permute-start.38 = (bf16[128,768]{1,0:T(8,128)(2,1)S(1)}, bf16[128,768]{1,0:T(8,128)(2,1)S(1)}, u32[]{:S(2)}, u32[]{:S(2)}) collective-permute-start(bf16[128,768]{1,0:T(8,128)(2,1)S(1)} %get-tuple-element.129), channel_id=1, source_target_pairs={{0,8},{4,36},{8,16},{12,44},{16,24},{20,52},{24,0},{28,60},{32,40}... | collective-permute-start | bytes 589832 | tf_op jit(solution)/shard_map/ppermute | solution.py:633
  161.5 10.4 %collective-permute-start.40 = (bf16[128,768]{1,0:T(8,128)(2,1)S(1)}, bf16[128,768]{1,0:T(8,128)(2,1)S(1)}, u32[]{:S(2)}, u32[]{:S(2)}) collective-permute-start(bf16[128,768]{1,0:T(8,128)(2,1)S(1)} %get-tuple-element.130), channel_id=1, source_target_pairs={{0,24},{4,100},{8,0},{12,108},{16,8},{20,116},{24,16},{28,124},{32... | collective-permute-start | bytes 589832 | tf_op jit(solution)/shard_map/ppermute | solution.py:633
  168.5 14.9 %collective-permute-start.28 = (bf16[512,1024]{1,0:T(8,128)(2,1)S(1)}, bf16[512,1024]{1,0:T(8,128)(2,1)S(1)}, u32[]{:S(2)}, u32[]{:S(2)}) collective-permute-start(bf16[512,1024]{1,0:T(8,128)(2,1)S(1)} %slice.202), channel_id=1, source_target_pairs={{0,3},{1,0},{2,1},{3,2},{4,5},{5,6},{6,7},{7,4},{8,11},{9,8},{10,9... | collective-permute-start | bytes 3145736 | tf_op jit(solution)/shard_map/ppermute | solution.py:640
  170.2 18.5 %collective-permute-start.30 = (bf16[512,1024]{1,0:T(8,128)(2,1)S(1)}, bf16[512,1024]{1,0:T(8,128)(2,1)S(1)}, u32[]{:S(2)}, u32[]{:S(2)}) collective-permute-start(bf16[512,1024]{1,0:T(8,128)(2,1)S(1)} %fusion), channel_id=1, source_target_pairs={{0,1},{1,2},{2,3},{3,0},{4,7},{5,4},{6,5},{7,6},{8,9},{9,10},{10,1... | collective-permute-start | bytes 3145736 | tf_op jit(solution)/shard_map/ppermute | solution.py:640
  171.8 24.6 %collective-permute-start.39 = (bf16[256,768]{1,0:T(8,128)(2,1)S(1)}, bf16[256,768]{1,0:T(8,128)(2,1)S(1)}, u32[]{:S(2)}, u32[]{:S(2)}) collective-permute-start(bf16[256,768]{1,0:T(8,128)(2,1)S(1)} %pad_maximum_fusion.3), channel_id=1, source_target_pairs={{0,8},{4,36},{8,16},{12,44},{16,24},{20,52},{24,0},{28,60},{32,40}... | collective-permute-start | bytes 1179656 | tf_op jit(solution)/shard_map/ppermute | solution.py:633
  172.0 24.4 %collective-permute-start.41 = (bf16[256,768]{1,0:T(8,128)(2,1)S(1)}, bf16[256,768]{1,0:T(8,128)(2,1)S(1)}, u32[]{:S(2)}, u32[]{:S(2)}) collective-permute-start(bf16[256,768]{1,0:T(8,128)(2,1)S(1)} %pad_maximum_fusion.4), channel_id=1, source_target_pairs={{0,24},{4,100},{8,0},{12,108},{16,8},{20,116},{24,16},{28,124},{32... | collective-permute-start | bytes 1179656 | tf_op jit(solution)/shard_map/ppermute | solution.py:633
  189.1 9.9 %collective-permute-start.31 = (bf16[512,512]{1,0:T(8,128)(2,1)S(1)}, bf16[512,512]{1,0:T(8,128)(2,1)S(1)}, u32[]{:S(2)}, u32[]{:S(2)}) collective-permute-start(bf16[512,512]{1,0:T(8,128)(2,1)S(1)} %get-tuple-element.106), channel_id=1, source_target_pairs={{0,4},{4,0},{1,5},{5,1},{2,6},{6,2},{3,7},{7,3},{8,12},{12,8},{9,1... | collective-permute-start | bytes 1572872 | tf_op jit(solution)/shard_map/ppermute | solution.py:622
  196.5 1.6 collective-permute-start.42
